TPU v7x, 128 devices: a whole 4x4x4 slice. The times are simulated.
128 devices in a mesh: dp: 8 (over y, z_lo), seq: 16 (over x, z_hi, core).
Axes of the slice: x: 4, y: 4, z: 4 (z_hi: 2, z_lo: 2; z = z_hi * 2 + z_lo), core: 2. Of those that a mesh axis runs over, the one named last changes fastest.
Arguments:
- video: bfloat16 [8, 64, 256, 768], P('dp', 'seq'), may hold values from -6 to 6
- space_qkv: bfloat16 [768, 2304], replicated, may hold values from -0.21875 to 0.21875
- space_out: bfloat16 [768, 768], replicated, may hold values from -0.21875 to 0.21875
- time_qkv: bfloat16 [768, 2304], replicated, may hold values from -0.21875 to 0.21875
- time_out: bfloat16 [768, 768], replicated, may hold values from -0.21875 to 0.21875
- proj_weight: bfloat16 [768, 128], replicated, may hold values from -0.21875 to 0.21875
- queries: bfloat16 [64, 32, 128], P('dp'), may hold values from -6 to 6
- query_len: int32 [64], P('dp'), may hold values from 1 to 32, 1280 in all
- positive: int32 [64], P('dp'), may hold values from 0 to 7
Outputs:
- video_grad: bfloat16 [8, 64, 256, 128], P('dp', None, 'seq')
- query_grad: bfloat16 [64, 32, 128], P('dp')
- pair_loss: float32 [64, 8], P(None, 'dp')
Inputs may be any that keep to these rules, and one draw needn't show every extreme that they name: `query_len`: the query lengths sum to 5 / 8 of all slots and the longest query fills all 32 slots.
All inputs are finite; a program needn't handle non-finite values. No bound on the sum of `query_len` on one device may be relied on, other than what follows from the above.
Results may differ from a plain program's by a relative error of at most 0.028.
Values may be sent and summed in bfloat16 or wider, within the bound.
No kernel may reach another device: no remote copies, remote signals or barrier semaphores. Data moves between devices by JAX's collectives and lax.ppermute only.
A program may use at most 128 MiB of HBM per device.

v0:
```python
import jax
import jax.numpy as jnp
from jax import lax
from jax.experimental import pallas as pl
from jax.experimental.pallas import tpu as pltpu
from jax.sharding import PartitionSpec as P

HEADS = 12
P_SIZE = 256
TEMPER = 0.05
SLOPE = 10.0
OFFSET = -5.0
SHARP = 10.0
LOG2E = 1.4426950408889634

D = 768
HEAD = D // HEADS
PAIR = 2 * HEAD
PAIRS = HEADS // 2
TILE = 256
SUB = 128
E = 128
F32 = jnp.float32
BF16 = jnp.bfloat16


def dot(a, b):
    return lax.dot_general(a, b, (((1,), (0,)), ((), ())), preferred_element_type=F32)


def dot_t(a, b):
    return lax.dot_general(a, b, (((1,), (1,)), ((), ())), preferred_element_type=F32)


def iota(shape, dim):
    return lax.broadcasted_iota(jnp.int32, shape, dim)


def layer_norm(tokens):
    values = tokens.astype(F32)
    center = values - jnp.mean(values, axis=-1, keepdims=True)
    spread = jnp.mean(center * center, axis=-1, keepdims=True)
    return (center * lax.rsqrt(spread + 1e-05)).astype(BF16)


def unit_heads(values, gain):
    same = (iota((TILE, TILE), 0) // HEAD == iota((TILE, TILE), 1) // HEAD).astype(BF16)
    parts = []
    for at in range(0, values.shape[1], TILE):
        part = values[:, at : at + TILE]
        squares = dot((part * part).astype(BF16), same)
        parts.append((part * (lax.rsqrt(squares + 1e-06) * gain)).astype(BF16))
    return jnp.concatenate(parts, axis=1)


def qkv_rows(tokens, weight_ref):
    packed = dot(layer_norm(tokens), weight_ref[...])
    query = unit_heads(packed[:, :D], SHARP * LOG2E)
    key = unit_heads(packed[:, D : 2 * D], 1.0)
    return query, key, packed[:, 2 * D :].astype(BF16)


def pair_blend(query, key, value, keep):
    extent = key.shape[0]
    low = iota((extent, PAIR), 1) < HEAD
    zero = jnp.zeros((extent, PAIR), BF16)
    one = jnp.ones((extent, PAIR), BF16)
    keys = jnp.concatenate([jnp.where(low, key, zero), jnp.where(low, zero, key)], axis=0)
    values = jnp.concatenate(
        [
            jnp.concatenate([jnp.where(low, value, zero), jnp.where(low, one, zero)], axis=1),
            jnp.concatenate([jnp.where(low, zero, value), jnp.where(low, zero, one)], axis=1),
        ],
        axis=0,
    )
    weights = jnp.exp2(dot_t(query, keys))
    if keep is not None:
        weights = jnp.where(keep, weights, 0.0)
    mixed = dot(weights.astype(BF16), values)
    return (mixed[:, :PAIR] / mixed[:, PAIR:]).astype(BF16)


def space_kernel(video_ref, qkv_ref, out_w_ref, out_ref):
    tokens = video_ref[0]
    query, key, value = qkv_rows(tokens, qkv_ref)
    blended = []
    for pair in range(PAIRS):
        at = slice(pair * PAIR, (pair + 1) * PAIR)
        blended.append(pair_blend(query[:, at], key[:, at], value[:, at], None))
    update = dot(jnp.concatenate(blended, axis=1), out_w_ref[...])
    result = (tokens.astype(F32) + update).astype(BF16)
    out_ref[...] = result.reshape(out_ref.shape)


def space(video, qkv_weight, out_weight, shards):
    frames, patches, _ = video.shape
    local = patches // shards
    return pl.pallas_call(
        space_kernel,
        grid=(frames,),
        in_specs=[
            pl.BlockSpec((1, patches, D), lambda f: (f, 0, 0)),
            pl.BlockSpec((D, 3 * D), lambda f: (0, 0)),
            pl.BlockSpec((D, D), lambda f: (0, 0)),
        ],
        out_specs=pl.BlockSpec((shards, 1, local, D), lambda f: (0, f, 0, 0)),
        out_shape=jax.ShapeDtypeStruct((shards, frames, local, D), BF16),
        compiler_params=pltpu.CompilerParams(vmem_limit_bytes=48 * 2**20),
        name="space",
    )(video, qkv_weight, out_weight)


def swap_rows(rows, side):
    extent = side * side
    row, col = iota((extent, extent), 0), iota((extent, extent), 1)
    swap = (col == (row % side) * side + row // side).astype(BF16)
    return dot(swap, rows).astype(BF16)


def time_kernel(x_ref, qkv_ref, out_w_ref, proj_ref, khat_ref, x_s, q_s, k_s, v_s, kh_s):
    step = pl.program_id(0)
    side = x_s.shape[0]
    tiles = pl.num_programs(0) // 2
    groups = TILE // x_s.shape[1]

    @pl.when(step < tiles)
    def _():
        tokens = swap_rows(x_ref[...], side)
        query, key, value = qkv_rows(tokens, qkv_ref)
        at = pl.ds(pl.multiple_of(step * side, side), side)
        x_s[:, at, :] = tokens.reshape(side, side, D)
        q_s[:, at, :] = query.reshape(side, side, D)
        k_s[:, at, :] = key.reshape(side, side, D)
        v_s[:, at, :] = value.reshape(side, side, D)

    @pl.when(step >= tiles)
    def _():
        at = pl.ds((step - tiles) * groups, groups)
        extent = x_s.shape[1]
        query = q_s[at].reshape(TILE, D)
        key = k_s[at].reshape(TILE, D)
        value = v_s[at].reshape(TILE, D)
        keep = iota((SUB, 2 * SUB), 0) // extent == (iota((SUB, 2 * SUB), 1) % SUB) // extent
        rows = []
        for sub in range(TILE // SUB):
            down = slice(sub * SUB, (sub + 1) * SUB)
            cols = []
            for pair in range(PAIRS):
                across = slice(pair * PAIR, (pair + 1) * PAIR)
                cols.append(
                    pair_blend(query[down, across], key[down, across], value[down, across], keep)
                )
            rows.append(jnp.concatenate(cols, axis=1))
        update = dot(jnp.concatenate(rows, axis=0), out_w_ref[...])
        tokens = x_s[at].reshape(TILE, D)
        mixed = (tokens.astype(F32) + update).astype(BF16)
        projected = dot(layer_norm(mixed), proj_ref[...])
        norm = jnp.sum(projected * projected, axis=-1, keepdims=True)
        unit = (projected * lax.rsqrt(norm + 1e-06)).astype(BF16)
        kh_s[at] = unit.reshape(groups, extent, E)

    @pl.when(step == 2 * tiles - 1)
    def _():
        for tile in range(khat_ref.shape[0] // TILE):
            rows = kh_s[:, tile * side : (tile + 1) * side, :].reshape(TILE, E)
            khat_ref[tile * TILE : (tile + 1) * TILE, :] = swap_rows(rows, side)


def time(x, qkv_weight, out_weight, proj_weight, patches):
    rows = x.shape[0]
    frames = rows // patches
    tiles = rows // TILE
    whole = lambda s: (0, 0)
    return pl.pallas_call(
        time_kernel,
        grid=(2 * tiles,),
        in_specs=[
            pl.BlockSpec((TILE, D), lambda s: (jnp.minimum(s, tiles - 1), 0)),
            pl.BlockSpec((D, 3 * D), whole),
            pl.BlockSpec((D, D), whole),
            pl.BlockSpec((D, E), whole),
        ],
        out_specs=pl.BlockSpec((rows, E), whole),
        out_shape=jax.ShapeDtypeStruct((rows, E), BF16),
        scratch_shapes=[pltpu.VMEM((patches, frames, D), BF16)] * 4
        + [pltpu.VMEM((patches, frames, E), BF16)],
        compiler_params=pltpu.CompilerParams(vmem_limit_bytes=48 * 2**20),
        name="time",
    )(x, qkv_weight, out_weight, proj_weight)


EXTRA = 16


def query_kernel(len_ref, pos_ref, q_ref, out_ref):
    rows = q_ref.shape[0]
    values = q_ref[...].astype(F32)
    norm = jnp.sum(values * values, axis=-1, keepdims=True)
    unit = (values / jnp.sqrt(norm + 1e-06)).astype(BF16)
    slots = rows // len_ref.shape[0]
    row, lane = iota((EXTRA, E), 0), iota((EXTRA, E), 1)
    owner = ((row % 2) * E + lane) // slots
    extra = jnp.zeros((EXTRA, E), F32)
    for query in range(len_ref.shape[0]):
        picked = jnp.where(row < 2, len_ref[query], pos_ref[query]).astype(F32)
        extra = jnp.where((owner == query) & (row < 4), picked, extra)
    for copy in range(out_ref.shape[0]):
        out_ref[copy, :rows, :] = unit
        out_ref[copy, rows:, :] = extra.astype(BF16)


def pack_queries(queries, query_len, positive, copies):
    rows = queries.shape[0]
    return pl.pallas_call(
        query_kernel,
        in_specs=[
            pl.BlockSpec(memory_space=pltpu.SMEM),
            pl.BlockSpec(memory_space=pltpu.SMEM),
            pl.BlockSpec(memory_space=pltpu.VMEM),
        ],
        out_specs=pl.BlockSpec(memory_space=pltpu.VMEM),
        out_shape=jax.ShapeDtypeStruct((copies, rows + EXTRA, E), BF16),
        name="pack_queries",
    )(query_len, positive, queries)


def terms_kernel(q_ref, khat_ref, expo_ref, blend_ref, sums_ref):
    rows = expo_ref.shape[0]
    khat = khat_ref[...]
    dots = dot_t(q_ref[0, :rows, :], khat)
    gain = LOG2E / TEMPER
    expo = jnp.exp2(dots * gain - gain).astype(BF16)
    expo_ref[...] = expo
    wide = jnp.concatenate([khat, jnp.ones_like(khat)], axis=1)
    both = dot(expo, wide)
    blend_ref[...] = both[:, :E]
    eye = iota((E, E), 0) == iota((E, E), 1)
    for part in range(rows // E):
        block = both[part * E : (part + 1) * E, E:]
        sums_ref[0, part : part + 1, :] = jnp.sum(
            jnp.where(eye, block, 0.0), axis=0, keepdims=True
        )


def terms(packed, khat):
    blocks, rows, _ = packed.shape
    rows = rows - EXTRA
    tokens = khat.shape[0]
    return pl.pallas_call(
        terms_kernel,
        grid=(blocks,),
        in_specs=[
            pl.BlockSpec((1, rows + EXTRA, E), lambda b: (b, 0, 0)),
            pl.BlockSpec((tokens, E), lambda b: (0, 0)),
        ],
        out_specs=[
            pl.BlockSpec((rows, tokens), lambda b: (b, 0)),
            pl.BlockSpec((rows, E), lambda b: (b, 0)),
            pl.BlockSpec((1, rows // E, E), lambda b: (b, 0, 0)),
        ],
        out_shape=[
            jax.ShapeDtypeStruct((blocks * rows, tokens), BF16),
            jax.ShapeDtypeStruct((blocks * rows, E), F32),
            jax.ShapeDtypeStruct((blocks, rows // E, E), F32),
        ],
        compiler_params=pltpu.CompilerParams(vmem_limit_bytes=48 * 2**20),
        name="terms",
    )(packed, khat)


def scale_kernel(slots, video_ref, sums_ref, packed_ref, blend_ref, part_ref, qt_ref, loss_ref):
    blocks, rows, _ = packed_ref.shape
    rows = rows - EXTRA
    per = rows // E
    total = jnp.sum(sums_ref[...], axis=0)
    lens = jnp.concatenate(
        [packed_ref[b, rows : rows + EXTRA, :].astype(F32)[:per] for b in range(blocks)], axis=0
    )
    pos = jnp.concatenate(
        [packed_ref[b, rows : rows + EXTRA, :].astype(F32)[2 : 2 + per] for b in range(blocks)],
        axis=0,
    )
    lane = iota(total.shape, 1)
    mask = ((lane % slots).astype(F32) < lens).astype(F32)
    smooth = (1.0 + TEMPER * jnp.log(total)) * mask
    same = (iota((E, E), 0) // slots == iota((E, E), 1) // slots).astype(F32)
    score = (
        lax.dot_general(
            smooth,
            same,
            (((1,), (0,)), ((), ())),
            preferred_element_type=F32,
            precision=lax.Precision.HIGHEST,
        )
        / lens
    )
    sign = jnp.where(pos == video_ref[0].astype(F32), 1.0, -1.0)
    margin = sign * (SLOPE * score + OFFSET)
    loss_ref[...] = jnp.maximum(-margin, 0.0) + jnp.log1p(jnp.exp(-jnp.abs(margin)))
    coeff = -SLOPE * sign / (1.0 + jnp.exp(margin)) * mask / lens
    scale = (coeff / total).T
    for b in range(blocks):
        for part in range(per):
            at = b * per + part
            column = scale[:, at : at + 1]
            down = slice(part * E, (part + 1) * E)
            flat = slice(at * E, (at + 1) * E)
            part_ref[b, down, :] = (blend_ref[flat, :] * column).astype(BF16)
            scaled = packed_ref[b, down, :].astype(F32) * column
            qt_ref[:, flat] = scaled.T.astype(BF16)


def scales(sums, packed, blend, video_id, slots):
    blocks, rows, _ = packed.shape
    rows = rows - EXTRA
    vmem = pl.BlockSpec(memory_space=pltpu.VMEM)
    return pl.pallas_call(
        lambda *refs: scale_kernel(slots, *refs),
        in_specs=[pl.BlockSpec(memory_space=pltpu.SMEM), vmem, vmem, vmem],
        out_specs=[vmem, vmem, vmem],
        out_shape=[
            jax.ShapeDtypeStruct((blocks, rows, E), BF16),
            jax.ShapeDtypeStruct((E, blocks * rows), BF16),
            jax.ShapeDtypeStruct(sums.shape[1:], F32),
        ],
        compiler_params=pltpu.CompilerParams(vmem_limit_bytes=32 * 2**20),
        name="scales",
    )(video_id, sums, packed, blend)


def keys_kernel(gain, qt_ref, expo_ref, out_ref, acc_ref):
    step = pl.program_id(0)
    product = dot(qt_ref[...], expo_ref[...])

    @pl.when(step == 0)
    def _():
        acc_ref[...] = product

    @pl.when(step > 0)
    def _():
        acc_ref[...] += product

    @pl.when(step == pl.num_programs(0) - 1)
    def _():
        out_ref[...] = (acc_ref[...].T * gain).astype(BF16)


def keys(qt, expo, gain):
    rows, tokens = expo.shape
    return pl.pallas_call(
        lambda *refs: keys_kernel(gain, *refs),
        grid=(rows // TILE,),
        in_specs=[
            pl.BlockSpec((E, TILE), lambda b: (0, b)),
            pl.BlockSpec((TILE, tokens), lambda b: (b, 0)),
        ],
        out_specs=pl.BlockSpec((tokens, E), lambda b: (0, 0)),
        out_shape=jax.ShapeDtypeStruct((tokens, E), BF16),
        scratch_shapes=[pltpu.VMEM((E, tokens), F32)],
        compiler_params=pltpu.CompilerParams(vmem_limit_bytes=32 * 2**20),
        name="keys",
    )(qt, expo)


def body(
    video, space_qkv, space_out, time_qkv, time_out, proj_weight, queries, query_len, positive
):
    _, frames_dev, patches, _ = video.shape
    shards = lax.axis_size("seq")
    blocks = lax.axis_size("dp")
    patch_loc = patches // shards
    frames = frames_dev * shards
    query_dev, slots, _ = queries.shape
    rows = query_dev * slots

    mine = pack_queries(queries.reshape(rows, E), query_len, positive, blocks)
    packed = lax.all_to_all(mine, "dp", 0, 0, tiled=True)

    spatial = space(video[0], space_qkv, space_out, shards)
    items = lax.all_to_all(spatial, "seq", 0, 0, tiled=True)
    khat = time(items.reshape(-1, D), time_qkv, time_out, proj_weight, patch_loc)

    expo, blend, sums = terms(packed, khat)
    sums = sums.reshape(-1, E)
    sums = lax.all_to_all(
        jnp.broadcast_to(sums[None], (shards,) + sums.shape), "seq", 0, 0, tiled=True
    )
    video_id = lax.axis_index("dp").astype(jnp.int32).reshape(1)
    parts, qt, loss = scales(sums, packed, blend, video_id, slots)
    parts = lax.all_to_all(parts, "dp", 0, 0, tiled=True)
    video_grad = keys(qt, expo, float(frames * P_SIZE)).reshape(1, frames, patch_loc, E)
    summed = jnp.sum(parts.astype(F32), axis=0).astype(BF16)
    summed = lax.all_to_all(
        jnp.broadcast_to(summed[None], (shards,) + summed.shape), "seq", 0, 0, tiled=True
    )
    total = jnp.sum(summed.astype(F32), axis=0)
    query_grad = (slots * total).astype(BF16).reshape(query_dev, slots, E)
    pair_loss = loss[:, ::slots].reshape(-1, 1)
    return (video_grad, query_grad, pair_loss)


def solution(mesh):
    placed = (
        P("dp", "seq", None, None),
        P(),
        P(),
        P(),
        P(),
        P(),
        P("dp", None, None),
        P("dp"),
        P("dp"),
    )
    return jax.shard_map(
        body,
        mesh=mesh,
        in_specs=placed,
        out_specs=(P("dp", None, "seq", None), P("dp", None, None), P(None, "dp")),
        check_vma=False,
    )
```

profile of v0, /device:TPU:1, one launch (start us, length us, event | category | flops | bytes accessed | tf_op | source)
XLA Modules:
  0.0 131.2 jit_solution(14821609569530074743)
XLA Ops:
  0.6 0.0 copy-start.2
  0.6 1.4 %copy-done.2 = bf16[1,4,256,768]{3,2,1,0:T(8,128)(2,1)S(1)} copy-done((bf16[1,4,256,768]{3,2,1,0:T(8,128)(2,1)S(1)}, bf16[1,4,256,768]{3,2,1,0:T(8,128)(2,1)}, u32[]{:S(2)}) %copy-start.2) | copy-done | bytes 1572888
  2.0 1.3 copy-done.4
  3.3 14.1 %space.1 = bf16[16,4,16,768]{3,2,1,0:T(8,128)(2,1)} custom-call(bf16[4,256,768]{2,1,0:T(8,128)(2,1)S(1)} %bitcast.8, bf16[768,2304]{1,0:T(8,128)(2,1)} %qkv_ref.2, bf16[768,768]{1,0:T(8,128)(2,1)S(1)} %copy-done.4), custom_call_target="tpu_custom_call" | custom-call | tf_op jit(solution)/shard_map/space/pallas_call | solution.py:98
  17.5 9.1 %all-to-all-start.1 = ((bf16[16,4,16,768]{3,2,1,0:T(8,128)(2,1)}), bf16[16,4,16,768]{3,2,1,0:T(8,128)(2,1)S(1)}, u32[]{:S(2)}, u32[]{:S(2)}) async-start(bf16[16,4,16,768]{3,2,1,0:T(8,128)(2,1)} %space.1), calls=%async_computation.1 | async-start | bytes 3145728 | tf_op jit(solution)/shard_map/all_to_all | solution.py:380
  26.6 0.0 copy-start.7
  26.6 1.9 %pack_queries.1 = bf16[8,272,128]{2,1,0:T(8,128)(2,1)} custom-call(s32[8]{0:T(128)} %len_ref.1, s32[8]{0:T(128)} %pos_ref.1, bf16[256,128]{1,0:T(8,128)(2,1)} %bitcast.11), custom_call_target="tpu_custom_call" | custom-call | tf_op jit(solution)/shard_map/pack_queries/pallas_call | solution.py:214
  28.5 20.9 %all-to-all-done.1 = bf16[16,4,16,768]{3,2,1,0:T(8,128)(2,1)S(1)} async-done(((bf16[16,4,16,768]{3,2,1,0:T(8,128)(2,1)}), bf16[16,4,16,768]{3,2,1,0:T(8,128)(2,1)S(1)}, u32[]{:S(2)}, u32[]{:S(2)}) %all-to-all-start.1) | async-done | bytes 1572896 | tf_op jit(solution)/shard_map/all_to_all | solution.py:380
  49.4 4.7 %all-to-all-start = ((bf16[8,272,128]{2,1,0:T(8,128)(2,1)}), bf16[8,272,128]{2,1,0:T(8,128)(2,1)S(1)}, u32[]{:S(2)}, u32[]{:S(2)}) async-start(bf16[8,272,128]{2,1,0:T(8,128)(2,1)} %pack_queries.1), calls=%async_computation | async-start | bytes 1114112 | tf_op jit(solution)/shard_map/all_to_all | solution.py:377
  54.1 15.9 %time.1.khat_ref = bf16[1024,128]{1,0:T(8,128)(2,1)S(1)} custom-call(bf16[1024,768]{1,0:T(8,128)(2,1)S(1)} %bitcast.7, bf16[768,2304]{1,0:T(8,128)(2,1)} %qkv_ref.3, bf16[768,768]{1,0:T(8,128)(2,1)S(1)} %copy-done.3, bf16[768,128]{1,0:T(8,128)(2,1)S(1)} %copy-done.7), custom_call_target="tpu_custom_call" | custom-call | tf_op jit(solution)/shard_map/time/pallas_call | solution.py:174
  69.9 0.0 copy-start.5
  70.0 0.7 copy-done.5
  70.7 0.0 all-to-all-done.q_ref.refs_2_
  70.7 0.9 copy-done.6
  71.6 4.5 %terms.1 = (bf16[2048,1024]{1,0:T(8,128)(2,1)S(1)}, f32[2048,128]{1,0:T(8,128)S(1)}, f32[8,2,128]{2,1,0:T(2,128)S(1)}) custom-call(bf16[8,272,128]{2,1,0:T(8,128)(2,1)S(1)} %all-to-all-done.q_ref.refs_2_, bf16[1024,128]{1,0:T(8,128)(2,1)S(1)} %copy-done.6), custom_call_target="tpu_custom_call" | custom-call | tf_op jit(solution)/shard_map/terms/pallas_call | solution.py:249
  76.1 0.0 copy-start
  76.1 1.9 %copy-done = bf16[2048,1024]{1,0:T(8,128)(2,1)} copy-done((bf16[2048,1024]{1,0:T(8,128)(2,1)}, bf16[2048,1024]{1,0:T(8,128)(2,1)S(1)}, u32[]{:S(2)}) %copy-start) | copy-done | bytes 4194328
  78.0 0.7 broadcast_in_dim.14
  78.7 5.7 %all-to-all-start.2 = ((f32[16,16,128]{2,1,0:T(8,128)}), f32[16,16,128]{2,1,0:T(8,128)S(1)}, u32[]{:S(2)}, u32[]{:S(2)}) async-start(f32[16,16,128]{2,1,0:T(8,128)} %broadcast_in_dim.14), calls=%async_computation.2 | async-start | bytes 262144 | tf_op jit(solution)/shard_map/all_to_all | solution.py:385
  84.4 7.7 %all-to-all-done.2.refs_1_ = f32[16,16,128]{2,1,0:T(8,128)S(1)} async-done(((f32[16,16,128]{2,1,0:T(8,128)}), f32[16,16,128]{2,1,0:T(8,128)S(1)}, u32[]{:S(2)}, u32[]{:S(2)}) %all-to-all-start.2) | async-done | bytes 131104 | tf_op jit(solution)/shard_map/all_to_all | solution.py:385
  92.1 1.0 scales.1
  93.1 13.2 %all_to_all.25 = bf16[8,256,128]{2,1,0:T(8,128)(2,1)S(1)} all-to-all(bf16[8,256,128]{2,1,0:T(8,128)(2,1)S(1)} %get-tuple-element.13), channel_id=1, replica_groups=mesh['dp'=8,'seq'=16] {'dp'}, dimensions={0} | all-to-all | bytes 1048576 | tf_op jit(solution)/shard_map/all_to_all | solution.py:390
  106.3 0.1 reduce_sum.21
  106.4 1.2 broadcast_in_dim.15
  107.6 5.5 %all-to-all-start.4 = ((bf16[16,256,128]{2,1,0:T(8,128)(2,1)}), bf16[16,256,128]{2,1,0:T(8,128)(2,1)S(1)}, u32[]{:S(2)}, u32[]{:S(2)}) async-start(bf16[16,256,128]{2,1,0:T(8,128)(2,1)} %broadcast_in_dim.15), calls=%async_computation.4 | async-start | bytes 2097152 | tf_op jit(solution)/shard_map/all_to_all | solution.py:393
  113.1 0.1 slice.3
  113.2 0.6 reshape.32
  113.8 2.2 %copy-done.1 = bf16[2048,1024]{1,0:T(8,128)(2,1)S(1)} copy-done((bf16[2048,1024]{1,0:T(8,128)(2,1)S(1)}, bf16[2048,1024]{1,0:T(8,128)(2,1)}, u32[]{:S(2)}) %copy-start.1) | copy-done | bytes 4194328
  116.0 3.4 %keys.1 = bf16[1024,128]{1,0:T(8,128)(2,1)} custom-call(bf16[128,2048]{1,0:T(8,128)(2,1)S(1)} %get-tuple-element.11.refs_0_, bf16[2048,1024]{1,0:T(8,128)(2,1)S(1)} %copy-done.1), custom_call_target="tpu_custom_call" | custom-call | tf_op jit(solution)/shard_map/keys/pallas_call | solution.py:350
  119.3 11.1 %all-to-all-done.4 = bf16[16,256,128]{2,1,0:T(8,128)(2,1)S(1)} async-done(((bf16[16,256,128]{2,1,0:T(8,128)(2,1)}), bf16[16,256,128]{2,1,0:T(8,128)(2,1)S(1)}, u32[]{:S(2)}, u32[]{:S(2)}) %all-to-all-start.4) | async-done | bytes 1048608 | tf_op jit(solution)/shard_map/all_to_all | solution.py:393
  130.4 0.1 convert_reduce_fusion
  130.5 0.6 multiply_convert_fusion
  (6 shorter events, 0.0 us)
Async XLA Ops:
  0.6 1.4 %copy-start.2 = (bf16[1,4,256,768]{3,2,1,0:T(8,128)(2,1)S(1)}, bf16[1,4,256,768]{3,2,1,0:T(8,128)(2,1)}, u32[]{:S(2)}) copy-start(bf16[1,4,256,768]{3,2,1,0:T(8,128)(2,1)} %param.9) | copy-start | bytes 4718596
  2.0 1.3 copy-start.4
  17.5 32.0 %all-to-all-start.1 = ((bf16[16,4,16,768]{3,2,1,0:T(8,128)(2,1)}), bf16[16,4,16,768]{3,2,1,0:T(8,128)(2,1)S(1)}, u32[]{:S(2)}, u32[]{:S(2)}) async-start(bf16[16,4,16,768]{3,2,1,0:T(8,128)(2,1)} %space.1), calls=%async_computation.1 | async-start | bytes 3145728 | tf_op jit(solution)/shard_map/all_to_all | solution.py:380
  26.6 27.5 %copy-start.3 = (bf16[768,768]{1,0:T(8,128)(2,1)S(1)}, bf16[768,768]{1,0:T(8,128)(2,1)}, u32[]{:S(2)}) copy-start(bf16[768,768]{1,0:T(8,128)(2,1)} %out_w_ref.3) | copy-start | bytes 3538948
  26.6 27.5 %copy-start.7 = (bf16[768,128]{1,0:T(8,128)(2,1)S(1)}, bf16[768,128]{1,0:T(8,128)(2,1)}, u32[]{:S(2)}) copy-start(bf16[768,128]{1,0:T(8,128)(2,1)} %proj_ref.1) | copy-start | bytes 589828
  49.4 21.2 %all-to-all-start = ((bf16[8,272,128]{2,1,0:T(8,128)(2,1)}), bf16[8,272,128]{2,1,0:T(8,128)(2,1)S(1)}, u32[]{:S(2)}, u32[]{:S(2)}) async-start(bf16[8,272,128]{2,1,0:T(8,128)(2,1)} %pack_queries.1), calls=%async_computation | async-start | bytes 1114112 | tf_op jit(solution)/shard_map/all_to_all | solution.py:377
  69.9 0.7 copy-start.5
  70.7 1.0 copy-start.6
  76.1 2.0 %copy-start = (bf16[2048,1024]{1,0:T(8,128)(2,1)}, bf16[2048,1024]{1,0:T(8,128)(2,1)S(1)}, u32[]{:S(2)}) copy-start(bf16[2048,1024]{1,0:T(8,128)(2,1)S(1)} %get-tuple-element.12.refs_1_) | copy-start | bytes 12582916
  78.7 13.4 %all-to-all-start.2 = ((f32[16,16,128]{2,1,0:T(8,128)}), f32[16,16,128]{2,1,0:T(8,128)S(1)}, u32[]{:S(2)}, u32[]{:S(2)}) async-start(f32[16,16,128]{2,1,0:T(8,128)} %broadcast_in_dim.14), calls=%async_computation.2 | async-start | bytes 262144 | tf_op jit(solution)/shard_map/all_to_all | solution.py:385
  107.6 22.8 %all-to-all-start.4 = ((bf16[16,256,128]{2,1,0:T(8,128)(2,1)}), bf16[16,256,128]{2,1,0:T(8,128)(2,1)S(1)}, u32[]{:S(2)}, u32[]{:S(2)}) async-start(bf16[16,256,128]{2,1,0:T(8,128)(2,1)} %broadcast_in_dim.15), calls=%async_computation.4 | async-start | bytes 2097152 | tf_op jit(solution)/shard_map/all_to_all | solution.py:393
  113.8 2.2 %copy-start.1 = (bf16[2048,1024]{1,0:T(8,128)(2,1)S(1)}, bf16[2048,1024]{1,0:T(8,128)(2,1)}, u32[]{:S(2)}) copy-start(bf16[2048,1024]{1,0:T(8,128)(2,1)} %copy-done) | copy-start | bytes 12582916
where the time goes:
time: 132 us; the launch traced here: 131 us
  Pallas kernels  40.7 us (31%)
  waiting for transfers between devices  39.6 us (30%)
  starting transfers between devices  25 us (19%)
  blocking collectives  13.2 us (10%)
  local copies, waits for them, and re-layouts  11 us (8%)
    all_to_all x1, waiting for transfers between devices, body(): items = lax.all_to_all(spatial, 'seq', 0, 0, tiled=True)  20.9 us
    pallas_call x1, Pallas kernels, time(): pl.pallas_call(time_kernel, grid=(2 * tiles,), in_specs=[pl.BlockSpec((TI...  15.9 us
    pallas_call x1, Pallas kernels, space(): pl.pallas_call(space_kernel, grid=(frames,), in_specs=[pl.BlockSpec((1, p...  14.1 us
    all_to_all x1, blocking collectives, body(): parts = lax.all_to_all(parts, 'dp', 0, 0, tiled=True)  13.2 us
    all_to_all x1, waiting for transfers between devices, body(): lax.all_to_all(jnp.broadcast_to(summed[None], (shards,) + summed.shape),...  11.1 us
    all_to_all x1, starting transfers between devices, body(): items = lax.all_to_all(spatial, 'seq', 0, 0, tiled=True)  9.13 us
    unnamed x16, local copies, waits for them, and re-layouts  8.46 us
    all_to_all x1, waiting for transfers between devices, body(): lax.all_to_all(jnp.broadcast_to(sums[None], (shards,) + sums.shape), 'seq...  7.68 us
  transfers between devices with their start and end apart: 4, of which 3 were waited for; matrix products, arithmetic and copies ran while one was open for 1% of the time, Pallas kernels for 16%

commit v1 on v0

--- a/solution.py
+++ b/solution.py
@@ -22,6 +22,13 @@
 E = 128
 F32 = jnp.float32
 BF16 = jnp.bfloat16
+VMEM = pl.BlockSpec(memory_space=pltpu.VMEM)
+SMEM = pl.BlockSpec(memory_space=pltpu.SMEM)
+HBM = pl.BlockSpec(memory_space=pltpu.HBM)
+
+
+def limit(mib):
+    return pltpu.CompilerParams(vmem_limit_bytes=mib * 2**20)
 
 
 def dot(a, b):
@@ -105,7 +112,7 @@
         ],
         out_specs=pl.BlockSpec((shards, 1, local, D), lambda f: (0, f, 0, 0)),
         out_shape=jax.ShapeDtypeStruct((shards, frames, local, D), BF16),
-        compiler_params=pltpu.CompilerParams(vmem_limit_bytes=48 * 2**20),
+        compiler_params=limit(28),
         name="space",
     )(video, qkv_weight, out_weight)
 
@@ -184,7 +191,7 @@
         out_shape=jax.ShapeDtypeStruct((rows, E), BF16),
         scratch_shapes=[pltpu.VMEM((patches, frames, D), BF16)] * 4
         + [pltpu.VMEM((patches, frames, E), BF16)],
-        compiler_params=pltpu.CompilerParams(vmem_limit_bytes=48 * 2**20),
+        compiler_params=limit(32),
         name="time",
     )(x, qkv_weight, out_weight, proj_weight)
 
@@ -196,7 +203,7 @@
     rows = q_ref.shape[0]
     values = q_ref[...].astype(F32)
     norm = jnp.sum(values * values, axis=-1, keepdims=True)
-    unit = (values / jnp.sqrt(norm + 1e-06)).astype(BF16)
+    out_ref[:rows, :] = (values / jnp.sqrt(norm + 1e-06)).astype(BF16)
     slots = rows // len_ref.shape[0]
     row, lane = iota((EXTRA, E), 0), iota((EXTRA, E), 1)
     owner = ((row % 2) * E + lane) // slots
@@ -204,84 +211,80 @@
     for query in range(len_ref.shape[0]):
         picked = jnp.where(row < 2, len_ref[query], pos_ref[query]).astype(F32)
         extra = jnp.where((owner == query) & (row < 4), picked, extra)
-    for copy in range(out_ref.shape[0]):
-        out_ref[copy, :rows, :] = unit
-        out_ref[copy, rows:, :] = extra.astype(BF16)
-
-
-def pack_queries(queries, query_len, positive, copies):
+    out_ref[rows:, :] = extra.astype(BF16)
+
+
+def pack_queries(queries, query_len, positive):
     rows = queries.shape[0]
     return pl.pallas_call(
         query_kernel,
-        in_specs=[
-            pl.BlockSpec(memory_space=pltpu.SMEM),
-            pl.BlockSpec(memory_space=pltpu.SMEM),
-            pl.BlockSpec(memory_space=pltpu.VMEM),
-        ],
-        out_specs=pl.BlockSpec(memory_space=pltpu.VMEM),
-        out_shape=jax.ShapeDtypeStruct((copies, rows + EXTRA, E), BF16),
+        in_specs=[SMEM, SMEM, VMEM],
+        out_specs=VMEM,
+        out_shape=jax.ShapeDtypeStruct((rows + EXTRA, E), BF16),
         name="pack_queries",
     )(query_len, positive, queries)
 
 
-def terms_kernel(q_ref, khat_ref, expo_ref, blend_ref, sums_ref):
-    rows = expo_ref.shape[0]
+def terms_kernel(blocks, at_ref, khat_ref, *refs):
+    packed_refs = refs[:blocks]
+    expo_ref, keep_ref, send_ref, sums_ref, expo_s, sem = refs[blocks:]
+    rows = packed_refs[0].shape[0] - EXTRA
+    first = at_ref[1] == 0
     khat = khat_ref[...]
-    dots = dot_t(q_ref[0, :rows, :], khat)
+    wide = jnp.concatenate([khat, jnp.ones_like(khat)], axis=1)
     gain = LOG2E / TEMPER
-    expo = jnp.exp2(dots * gain - gain).astype(BF16)
-    expo_ref[...] = expo
-    wide = jnp.concatenate([khat, jnp.ones_like(khat)], axis=1)
-    both = dot(expo, wide)
-    blend_ref[...] = both[:, :E]
     eye = iota((E, E), 0) == iota((E, E), 1)
-    for part in range(rows // E):
-        block = both[part * E : (part + 1) * E, E:]
-        sums_ref[0, part : part + 1, :] = jnp.sum(
-            jnp.where(eye, block, 0.0), axis=0, keepdims=True
-        )
-
-
-def terms(packed, khat):
-    blocks, rows, _ = packed.shape
-    rows = rows - EXTRA
+    sums = []
+    for block in range(blocks):
+        dots = dot_t(packed_refs[block][:rows, :], khat)
+        expo = jnp.exp2(dots * gain - gain).astype(BF16)
+        expo_s[block] = expo
+        pltpu.make_async_copy(expo_s.at[block], expo_ref.at[block], sem.at[block]).start()
+        both = dot(expo, wide)
+        low, high = both[:E, :E], both[E:, :E]
+        keep_ref[block] = jnp.where(first, low, high)
+        send_ref[block] = jnp.where(first, high, low).astype(BF16)
+        for part in range(rows // E):
+            square = both[part * E : (part + 1) * E, E:]
+            sums.append(jnp.sum(jnp.where(eye, square, 0.0), axis=0, keepdims=True))
+    sums = jnp.concatenate(sums, axis=0)
+    for copy in range(sums_ref.shape[0]):
+        sums_ref[copy] = sums
+    for block in range(blocks):
+        pltpu.make_async_copy(expo_s.at[block], expo_ref.at[block], sem.at[block]).wait()
+
+
+def terms(packed, khat, place, shards):
+    blocks, rows = len(packed), packed[0].shape[0] - EXTRA
     tokens = khat.shape[0]
     return pl.pallas_call(
-        terms_kernel,
-        grid=(blocks,),
-        in_specs=[
-            pl.BlockSpec((1, rows + EXTRA, E), lambda b: (b, 0, 0)),
-            pl.BlockSpec((tokens, E), lambda b: (0, 0)),
-        ],
-        out_specs=[
-            pl.BlockSpec((rows, tokens), lambda b: (b, 0)),
-            pl.BlockSpec((rows, E), lambda b: (b, 0)),
-            pl.BlockSpec((1, rows // E, E), lambda b: (b, 0, 0)),
-        ],
+        lambda *refs: terms_kernel(blocks, *refs),
+        in_specs=[SMEM] + [VMEM] * (1 + blocks),
+        out_specs=[HBM] + [VMEM] * 3,
         out_shape=[
-            jax.ShapeDtypeStruct((blocks * rows, tokens), BF16),
-            jax.ShapeDtypeStruct((blocks * rows, E), F32),
-            jax.ShapeDtypeStruct((blocks, rows // E, E), F32),
-        ],
-        compiler_params=pltpu.CompilerParams(vmem_limit_bytes=48 * 2**20),
+            pltpu.HBM((blocks, rows, tokens), BF16),
+            jax.ShapeDtypeStruct((blocks, rows // 2, E), F32),
+            jax.ShapeDtypeStruct((blocks, rows // 2, E), BF16),
+            jax.ShapeDtypeStruct((shards, blocks * rows // E, E), F32),
+        ],
+        scratch_shapes=[
+            pltpu.VMEM((blocks, rows, tokens), BF16),
+            pltpu.SemaphoreType.DMA((blocks,)),
+        ],
+        compiler_params=limit(16),
         name="terms",
-    )(packed, khat)
-
-
-def scale_kernel(slots, video_ref, sums_ref, packed_ref, blend_ref, part_ref, qt_ref, loss_ref):
-    blocks, rows, _ = packed_ref.shape
-    rows = rows - EXTRA
+    )(place, khat, *packed)
+
+
+def scale_kernel(slots, blocks, at_ref, sums_ref, keep_ref, got_ref, *refs):
+    packed_refs, (part_ref, scale_ref, loss_ref) = refs[:blocks], refs[blocks:]
+    rows = packed_refs[0].shape[0] - EXTRA
     per = rows // E
     total = jnp.sum(sums_ref[...], axis=0)
-    lens = jnp.concatenate(
-        [packed_ref[b, rows : rows + EXTRA, :].astype(F32)[:per] for b in range(blocks)], axis=0
-    )
-    pos = jnp.concatenate(
-        [packed_ref[b, rows : rows + EXTRA, :].astype(F32)[2 : 2 + per] for b in range(blocks)],
-        axis=0,
-    )
-    lane = iota(total.shape, 1)
-    mask = ((lane % slots).astype(F32) < lens).astype(F32)
+    notes = [packed_refs[b][rows:, :].astype(F32) for b in range(blocks)]
+    lens = jnp.concatenate([note[:per] for note in notes], axis=0)
+    pos = jnp.concatenate([note[per : 2 * per] for note in notes], axis=0)
+    mask = ((iota(total.shape, 1) % slots).astype(F32) < lens).astype(F32)
     smooth = (1.0 + TEMPER * jnp.log(total)) * mask
     same = (iota((E, E), 0) // slots == iota((E, E), 1) // slots).astype(F32)
     score = (
@@ -294,72 +297,86 @@
         )
         / lens
     )
-    sign = jnp.where(pos == video_ref[0].astype(F32), 1.0, -1.0)
+    sign = jnp.where(pos == at_ref[0].astype(F32), 1.0, -1.0)
     margin = sign * (SLOPE * score + OFFSET)
-    loss_ref[...] = jnp.maximum(-margin, 0.0) + jnp.log1p(jnp.exp(-jnp.abs(margin)))
+    loss = jnp.maximum(-margin, 0.0) + jnp.log1p(jnp.exp(-jnp.abs(margin)))
     coeff = -SLOPE * sign / (1.0 + jnp.exp(margin)) * mask / lens
     scale = (coeff / total).T
-    for b in range(blocks):
+    scale_ref[...] = scale
+    first = at_ref[1] == 0
+    for block in range(blocks):
+        group = lax.rem(at_ref[0] + blocks - block, blocks)
+        at = block * per
+        column = jnp.where(first, scale[:, at : at + 1], scale[:, at + 1 : at + 2])
+        part_ref[group] = ((keep_ref[block] + got_ref[block].astype(F32)) * column).astype(BF16)
+        loss_ref[group] = loss[at : at + per]
+
+
+def scales(sums, keep, got, packed, place, slots):
+    blocks, rows = len(packed), packed[0].shape[0] - EXTRA
+    return pl.pallas_call(
+        lambda *refs: scale_kernel(slots, blocks, *refs),
+        in_specs=[SMEM] + [VMEM] * (3 + blocks),
+        out_specs=[VMEM] * 3,
+        out_shape=[
+            jax.ShapeDtypeStruct(keep.shape, BF16),
+            jax.ShapeDtypeStruct((E, blocks * rows // E), F32),
+            jax.ShapeDtypeStruct((blocks, rows // E, E), F32),
+        ],
+        compiler_params=limit(8),
+        name="scales",
+    )(place, sums, keep, got, *packed)
+
+
+def keys_kernel(gain, blocks, scale_ref, expo_ref, *refs):
+    packed_refs, (out_ref, expo_s, sem) = refs[:blocks], refs[blocks:]
+    for block in range(blocks):
+        pltpu.make_async_copy(expo_ref.at[block], expo_s.at[block], sem.at[block]).start()
+    rows = packed_refs[0].shape[0] - EXTRA
+    per = rows // E
+    total = jnp.zeros((E, expo_ref.shape[2]), F32)
+    for block in range(blocks):
+        parts = []
         for part in range(per):
-            at = b * per + part
-            column = scale[:, at : at + 1]
-            down = slice(part * E, (part + 1) * E)
-            flat = slice(at * E, (at + 1) * E)
-            part_ref[b, down, :] = (blend_ref[flat, :] * column).astype(BF16)
-            scaled = packed_ref[b, down, :].astype(F32) * column
-            qt_ref[:, flat] = scaled.T.astype(BF16)
-
-
-def scales(sums, packed, blend, video_id, slots):
-    blocks, rows, _ = packed.shape
-    rows = rows - EXTRA
-    vmem = pl.BlockSpec(memory_space=pltpu.VMEM)
-    return pl.pallas_call(
-        lambda *refs: scale_kernel(slots, *refs),
-        in_specs=[pl.BlockSpec(memory_space=pltpu.SMEM), vmem, vmem, vmem],
-        out_specs=[vmem, vmem, vmem],
-        out_shape=[
-            jax.ShapeDtypeStruct((blocks, rows, E), BF16),
-            jax.ShapeDtypeStruct((E, blocks * rows), BF16),
-            jax.ShapeDtypeStruct(sums.shape[1:], F32),
-        ],
-        compiler_params=pltpu.CompilerParams(vmem_limit_bytes=32 * 2**20),
-        name="scales",
-    )(video_id, sums, packed, blend)
-
-
-def keys_kernel(gain, qt_ref, expo_ref, out_ref, acc_ref):
-    step = pl.program_id(0)
-    product = dot(qt_ref[...], expo_ref[...])
-
-    @pl.when(step == 0)
-    def _():
-        acc_ref[...] = product
-
-    @pl.when(step > 0)
-    def _():
-        acc_ref[...] += product
-
-    @pl.when(step == pl.num_programs(0) - 1)
-    def _():
-        out_ref[...] = (acc_ref[...].T * gain).astype(BF16)
-
-
-def keys(qt, expo, gain):
-    rows, tokens = expo.shape
-    return pl.pallas_call(
-        lambda *refs: keys_kernel(gain, *refs),
-        grid=(rows // TILE,),
-        in_specs=[
-            pl.BlockSpec((E, TILE), lambda b: (0, b)),
-            pl.BlockSpec((TILE, tokens), lambda b: (b, 0)),
-        ],
-        out_specs=pl.BlockSpec((tokens, E), lambda b: (0, 0)),
+            at = block * per + part
+            query = packed_refs[block][part * E : (part + 1) * E, :].astype(F32)
+            parts.append((query * scale_ref[:, at : at + 1]).T.astype(BF16))
+        pltpu.make_async_copy(expo_ref.at[block], expo_s.at[block], sem.at[block]).wait()
+        total = total + dot(jnp.concatenate(parts, axis=1), expo_s[block])
+    out_ref[...] = (total.T * gain).astype(BF16)
+
+
+def keys(scale, expo, packed, gain):
+    tokens = expo.shape[2]
+    return pl.pallas_call(
+        lambda *refs: keys_kernel(gain, len(packed), *refs),
+        in_specs=[VMEM, HBM] + [VMEM] * len(packed),
+        out_specs=VMEM,
         out_shape=jax.ShapeDtypeStruct((tokens, E), BF16),
-        scratch_shapes=[pltpu.VMEM((E, tokens), F32)],
-        compiler_params=pltpu.CompilerParams(vmem_limit_bytes=32 * 2**20),
+        scratch_shapes=[
+            pltpu.VMEM(expo.shape, BF16),
+            pltpu.SemaphoreType.DMA((len(packed),)),
+        ],
+        compiler_params=limit(16),
         name="keys",
-    )(qt, expo)
+    )(scale, pltpu.with_memory_space_constraint(expo, pltpu.HBM), *packed)
+
+
+def fold_kernel(gain, in_ref, out_ref):
+    total = jnp.sum(in_ref[...].astype(F32), axis=0) * gain
+    for copy in range(out_ref.shape[0]):
+        out_ref[copy] = total.astype(BF16)
+
+
+def fold(parts, gain, copies):
+    return pl.pallas_call(
+        lambda *refs: fold_kernel(gain, *refs),
+        in_specs=[VMEM],
+        out_specs=VMEM,
+        out_shape=jax.ShapeDtypeStruct((copies,) + parts.shape[1:], BF16),
+        compiler_params=limit(4),
+        name="fold",
+    )(parts)
 
 
 def body(
@@ -372,31 +389,41 @@
     frames = frames_dev * shards
     query_dev, slots, _ = queries.shape
     rows = query_dev * slots
-
-    mine = pack_queries(queries.reshape(rows, E), query_len, positive, blocks)
-    packed = lax.all_to_all(mine, "dp", 0, 0, tiled=True)
+    core = lax.rem(lax.axis_index("seq"), 2)
+    place = jnp.stack([lax.axis_index("dp"), core]).astype(jnp.int32)
+    partner = [(i, i ^ 1) for i in range(shards)]
+    chips = [[2 * chip + own for chip in range(shards // 2)] for own in range(2)]
 
     spatial = space(video[0], space_qkv, space_out, shards)
+    spatial, flat = lax.optimization_barrier((spatial, queries.reshape(rows, E)))
     items = lax.all_to_all(spatial, "seq", 0, 0, tiled=True)
+    mine = pack_queries(flat, query_len, positive)
+    packed = [mine] + [
+        lax.ppermute(mine, "dp", [(i, (i + by) % blocks) for i in range(blocks)])
+        for by in range(1, blocks)
+    ]
     khat = time(items.reshape(-1, D), time_qkv, time_out, proj_weight, patch_loc)
 
-    expo, blend, sums = terms(packed, khat)
-    sums = sums.reshape(-1, E)
-    sums = lax.all_to_all(
-        jnp.broadcast_to(sums[None], (shards,) + sums.shape), "seq", 0, 0, tiled=True
-    )
-    video_id = lax.axis_index("dp").astype(jnp.int32).reshape(1)
-    parts, qt, loss = scales(sums, packed, blend, video_id, slots)
+    expo, keep, send, sums = terms(packed, khat, place, shards)
+    sums = lax.all_to_all(sums, "seq", 0, 0, tiled=True)
+    got = lax.ppermute(send, "seq", partner)
+    parts, scale, loss = scales(sums, keep, got, packed, place, slots)
     parts = lax.all_to_all(parts, "dp", 0, 0, tiled=True)
-    video_grad = keys(qt, expo, float(frames * P_SIZE)).reshape(1, frames, patch_loc, E)
-    summed = jnp.sum(parts.astype(F32), axis=0).astype(BF16)
-    summed = lax.all_to_all(
-        jnp.broadcast_to(summed[None], (shards,) + summed.shape), "seq", 0, 0, tiled=True
-    )
-    total = jnp.sum(summed.astype(F32), axis=0)
-    query_grad = (slots * total).astype(BF16).reshape(query_dev, slots, E)
-    pair_loss = loss[:, ::slots].reshape(-1, 1)
-    return (video_grad, query_grad, pair_loss)
+    video_grad = keys(scale, expo, packed, float(frames * P_SIZE))
+    halves = fold(parts, 1.0, shards // 2)
+    halves = lax.all_to_all(halves, "seq", 0, 0, tiled=True, axis_index_groups=chips)
+    halves, video_grad = lax.optimization_barrier((halves, video_grad))
+    half = fold(halves, float(slots), 1)[0]
+    other = lax.ppermute(half, "seq", partner)
+    first = core == 0
+    query_grad = jnp.concatenate(
+        [jnp.where(first, half, other), jnp.where(first, other, half)], axis=0
+    )
+    return (
+        video_grad.reshape(1, frames, patch_loc, E),
+        query_grad.reshape(query_dev, slots, E),
+        loss[:, :, ::slots].reshape(-1, 1),
+    )
 
 
 def solution(mesh):

time: 132 us -> 115 us (0.87)
  waiting for transfers between devices: 39.6 us -> 19.3 us
  blocking collectives: 13.2 us -> 25.1 us
  Pallas kernels: 40.7 us -> 37 us
  local copies, waits for them, and re-layouts: 11 us -> 7.39 us
    all_to_all x1, waiting for transfers between devices: 20.9 us -> 0.7 us  [body(): items = lax.all_to_all(spatial, 'seq', 0, 0, tiled=True)]
    all_to_all x3 -> x1, waiting for transfers between devices: 18.7 us -> 3.62 us  [body(): lax.all_to_all(halves, 'seq', 0, 0, tiled=True, axis_index_groups=chips)]
    ppermute x0 -> x9, waiting for transfers between devices: none -> 14.9 us  [the longest x7 14.8 us: body(): lax.ppermute(mine, 'dp', [(i, (i + by) % blocks) for i in range(blocks)])]
    all_to_all x0 -> x1, blocking collectives: none -> 14.9 us  [body(): sums = lax.all_to_all(sums, 'seq', 0, 0, tiled=True)]
    all_to_all x3 -> x1, starting transfers between devices: 15.9 us -> 3.41 us  [body(): lax.all_to_all(halves, 'seq', 0, 0, tiled=True, axis_index_groups=chips)]
    ppermute x0 -> x9, starting transfers between devices: none -> 11.8 us  [the longest x7 8.21 us: body(): lax.ppermute(mine, 'dp', [(i, (i + by) % blocks) for i in range(blocks)])]
    all_to_all x1, blocking collectives: 13.2 us -> 10.3 us  [body(): parts = lax.all_to_all(parts, 'dp', 0, 0, tiled=True)]
    pallas_call x1, Pallas kernels: 15.9 us -> 13.8 us  [time(): pl.pallas_call(time_kernel, grid=(2 * tiles,), in_specs=[pl.BlockSpec((TI...]
  transfers between devices with their start and end apart: 4 -> 11, of which waited for: 3 -> 4; matrix products, arithmetic and copies ran while one was open for 1% -> 1% of each run, Pallas kernels for 16% -> 17%
where the time goes in v1:
time: 115 us
  Pallas kernels  37 us (32%)
  blocking collectives  25.1 us (22%)
  starting transfers between devices  24.5 us (21%)
  waiting for transfers between devices  19.3 us (17%)
  local copies, waits for them, and re-layouts  7.39 us (6%)
    all_to_all x1, blocking collectives, body(): sums = lax.all_to_all(sums, 'seq', 0, 0, tiled=True)  14.9 us
    ppermute x7, waiting for transfers between devices, body(): lax.ppermute(mine, 'dp', [(i, (i + by) % blocks) for i in range(blocks)])  14.8 us
    pallas_call x1, Pallas kernels, time(): pl.pallas_call(time_kernel, grid=(2 * tiles,), in_specs=[pl.BlockSpec((TI...  13.8 us
    pallas_call x1, Pallas kernels, space(): pl.pallas_call(space_kernel, grid=(frames,), in_specs=[pl.BlockSpec((1, p...  12.1 us
    all_to_all x1, blocking collectives, body(): parts = lax.all_to_all(parts, 'dp', 0, 0, tiled=True)  10.3 us
    all_to_all x1, starting transfers between devices, body(): items = lax.all_to_all(spatial, 'seq', 0, 0, tiled=True)  9.26 us
    ppermute x7, starting transfers between devices, body(): lax.ppermute(mine, 'dp', [(i, (i + by) % blocks) for i in range(blocks)])  8.21 us
    unnamed x14, local copies, waits for them, and re-layouts  6.68 us
  transfers between devices with their start and end apart: 11, of which 4 were waited for; matrix products, arithmetic and copies ran while one was open for 1% of the time, Pallas kernels for 17%

profile of v1, /device:TPU:1, one launch (start us, length us, event | category | flops | bytes accessed | tf_op | source)
XLA Modules:
  0.0 114.7 jit_solution(17608571272464539210)
XLA Ops:
  0.6 2.0 %copy-done.1 = bf16[768,2304]{1,0:T(8,128)(2,1)S(1)} copy-done((bf16[768,2304]{1,0:T(8,128)(2,1)S(1)}, bf16[768,2304]{1,0:T(8,128)(2,1)}, u32[]{:S(2)}) %copy-start.1) | copy-done | bytes 3538968
  2.6 1.4 %copy-done.2 = bf16[1,4,256,768]{3,2,1,0:T(8,128)(2,1)S(1)} copy-done((bf16[1,4,256,768]{3,2,1,0:T(8,128)(2,1)S(1)}, bf16[1,4,256,768]{3,2,1,0:T(8,128)(2,1)}, u32[]{:S(2)}) %copy-start.2) | copy-done | bytes 1572888
  4.0 1.3 %copy-done.4 = bf16[768,768]{1,0:T(8,128)(2,1)S(1)} copy-done((bf16[768,768]{1,0:T(8,128)(2,1)S(1)}, bf16[768,768]{1,0:T(8,128)(2,1)}, u32[]{:S(2)}) %copy-start.4) | copy-done | bytes 1179672
  5.3 12.1 %space.1 = bf16[16,4,16,768]{3,2,1,0:T(8,128)(2,1)} custom-call(bf16[4,256,768]{2,1,0:T(8,128)(2,1)S(1)} %bitcast.11, bf16[768,2304]{1,0:T(8,128)(2,1)S(1)} %copy-done.1, bf16[768,768]{1,0:T(8,128)(2,1)S(1)} %copy-done.4), custom_call_target="tpu_custom_call" | custom-call | tf_op jit(solution)/shard_map/space/pallas_call | solution.py:105
  17.5 9.3 %all-to-all-start = ((bf16[16,4,16,768]{3,2,1,0:T(8,128)(2,1)}), bf16[16,4,16,768]{3,2,1,0:T(8,128)(2,1)S(1)}, u32[]{:S(2)}, u32[]{:S(2)}) async-start(bf16[16,4,16,768]{3,2,1,0:T(8,128)(2,1)} %space.1), calls=%async_computation | async-start | bytes 3145728 | tf_op jit(solution)/shard_map/all_to_all | solution.py:399
  26.7 1.6 %pack_queries.1.refs_2_.refs_4_ = bf16[272,128]{1,0:T(8,128)(2,1)} custom-call(s32[8]{0:T(128)} %len_ref.1, s32[8]{0:T(128)} %pos_ref.1, bf16[256,128]{1,0:T(8,128)(2,1)} %bitcast.14), custom_call_target="tpu_custom_call" | custom-call | tf_op jit(solution)/shard_map/pack_queries/pallas_call | solution.py:219
  28.3 3.2 %collective-permute-start.6 = (bf16[272,128]{1,0:T(8,128)(2,1)}, bf16[272,128]{1,0:T(8,128)(2,1)S(1)}, u32[]{:S(2)}, u32[]{:S(2)}) collective-permute-start(bf16[272,128]{1,0:T(8,128)(2,1)} %pack_queries.1.refs_2_.refs_4_), channel_id=1, source_target_pairs={{0,112},{16,0},{32,16},{48,32},{64,48},{80,64},{96,80},{112,96},{1... | collective-permute-start | bytes 208904 | tf_op jit(solution)/shard_map/ppermute | solution.py:402
  31.5 0.5 collective-permute-start.5
  32.0 0.6 collective-permute-start.4
  32.6 2.6 %collective-permute-start.3 = (bf16[272,128]{1,0:T(8,128)(2,1)}, bf16[272,128]{1,0:T(8,128)(2,1)S(1)}, u32[]{:S(2)}, u32[]{:S(2)}) collective-permute-start(bf16[272,128]{1,0:T(8,128)(2,1)} %pack_queries.1.refs_2_.refs_4_), channel_id=1, source_target_pairs={{0,64},{16,80},{32,96},{48,112},{64,0},{80,16},{96,32},{112,48},{1... | collective-permute-start | bytes 208904 | tf_op jit(solution)/shard_map/ppermute | solution.py:402
  35.2 0.0 collective-permute-start.2
  35.2 14.8 %collective-permute-done.6.refs_9_.refs_11_ = bf16[272,128]{1,0:T(8,128)(2,1)S(1)} collective-permute-done((bf16[272,128]{1,0:T(8,128)(2,1)}, bf16[272,128]{1,0:T(8,128)(2,1)S(1)}, u32[]{:S(2)}, u32[]{:S(2)}) %collective-permute-start.6) | collective-permute-done | bytes 69664 | tf_op jit(solution)/shard_map/ppermute | solution.py:402
  50.0 1.3 %collective-permute-start.1 = (bf16[272,128]{1,0:T(8,128)(2,1)}, bf16[272,128]{1,0:T(8,128)(2,1)S(1)}, u32[]{:S(2)}, u32[]{:S(2)}) collective-permute-start(bf16[272,128]{1,0:T(8,128)(2,1)} %pack_queries.1.refs_2_.refs_4_), channel_id=1, source_target_pairs={{0,32},{16,48},{32,64},{48,80},{64,96},{80,112},{96,0},{112,16},{1... | collective-permute-start | bytes 208904 | tf_op jit(solution)/shard_map/ppermute | solution.py:402
  51.3 0.0 collective-permute-start
  51.3 0.1 pad_add_fusion.refs_0_
  51.4 0.7 all-to-all-done
  52.1 2.0 %copy-done = bf16[768,2304]{1,0:T(8,128)(2,1)S(1)} copy-done((bf16[768,2304]{1,0:T(8,128)(2,1)S(1)}, bf16[768,2304]{1,0:T(8,128)(2,1)}, u32[]{:S(2)}) %copy-start) | copy-done | bytes 3538968
  54.1 13.8 %time.1.refs_1_ = bf16[1024,128]{1,0:T(8,128)(2,1)S(1)} custom-call(bf16[1024,768]{1,0:T(8,128)(2,1)S(1)} %bitcast.10, bf16[768,2304]{1,0:T(8,128)(2,1)S(1)} %copy-done, bf16[768,768]{1,0:T(8,128)(2,1)S(1)} %copy-done.3, bf16[768,128]{1,0:T(8,128)(2,1)S(1)} %copy-done.6), custom_call_target="tpu_custom_call" | custom-call | tf_op jit(solution)/shard_map/time/pallas_call | solution.py:181
  68.0 3.8 %terms.1 = (bf16[8,256,1024]{2,1,0:T(8,128)(2,1)}, f32[8,128,128]{2,1,0:T(8,128)S(1)}, bf16[8,128,128]{2,1,0:T(8,128)(2,1)S(1)}, f32[16,16,128]{2,1,0:T(8,128)S(1)}) custom-call(s32[2]{0:T(128)S(1)} %pad_add_fusion.refs_0_, bf16[1024,128]{1,0:T(8,128)(2,1)S(1)} %time.1.refs_1_, bf16[272,128]{1,0:T(8,128)(2,1)S(1)} %copy-done.5, ...), custom_call_target="tpu_custom_call" | custom-call | tf_op jit(solution)/shard_map/terms/pallas_call | solution.py:260
  71.8 0.5 collective-permute-start.7
  72.2 14.9 %all_to_all.20.refs_1_ = f32[16,16,128]{2,1,0:T(8,128)S(1)} all-to-all(f32[16,16,128]{2,1,0:T(8,128)S(1)} %get-tuple-element.16), channel_id=1, replica_groups=mesh['dp'=8,'seq'=16] {'seq'}, dimensions={0} | all-to-all | bytes 262144 | tf_op jit(solution)/shard_map/all_to_all | solution.py:408
  87.1 1.2 %scales.1 = (bf16[8,128,128]{2,1,0:T(8,128)(2,1)S(1)}, f32[128,16]{1,0:T(8,128)S(1)}, f32[8,2,128]{2,1,0:T(2,128)S(1)}) custom-call(s32[2]{0:T(128)S(1)} %pad_add_fusion.refs_0_, f32[16,16,128]{2,1,0:T(8,128)S(1)} %all_to_all.20.refs_1_, f32[8,128,128]{2,1,0:T(8,128)S(1)} %get-tuple-element.17.refs_2_, ...), custom_call_target="tpu_custom_call" | custom-call | tf_op jit(solution)/shard_map/scales/pallas_call | solution.py:317
  88.3 10.3 %all_to_all.21.refs_0_ = bf16[8,128,128]{2,1,0:T(8,128)(2,1)S(1)} all-to-all(bf16[8,128,128]{2,1,0:T(8,128)(2,1)S(1)} %get-tuple-element.19), channel_id=1, replica_groups=mesh['dp'=8,'seq'=16] {'dp'}, dimensions={0} | all-to-all | bytes 524288 | tf_op jit(solution)/shard_map/all_to_all | solution.py:411
  98.5 0.8 fold.2
  99.3 3.4 %all-to-all-start.3 = ((bf16[8,128,128]{2,1,0:T(8,128)(2,1)}), bf16[8,128,128]{2,1,0:T(8,128)(2,1)S(1)}, u32[]{:S(2)}, u32[]{:S(2)}) async-start(bf16[8,128,128]{2,1,0:T(8,128)(2,1)} %fold.2), calls=%async_computation.3 | async-start | bytes 524288 | tf_op jit(solution)/shard_map/all_to_all | solution.py:414
  102.7 3.7 %keys.1 = bf16[1024,128]{1,0:T(8,128)(2,1)} custom-call(f32[128,16]{1,0:T(8,128)S(1)} %get-tuple-element.20.refs_0_, bf16[8,256,1024]{2,1,0:T(8,128)(2,1)} %get-tuple-element.21.refs_1_, bf16[272,128]{1,0:T(8,128)(2,1)S(1)} %copy-done.5, bf16[272,128]{1,0:T(8,128)(2,1)S(1)} %collective-permute-done.refs_3_.refs_5_, ...), custom_call_target="tpu_custom_call" | custom-call | tf_op jit(solution)/shard_map/keys/pallas_call | solution.py:351
  106.4 3.6 %all-to-all-done.3.refs_0_ = bf16[8,128,128]{2,1,0:T(8,128)(2,1)S(1)} async-done(((bf16[8,128,128]{2,1,0:T(8,128)(2,1)}), bf16[8,128,128]{2,1,0:T(8,128)(2,1)S(1)}, u32[]{:S(2)}, u32[]{:S(2)}) %all-to-all-start.3) | async-done | bytes 262176 | tf_op jit(solution)/shard_map/all_to_all | solution.py:414
  110.1 3.1 %collective-permute-start.8 = (bf16[128,128]{1,0:T(8,128)(2,1)S(1)}, bf16[128,128]{1,0:T(8,128)(2,1)S(1)}, u32[]{:S(2)}, u32[]{:S(2)}) collective-permute-start(bf16[128,128]{1,0:T(8,128)(2,1)S(1)} %bitcast.12), channel_id=1, source_target_pairs={{0,1},{1,0},{2,3},{3,2},{4,5},{5,4},{6,7},{7,6},{8,9},{9,8},{10,11... | collective-permute-start | bytes 98312 | tf_op jit(solution)/shard_map/ppermute | solution.py:417
  113.2 0.1 slice.3
  113.3 0.6 reshape.25
  113.9 0.2 collective-permute-done.8
  114.1 0.6 pad_maximum_fusion
  (19 shorter events, 0.1 us)
Async XLA Ops:
  0.6 2.0 %copy-start.1 = (bf16[768,2304]{1,0:T(8,128)(2,1)S(1)}, bf16[768,2304]{1,0:T(8,128)(2,1)}, u32[]{:S(2)}) copy-start(bf16[768,2304]{1,0:T(8,128)(2,1)} %qkv_ref.2) | copy-start | bytes 10616836
  2.6 1.4 %copy-start.2 = (bf16[1,4,256,768]{3,2,1,0:T(8,128)(2,1)S(1)}, bf16[1,4,256,768]{3,2,1,0:T(8,128)(2,1)}, u32[]{:S(2)}) copy-start(bf16[1,4,256,768]{3,2,1,0:T(8,128)(2,1)} %param.9) | copy-start | bytes 4718596
  4.0 1.3 %copy-start.4 = (bf16[768,768]{1,0:T(8,128)(2,1)S(1)}, bf16[768,768]{1,0:T(8,128)(2,1)}, u32[]{:S(2)}) copy-start(bf16[768,768]{1,0:T(8,128)(2,1)} %out_w_ref.2) | copy-start | bytes 3538948
  17.4 34.6 %copy-start.3 = (bf16[768,768]{1,0:T(8,128)(2,1)S(1)}, bf16[768,768]{1,0:T(8,128)(2,1)}, u32[]{:S(2)}) copy-start(bf16[768,768]{1,0:T(8,128)(2,1)} %out_w_ref.3) | copy-start | bytes 3538948
  17.5 34.6 %copy-start.6 = (bf16[768,128]{1,0:T(8,128)(2,1)S(1)}, bf16[768,128]{1,0:T(8,128)(2,1)}, u32[]{:S(2)}) copy-start(bf16[768,128]{1,0:T(8,128)(2,1)} %proj_ref.1) | copy-start | bytes 589828
  17.5 34.6 %all-to-all-start = ((bf16[16,4,16,768]{3,2,1,0:T(8,128)(2,1)}), bf16[16,4,16,768]{3,2,1,0:T(8,128)(2,1)S(1)}, u32[]{:S(2)}, u32[]{:S(2)}) async-start(bf16[16,4,16,768]{3,2,1,0:T(8,128)(2,1)} %space.1), calls=%async_computation | async-start | bytes 3145728 | tf_op jit(solution)/shard_map/all_to_all | solution.py:399
  28.3 21.7 %collective-permute-start.6 = (bf16[272,128]{1,0:T(8,128)(2,1)}, bf16[272,128]{1,0:T(8,128)(2,1)S(1)}, u32[]{:S(2)}, u32[]{:S(2)}) collective-permute-start(bf16[272,128]{1,0:T(8,128)(2,1)} %pack_queries.1.refs_2_.refs_4_), channel_id=1, source_target_pairs={{0,112},{16,0},{32,16},{48,32},{64,48},{80,64},{96,80},{112,96},{1... | collective-permute-start | bytes 208904 | tf_op jit(solution)/shard_map/ppermute | solution.py:402
  31.5 19.8 %collective-permute-start.5 = (bf16[272,128]{1,0:T(8,128)(2,1)}, bf16[272,128]{1,0:T(8,128)(2,1)S(1)}, u32[]{:S(2)}, u32[]{:S(2)}) collective-permute-start(bf16[272,128]{1,0:T(8,128)(2,1)} %pack_queries.1.refs_2_.refs_4_), channel_id=1, source_target_pairs={{0,96},{16,112},{32,0},{48,16},{64,32},{80,48},{96,64},{112,80},{1... | collective-permute-start | bytes 208904 | tf_op jit(solution)/shard_map/ppermute | solution.py:402
  32.0 35.9 %collective-permute-start.4 = (bf16[272,128]{1,0:T(8,128)(2,1)}, bf16[272,128]{1,0:T(8,128)(2,1)S(1)}, u32[]{:S(2)}, u32[]{:S(2)}) collective-permute-start(bf16[272,128]{1,0:T(8,128)(2,1)} %pack_queries.1.refs_2_.refs_4_), channel_id=1, source_target_pairs={{0,80},{16,96},{32,112},{48,0},{64,16},{80,32},{96,48},{112,64},{1... | collective-permute-start | bytes 208904 | tf_op jit(solution)/shard_map/ppermute | solution.py:402
  32.6 35.3 %collective-permute-start.3 = (bf16[272,128]{1,0:T(8,128)(2,1)}, bf16[272,128]{1,0:T(8,128)(2,1)S(1)}, u32[]{:S(2)}, u32[]{:S(2)}) collective-permute-start(bf16[272,128]{1,0:T(8,128)(2,1)} %pack_queries.1.refs_2_.refs_4_), channel_id=1, source_target_pairs={{0,64},{16,80},{32,96},{48,112},{64,0},{80,16},{96,32},{112,48},{1... | collective-permute-start | bytes 208904 | tf_op jit(solution)/shard_map/ppermute | solution.py:402
  35.2 32.7 %collective-permute-start.2 = (bf16[272,128]{1,0:T(8,128)(2,1)}, bf16[272,128]{1,0:T(8,128)(2,1)S(1)}, u32[]{:S(2)}, u32[]{:S(2)}) collective-permute-start(bf16[272,128]{1,0:T(8,128)(2,1)} %pack_queries.1.refs_2_.refs_4_), channel_id=1, source_target_pairs={{0,48},{16,64},{32,80},{48,96},{64,112},{80,0},{96,16},{112,32},{1... | collective-permute-start | bytes 208904 | tf_op jit(solution)/shard_map/ppermute | solution.py:402
  50.0 18.0 %collective-permute-start.1 = (bf16[272,128]{1,0:T(8,128)(2,1)}, bf16[272,128]{1,0:T(8,128)(2,1)S(1)}, u32[]{:S(2)}, u32[]{:S(2)}) collective-permute-start(bf16[272,128]{1,0:T(8,128)(2,1)} %pack_queries.1.refs_2_.refs_4_), channel_id=1, source_target_pairs={{0,32},{16,48},{32,64},{48,80},{64,96},{80,112},{96,0},{112,16},{1... | collective-permute-start | bytes 208904 | tf_op jit(solution)/shard_map/ppermute | solution.py:402
  51.3 16.7 %collective-permute-start = (bf16[272,128]{1,0:T(8,128)(2,1)}, bf16[272,128]{1,0:T(8,128)(2,1)S(1)}, u32[]{:S(2)}, u32[]{:S(2)}) collective-permute-start(bf16[272,128]{1,0:T(8,128)(2,1)} %pack_queries.1.refs_2_.refs_4_), channel_id=1, source_target_pairs={{0,16},{16,32},{32,48},{48,64},{64,80},{80,96},{96,112},{112,0},{1... | collective-permute-start | bytes 208904 | tf_op jit(solution)/shard_map/ppermute | solution.py:402
  52.1 2.0 %copy-start = (bf16[768,2304]{1,0:T(8,128)(2,1)S(1)}, bf16[768,2304]{1,0:T(8,128)(2,1)}, u32[]{:S(2)}) copy-start(bf16[768,2304]{1,0:T(8,128)(2,1)} %qkv_ref.3) | copy-start | bytes 10616836
  54.1 13.9 %copy-start.5 = (bf16[272,128]{1,0:T(8,128)(2,1)S(1)}, bf16[272,128]{1,0:T(8,128)(2,1)}, u32[]{:S(2)}) copy-start(bf16[272,128]{1,0:T(8,128)(2,1)} %pack_queries.1.refs_2_.refs_4_) | copy-start | bytes 208900
  71.8 15.3 %collective-permute-start.7 = (bf16[8,128,128]{2,1,0:T(8,128)(2,1)S(1)}, bf16[8,128,128]{2,1,0:T(8,128)(2,1)S(1)}, u32[]{:S(2)}, u32[]{:S(2)}) collective-permute-start(bf16[8,128,128]{2,1,0:T(8,128)(2,1)S(1)} %get-tuple-element.18), channel_id=1, source_target_pairs={{0,1},{1,0},{2,3},{3,2},{4,5},{5,4},{6,7},{7,6},{8,9},{9,8},{10,11... | collective-permute-start | bytes 786440 | tf_op jit(solution)/shard_map/ppermute | solution.py:409
  99.3 10.7 %all-to-all-start.3 = ((bf16[8,128,128]{2,1,0:T(8,128)(2,1)}), bf16[8,128,128]{2,1,0:T(8,128)(2,1)S(1)}, u32[]{:S(2)}, u32[]{:S(2)}) async-start(bf16[8,128,128]{2,1,0:T(8,128)(2,1)} %fold.2), calls=%async_computation.3 | async-start | bytes 524288 | tf_op jit(solution)/shard_map/all_to_all | solution.py:414
  110.1 4.0 %collective-permute-start.8 = (bf16[128,128]{1,0:T(8,128)(2,1)S(1)}, bf16[128,128]{1,0:T(8,128)(2,1)S(1)}, u32[]{:S(2)}, u32[]{:S(2)}) collective-permute-start(bf16[128,128]{1,0:T(8,128)(2,1)S(1)} %bitcast.12), channel_id=1, source_target_pairs={{0,1},{1,0},{2,3},{3,2},{4,5},{5,4},{6,7},{7,6},{8,9},{9,8},{10,11... | collective-permute-start | bytes 98312 | tf_op jit(solution)/shard_map/ppermute | solution.py:417

commit v2 on v1

v2 whole, which is shorter than its diff:
```python
import jax
import jax.numpy as jnp
from jax import lax
from jax.experimental import pallas as pl
from jax.experimental.pallas import tpu as pltpu
from jax.sharding import PartitionSpec as P

HEADS = 12
P_SIZE = 256
TEMPER = 0.05
SLOPE = 10.0
OFFSET = -5.0
SHARP = 10.0
LOG2E = 1.4426950408889634

D = 768
HEAD = D // HEADS
PAIR = 2 * HEAD
PAIRS = HEADS // 2
TILE = 256
SUB = 128
E = 128
F32 = jnp.float32
BF16 = jnp.bfloat16
VMEM = pl.BlockSpec(memory_space=pltpu.VMEM)
SMEM = pl.BlockSpec(memory_space=pltpu.SMEM)
HBM = pl.BlockSpec(memory_space=pltpu.HBM)


def limit(mib):
    return pltpu.CompilerParams(vmem_limit_bytes=mib * 2**20)


def dot(a, b):
    return lax.dot_general(a, b, (((1,), (0,)), ((), ())), preferred_element_type=F32)


def dot_t(a, b):
    return lax.dot_general(a, b, (((1,), (1,)), ((), ())), preferred_element_type=F32)


def iota(shape, dim):
    return lax.broadcasted_iota(jnp.int32, shape, dim)


def layer_norm(tokens):
    values = tokens.astype(F32)
    center = values - jnp.mean(values, axis=-1, keepdims=True)
    spread = jnp.mean(center * center, axis=-1, keepdims=True)
    return (center * lax.rsqrt(spread + 1e-05)).astype(BF16)


def unit_heads(values, gain):
    same = (iota((TILE, TILE), 0) // HEAD == iota((TILE, TILE), 1) // HEAD).astype(BF16)
    parts = []
    for at in range(0, values.shape[1], TILE):
        part = values[:, at : at + TILE]
        squares = dot((part * part).astype(BF16), same)
        parts.append((part * (lax.rsqrt(squares + 1e-06) * gain)).astype(BF16))
    return jnp.concatenate(parts, axis=1)


def pair_blend(query, key, value, keep):
    extent = key.shape[0]
    low = iota((extent, PAIR), 1) < HEAD
    zero = jnp.zeros((extent, PAIR), BF16)
    one = jnp.ones((extent, PAIR), BF16)
    keys = jnp.concatenate([jnp.where(low, key, zero), jnp.where(low, zero, key)], axis=0)
    values = jnp.concatenate(
        [
            jnp.concatenate([jnp.where(low, value, zero), jnp.where(low, one, zero)], axis=1),
            jnp.concatenate([jnp.where(low, zero, value), jnp.where(low, zero, one)], axis=1),
        ],
        axis=0,
    )
    weights = jnp.exp2(dot_t(query, keys))
    if keep is not None:
        weights = jnp.where(keep, weights, 0.0)
    mixed = dot(weights.astype(BF16), values)
    return (mixed[:, :PAIR] / mixed[:, PAIR:]).astype(BF16)


def fetch(pairs, sem):
    copies = [pltpu.make_async_copy(a, b, sem.at[i]) for i, (a, b) in enumerate(pairs)]
    for copy in copies:
        copy.start()
    return copies


def columns(ref, third):
    return ref.at[:, pl.ds(third * D, D)]


def in_hbm(*arrays):
    return [pltpu.with_memory_space_constraint(array, pltpu.HBM) for array in arrays]


def qkv_all(normed, weight_s, copies, outs):
    for third, (out, gain) in enumerate(zip(outs, (SHARP * LOG2E, 1.0, None))):
        copies[third].wait()
        part = dot(normed, weight_s[:, third * D : (third + 1) * D])
        out[...] = part.astype(BF16) if gain is None else unit_heads(part, gain)


def space_kernel(
    video_ref, qkv_ref, out_w_ref, out_ref, x_s, qkv_s, w_s, n_s, q_s, k_s, v_s, y_s, sem, out_sem
):
    frames, patches, _ = x_s.shape
    video = fetch([(video_ref.at[f], x_s.at[f]) for f in range(frames)], sem)
    weights = fetch(
        [(columns(qkv_ref, i), columns(qkv_s, i)) for i in range(3)] + [(out_w_ref, w_s)],
        sem.at[pl.ds(frames, 4)],
    )
    for f in range(frames):
        video[f].wait()
        n_s[f * patches : (f + 1) * patches, :] = layer_norm(x_s[f])
    qkv_all(n_s[...], qkv_s, weights, (q_s, k_s, v_s))
    weights[3].wait()
    stores = []
    for f in range(frames):
        down = slice(f * patches, (f + 1) * patches)
        blended = []
        for pair in range(PAIRS):
            at = slice(pair * PAIR, (pair + 1) * PAIR)
            blended.append(pair_blend(q_s[down, at], k_s[down, at], v_s[down, at], None))
        update = dot(jnp.concatenate(blended, axis=1), w_s[...])
        y_s[f] = (x_s[f].astype(F32) + update).astype(BF16).reshape(y_s.shape[1:])
        stores.append(pltpu.make_async_copy(y_s.at[f], out_ref.at[:, f], out_sem.at[f]))
        stores[-1].start()
    for store in stores:
        store.wait()


def space(video, qkv_weight, out_weight, shards):
    frames, patches, _ = video.shape
    local = patches // shards
    return pl.pallas_call(
        space_kernel,
        in_specs=[HBM] * 3,
        out_specs=HBM,
        out_shape=pltpu.HBM((shards, frames, local, D), BF16),
        scratch_shapes=[
            pltpu.VMEM((frames, patches, D), BF16),
            pltpu.VMEM((D, 3 * D), BF16),
            pltpu.VMEM((D, D), BF16),
        ]
        + [pltpu.VMEM((frames * patches, D), BF16)] * 4
        + [
            pltpu.VMEM((frames, shards, local, D), BF16),
            pltpu.SemaphoreType.DMA((frames + 4,)),
            pltpu.SemaphoreType.DMA((frames,)),
        ],
        compiler_params=limit(40),
        name="space",
    )(*in_hbm(video, qkv_weight, out_weight))


def swap_rows(rows, side):
    extent = side * side
    row, col = iota((extent, extent), 0), iota((extent, extent), 1)
    swap = (col == (row % side) * side + row // side).astype(BF16)
    return dot(swap, rows).astype(BF16)


def time_kernel(
    x_ref, qkv_ref, out_w_ref, proj_ref, khat_ref,
    x_s, n_s, qkv_s, w_s, p_s, q_s, k_s, v_s, b_s, kh_s, sem,
):
    side, frames, _ = x_s.shape
    rows = x_ref.shape[0]
    weights = fetch(
        [(columns(qkv_ref, i), columns(qkv_s, i)) for i in range(3)]
        + [(out_w_ref, w_s), (proj_ref, p_s)],
        sem,
    )
    for tile in range(rows // TILE):
        tokens = swap_rows(x_ref[tile * TILE : (tile + 1) * TILE, :], side)
        at = slice(tile * side, (tile + 1) * side)
        x_s[:, at, :] = tokens.reshape(side, side, D)
        n_s[:, at, :] = layer_norm(tokens).reshape(side, side, D)
    qkv_all(n_s[...].reshape(rows, D), qkv_s, weights, (q_s, k_s, v_s))
    keep = iota((SUB, 2 * SUB), 0) // frames == (iota((SUB, 2 * SUB), 1) % SUB) // frames
    for sub in range(rows // SUB):
        down = slice(sub * SUB, (sub + 1) * SUB)
        for pair in range(PAIRS):
            at = slice(pair * PAIR, (pair + 1) * PAIR)
            b_s[down, at] = pair_blend(q_s[down, at], k_s[down, at], v_s[down, at], keep)
    weights[3].wait()
    weights[4].wait()
    update = dot(b_s[...], w_s[...])
    mixed = (x_s[...].reshape(rows, D).astype(F32) + update).astype(BF16)
    projected = dot(layer_norm(mixed), p_s[...])
    norm = jnp.sum(projected * projected, axis=-1, keepdims=True)
    kh_s[...] = (projected * lax.rsqrt(norm + 1e-06)).astype(BF16).reshape(kh_s.shape)
    for tile in range(rows // TILE):
        part = kh_s[:, tile * side : (tile + 1) * side, :].reshape(TILE, E)
        khat_ref[tile * TILE : (tile + 1) * TILE, :] = swap_rows(part, side)


def time(x, qkv_weight, out_weight, proj_weight, patches):
    rows = x.shape[0]
    frames = rows // patches
    return pl.pallas_call(
        time_kernel,
        in_specs=[VMEM] + [HBM] * 3,
        out_specs=VMEM,
        out_shape=jax.ShapeDtypeStruct((rows, E), BF16),
        scratch_shapes=[
            pltpu.VMEM((patches, frames, D), BF16),
            pltpu.VMEM((patches, frames, D), BF16),
            pltpu.VMEM((D, 3 * D), BF16),
            pltpu.VMEM((D, D), BF16),
            pltpu.VMEM((D, E), BF16),
        ]
        + [pltpu.VMEM((rows, D), BF16)] * 4
        + [pltpu.VMEM((patches, frames, E), BF16), pltpu.SemaphoreType.DMA((5,))],
        compiler_params=limit(40),
        name="time",
    )(x, *in_hbm(qkv_weight, out_weight, proj_weight))


EXTRA = 16


def query_kernel(len_ref, pos_ref, q_ref, out_ref):
    rows = q_ref.shape[0]
    values = q_ref[...].astype(F32)
    norm = jnp.sum(values * values, axis=-1, keepdims=True)
    out_ref[:rows, :] = (values / jnp.sqrt(norm + 1e-06)).astype(BF16)
    slots = rows // len_ref.shape[0]
    row, lane = iota((EXTRA, E), 0), iota((EXTRA, E), 1)
    owner = ((row % 2) * E + lane) // slots
    extra = jnp.zeros((EXTRA, E), F32)
    for query in range(len_ref.shape[0]):
        picked = jnp.where(row < 2, len_ref[query], pos_ref[query]).astype(F32)
        extra = jnp.where((owner == query) & (row < 4), picked, extra)
    out_ref[rows:, :] = extra.astype(BF16)


def pack_queries(queries, query_len, positive):
    rows = queries.shape[0]
    return pl.pallas_call(
        query_kernel,
        in_specs=[SMEM, SMEM, VMEM],
        out_specs=VMEM,
        out_shape=jax.ShapeDtypeStruct((rows + EXTRA, E), BF16),
        name="pack_queries",
    )(query_len, positive, queries)


def group_of(mine, blocks, block):
    return lax.rem(mine + blocks - block // 2 * 2, blocks) ^ (block % 2)


def terms_kernel(blocks, at_ref, khat_ref, *refs):
    packed_refs = refs[: blocks // 2]
    expo_ref, keep_ref, send_ref, sums_ref, expo_s, sem = refs[blocks // 2 :]
    rows = expo_s.shape[1]
    first = at_ref[1] == 0
    khat = khat_ref[...]
    wide = jnp.concatenate([khat, jnp.ones_like(khat)], axis=1)
    gain = LOG2E / TEMPER
    eye = iota((E, E), 0) == iota((E, E), 1)
    sums = []
    for block in range(blocks):
        dots = dot_t(packed_refs[block // 2][block % 2, :rows, :], khat)
        expo = jnp.exp2(dots * gain - gain).astype(BF16)
        expo_s[block] = expo
        pltpu.make_async_copy(expo_s.at[block], expo_ref.at[block], sem.at[block]).start()
        both = dot(expo, wide)
        low, high = both[:E, :E], both[E:, :E]
        keep_ref[block] = jnp.where(first, low, high)
        send_ref[block] = jnp.where(first, high, low).astype(BF16)
        for part in range(rows // E):
            square = both[part * E : (part + 1) * E, E:]
            sums.append(jnp.sum(jnp.where(eye, square, 0.0), axis=0, keepdims=True))
    sums_ref[...] = jnp.concatenate(sums, axis=0)
    for block in range(blocks):
        pltpu.make_async_copy(expo_s.at[block], expo_ref.at[block], sem.at[block]).wait()


def terms(packed, khat, place):
    blocks, rows = 2 * len(packed), packed[0].shape[1] - EXTRA
    tokens = khat.shape[0]
    return pl.pallas_call(
        lambda *refs: terms_kernel(blocks, *refs),
        in_specs=[SMEM] + [VMEM] * (1 + len(packed)),
        out_specs=[HBM] + [VMEM] * 3,
        out_shape=[
            pltpu.HBM((blocks, rows, tokens), BF16),
            jax.ShapeDtypeStruct((blocks, rows // 2, E), F32),
            jax.ShapeDtypeStruct((blocks, rows // 2, E), BF16),
            jax.ShapeDtypeStruct((blocks * rows // E, E), F32),
        ],
        scratch_shapes=[
            pltpu.VMEM((blocks, rows, tokens), BF16),
            pltpu.SemaphoreType.DMA((blocks,)),
        ],
        compiler_params=limit(16),
        name="terms",
    )(place, khat, *packed)


def join_kernel(keep_ref, got_ref, sums_ref, others_ref, out_ref):
    blocks, half, _ = keep_ref.shape
    chips = out_ref.shape[0]
    piece = half // chips
    sums = sums_ref[...] + others_ref[...]
    upper = sums.astype(BF16)
    lower = (sums - upper.astype(F32)).astype(BF16)
    notes = jnp.concatenate([upper, lower], axis=0)
    for block in range(blocks):
        both = (keep_ref[block] + got_ref[block].astype(F32)).astype(BF16)
        for chip in range(chips):
            out_ref[chip, block * piece : (block + 1) * piece, :] = both[
                chip * piece : (chip + 1) * piece
            ]
    for chip in range(chips):
        out_ref[chip, blocks * piece :, :] = notes


def join(keep, got, sums, others, chips):
    blocks, half, _ = keep.shape
    return pl.pallas_call(
        join_kernel,
        in_specs=[VMEM] * 4,
        out_specs=VMEM,
        out_shape=jax.ShapeDtypeStruct(
            (chips, blocks * half // chips + 2 * sums.shape[0], E), BF16
        ),
        compiler_params=limit(8),
        name="join",
    )(keep, got, sums, others)


def scale_kernel(slots, at_ref, got_ref, *refs):
    packed_refs, (part_ref, scale_ref, loss_ref) = refs[:-3], refs[-3:]
    blocks, shards, piece, _ = part_ref.shape
    rows = packed_refs[0].shape[1] - EXTRA
    per = rows // E
    got = jnp.sum(got_ref[...].astype(F32), axis=0)
    blend, notes = got[: blocks * piece], got[blocks * piece :]
    total = notes[: blocks * per] + notes[blocks * per :]
    notes = [packed_refs[b // 2][b % 2, rows:, :].astype(F32) for b in range(blocks)]
    lens = jnp.concatenate([note[:per] for note in notes], axis=0)
    pos = jnp.concatenate([note[per : 2 * per] for note in notes], axis=0)
    mask = ((iota(total.shape, 1) % slots).astype(F32) < lens).astype(F32)
    smooth = (1.0 + TEMPER * jnp.log(total)) * mask
    same = (iota((E, E), 0) // slots == iota((E, E), 1) // slots).astype(F32)
    score = (
        lax.dot_general(
            smooth,
            same,
            (((1,), (0,)), ((), ())),
            preferred_element_type=F32,
            precision=lax.Precision.HIGHEST,
        )
        / lens
    )
    sign = jnp.where(pos == at_ref[0].astype(F32), 1.0, -1.0)
    margin = sign * (SLOPE * score + OFFSET)
    loss = jnp.maximum(-margin, 0.0) + jnp.log1p(jnp.exp(-jnp.abs(margin)))
    coeff = -SLOPE * sign / (1.0 + jnp.exp(margin)) * mask / lens
    scale_ref[...] = (coeff / total).T
    scale = scale_ref[pl.ds(pl.multiple_of(at_ref[2] * piece, piece), piece), :]
    first = at_ref[1] == 0
    for block in range(blocks):
        group = group_of(at_ref[0], blocks, block)
        at = block * per
        column = jnp.where(first, scale[:, at : at + 1], scale[:, at + 1 : at + 2])
        part = (blend[block * piece : (block + 1) * piece] * column).astype(BF16)
        for shard in range(shards):
            part_ref[group, shard] = part
        loss_ref[group] = loss[at : at + per]


def scales(got, packed, place, slots, shards):
    blocks, rows = 2 * len(packed), packed[0].shape[1] - EXTRA
    piece = rows // shards
    return pl.pallas_call(
        lambda *refs: scale_kernel(slots, *refs),
        in_specs=[SMEM] + [VMEM] * (1 + len(packed)),
        out_specs=[VMEM] * 3,
        out_shape=[
            jax.ShapeDtypeStruct((blocks, shards, piece, E), BF16),
            jax.ShapeDtypeStruct((E, blocks * rows // E), F32),
            jax.ShapeDtypeStruct((blocks, rows // E, E), F32),
        ],
        compiler_params=limit(8),
        name="scales",
    )(place, got, *packed)


def keys_kernel(gain, blocks, scale_ref, expo_ref, *refs):
    packed_refs, (out_ref, expo_s, sem) = refs[:-3], refs[-3:]
    copies = fetch([(expo_ref.at[b], expo_s.at[b]) for b in range(blocks)], sem)
    rows = expo_s.shape[1]
    per = rows // E
    total = jnp.zeros((E, expo_s.shape[2]), F32)
    for block in range(blocks):
        parts = []
        for part in range(per):
            at = block * per + part
            down = slice(part * E, (part + 1) * E)
            query = packed_refs[block // 2][block % 2, down, :].astype(F32)
            parts.append((query * scale_ref[:, at : at + 1]).T.astype(BF16))
        copies[block].wait()
        total = total + dot(jnp.concatenate(parts, axis=1), expo_s[block])
    out_ref[...] = (total.T * gain).astype(BF16)


def keys(scale, expo, packed, gain):
    blocks, _, tokens = expo.shape
    return pl.pallas_call(
        lambda *refs: keys_kernel(gain, blocks, *refs),
        in_specs=[VMEM, HBM] + [VMEM] * len(packed),
        out_specs=VMEM,
        out_shape=jax.ShapeDtypeStruct((tokens, E), BF16),
        scratch_shapes=[
            pltpu.VMEM(expo.shape, BF16),
            pltpu.SemaphoreType.DMA((blocks,)),
        ],
        compiler_params=limit(16),
        name="keys",
    )(scale, *in_hbm(expo), *packed)


def total_kernel(gain, in_ref, out_ref):
    _, shards, piece, _ = in_ref.shape
    total = (jnp.sum(in_ref[...].astype(F32), axis=0) * gain).astype(BF16)
    for shard in range(shards):
        at = (shard % 2) * (shards // 2) + shard // 2
        out_ref[at * piece : (at + 1) * piece, :] = total[shard]


def totals(parts, gain):
    _, shards, piece, _ = parts.shape
    return pl.pallas_call(
        lambda *refs: total_kernel(gain, *refs),
        in_specs=[VMEM],
        out_specs=VMEM,
        out_shape=jax.ShapeDtypeStruct((shards * piece, E), BF16),
        compiler_params=limit(4),
        name="totals",
    )(parts)


def body(
    video, space_qkv, space_out, time_qkv, time_out, proj_weight, queries, query_len, positive
):
    _, frames_dev, patches, _ = video.shape
    shards = lax.axis_size("seq")
    blocks = lax.axis_size("dp")
    patch_loc = patches // shards
    frames = frames_dev * shards
    query_dev, slots, _ = queries.shape
    rows = query_dev * slots
    seat = lax.axis_index("seq")
    place = jnp.stack([lax.axis_index("dp"), lax.rem(seat, 2), seat // 2]).astype(jnp.int32)
    partner = [(i, i ^ 1) for i in range(shards)]
    chips = [[2 * chip + own for chip in range(shards // 2)] for own in range(2)]

    spatial = space(video[0], space_qkv, space_out, shards)
    spatial, flat = lax.optimization_barrier((spatial, queries.reshape(rows, E)))
    items = lax.all_to_all(spatial, "seq", 0, 0, tiled=True)
    mine = pack_queries(flat, query_len, positive)
    near = lax.ppermute(mine, "dp", [(i, i ^ 1) for i in range(blocks)])
    mine = jnp.stack([mine, near])
    packed = [mine] + [
        lax.ppermute(mine, "dp", [(i, (i + by) % blocks) for i in range(blocks)])
        for by in range(2, blocks, 2)
    ]
    khat = time(items.reshape(-1, D), time_qkv, time_out, proj_weight, patch_loc)

    expo, keep, send, sums = terms(packed, khat, place)
    got = lax.ppermute(send, "seq", partner)
    others = lax.ppermute(sums, "seq", partner)
    joined = join(keep, got, sums, others, shards // 2)
    joined = lax.all_to_all(joined, "seq", 0, 0, tiled=True, axis_index_groups=chips)
    parts, scale, loss = scales(joined, packed, place, slots, shards)
    parts = lax.all_to_all(
        parts.reshape((-1,) + parts.shape[2:]), ("dp", "seq"), 0, 0, tiled=True
    )
    video_grad = keys(scale, expo, packed, float(frames * P_SIZE))
    pair_loss = loss[:, :, ::slots].reshape(-1, 1)
    parts, video_grad, pair_loss = lax.optimization_barrier((parts, video_grad, pair_loss))
    query_grad = totals(parts.reshape((blocks, shards) + parts.shape[1:]), float(slots))
    return (
        video_grad.reshape(1, frames, patch_loc, E),
        query_grad.reshape(query_dev, slots, E),
        pair_loss,
    )


def solution(mesh):
    placed = (
        P("dp", "seq", None, None),
        P(),
        P(),
        P(),
        P(),
        P(),
        P("dp", None, None),
        P("dp"),
        P("dp"),
    )
    return jax.shard_map(
        body,
        mesh=mesh,
        in_specs=placed,
        out_specs=(P("dp", None, "seq", None), P("dp", None, None), P(None, "dp")),
        check_vma=False,
    )
```

time: 115 us -> 107 us (0.930)
  local copies, waits for them, and re-layouts: 7.39 us -> 0.71 us
  blocking collectives: 25.1 us -> 18.5 us
  waiting for transfers between devices: 19.3 us -> 25.9 us
  starting transfers between devices: 24.5 us -> 20.6 us
  Pallas kernels: 37 us -> 38.9 us
    ppermute x7 -> x3, waiting for transfers between devices: 14.8 us -> 0.01 us  [body(): lax.ppermute(mine, 'dp', [(i, (i + by) % blocks) for i in range(blocks)])]
    ppermute x1 -> x2, waiting for transfers between devices: 0.15 us -> 12.7 us  [the longest x1 11.6 us: body(): near = lax.ppermute(mine, 'dp', [(i, i ^ 1) for i in range(blocks)])]
    unnamed x14 -> x0, local copies, waits for them, and re-layouts: 6.68 us -> none
    all_to_all x2 -> x1, blocking collectives: 25.1 us -> 18.5 us  [body(): lax.all_to_all(joined, 'seq', 0, 0, tiled=True, axis_index_groups=chips)]
    all_to_all x1, waiting for transfers between devices: 3.62 us -> 9.13 us  [body(): lax.all_to_all(parts.reshape((-1,) + parts.shape[2:]), ('dp', 'seq'), 0,...]
    ppermute x7 -> x3, starting transfers between devices: 8.21 us -> 3.84 us  [body(): lax.ppermute(mine, 'dp', [(i, (i + by) % blocks) for i in range(blocks)])]
    all_to_all x1, waiting for transfers between devices: 0.7 us -> 4.02 us  [body(): items = lax.all_to_all(spatial, 'seq', 0, 0, tiled=True)]
    all_to_all x1, starting transfers between devices: 3.41 us -> 5.81 us  [body(): lax.all_to_all(parts.reshape((-1,) + parts.shape[2:]), ('dp', 'seq'), 0,...]
  transfers between devices with their start and end apart: 11 -> 8, of which waited for: 4 -> 4; matrix products, arithmetic and copies ran while one was open for 1% -> 2% of each run, Pallas kernels for 17% -> 17%
where the time goes in v2:
time: 107 us; the launch traced here: 106 us
  Pallas kernels  38.9 us (36%)
  waiting for transfers between devices  25.9 us (24%)
  starting transfers between devices  20.6 us (19%)
  blocking collectives  18.5 us (17%)
    all_to_all x1, blocking collectives, body(): lax.all_to_all(joined, 'seq', 0, 0, tiled=True, axis_index_groups=chips)  18.5 us
    pallas_call x1, Pallas kernels, space(): pl.pallas_call(space_kernel, in_specs=[HBM] * 3, out_specs=HBM, out_shape...  13.8 us
    pallas_call x1, Pallas kernels, time(): pl.pallas_call(time_kernel, in_specs=[VMEM] + [HBM] * 3, out_specs=VMEM,...  13.2 us
    ppermute x1, waiting for transfers between devices, body(): near = lax.ppermute(mine, 'dp', [(i, i ^ 1) for i in range(blocks)])  11.6 us
    all_to_all x1, starting transfers between devices, body(): items = lax.all_to_all(spatial, 'seq', 0, 0, tiled=True)  9.14 us
    all_to_all x1, waiting for transfers between devices, body(): lax.all_to_all(parts.reshape((-1,) + parts.shape[2:]), ('dp', 'seq'), 0,...  9.13 us
    all_to_all x1, starting transfers between devices, body(): lax.all_to_all(parts.reshape((-1,) + parts.shape[2:]), ('dp', 'seq'), 0,...  5.81 us
    all_to_all x1, waiting for transfers between devices, body(): items = lax.all_to_all(spatial, 'seq', 0, 0, tiled=True)  4.02 us
  transfers between devices with their start and end apart: 8, of which 4 were waited for; matrix products, arithmetic and copies ran while one was open for 2% of the time, Pallas kernels for 17%

profile of v2, /device:TPU:1, one launch (start us, length us, event | category | flops | bytes accessed | tf_op | source)
XLA Modules:
  0.0 106.2 jit_solution(6206811811229592426)
XLA Ops:
  0.6 13.8 %space.1 = bf16[16,4,16,768]{3,2,1,0:T(8,128)(2,1)} custom-call(bf16[4,256,768]{2,1,0:T(8,128)(2,1)} %bitcast.14, bf16[768,2304]{1,0:T(8,128)(2,1)} %qkv_ref.2, bf16[768,768]{1,0:T(8,128)(2,1)} %out_w_ref.2), custom_call_target="tpu_custom_call" | custom-call | tf_op jit(solution)/shard_map/space/pallas_call | solution.py:137
  14.4 9.1 %all-to-all-start = ((bf16[16,4,16,768]{3,2,1,0:T(8,128)(2,1)}), bf16[16,4,16,768]{3,2,1,0:T(8,128)(2,1)S(1)}, u32[]{:S(2)}, u32[]{:S(2)}) async-start(bf16[16,4,16,768]{3,2,1,0:T(8,128)(2,1)} %space.1), calls=%async_computation | async-start | bytes 3145728 | tf_op jit(solution)/shard_map/all_to_all | solution.py:465
  23.6 1.6 %pack_queries.1 = bf16[272,128]{1,0:T(8,128)(2,1)} custom-call(s32[8]{0:T(128)} %len_ref.1, s32[8]{0:T(128)} %pos_ref.1, bf16[256,128]{1,0:T(8,128)(2,1)} %bitcast.19), custom_call_target="tpu_custom_call" | custom-call | tf_op jit(solution)/shard_map/pack_queries/pallas_call | solution.py:242
  25.2 0.8 collective-permute-start
  26.0 11.6 %collective-permute-done = bf16[272,128]{1,0:T(8,128)(2,1)S(1)} collective-permute-done((bf16[272,128]{1,0:T(8,128)(2,1)}, bf16[272,128]{1,0:T(8,128)(2,1)S(1)}, u32[]{:S(2)}, u32[]{:S(2)}) %collective-permute-start) | collective-permute-done | bytes 69664 | tf_op jit(solution)/shard_map/ppermute | solution.py:467
  37.6 0.9 pad_maximum_fusion.refs_2_
  38.5 2.8 %collective-permute-start.3 = (bf16[2,272,128]{2,1,0:T(8,128)(2,1)S(1)}, bf16[2,272,128]{2,1,0:T(8,128)(2,1)S(1)}, u32[]{:S(2)}, u32[]{:S(2)}) collective-permute-start(bf16[2,272,128]{2,1,0:T(8,128)(2,1)S(1)} %pad_maximum_fusion.refs_2_), channel_id=1, source_target_pairs={{0,96},{16,112},{32,0},{48,16},{64,32},{80,48},{96,64},{112,80},{1... | collective-permute-start | bytes 417800 | tf_op jit(solution)/shard_map/ppermute | solution.py:470
  41.3 0.4 collective-permute-start.2
  41.6 0.7 collective-permute-start.1
  42.3 0.1 pad_add_fusion.refs_0_
  42.4 4.0 %all-to-all-done = bf16[16,4,16,768]{3,2,1,0:T(8,128)(2,1)S(1)} async-done(((bf16[16,4,16,768]{3,2,1,0:T(8,128)(2,1)}), bf16[16,4,16,768]{3,2,1,0:T(8,128)(2,1)S(1)}, u32[]{:S(2)}, u32[]{:S(2)}) %all-to-all-start) | async-done | bytes 1572896 | tf_op jit(solution)/shard_map/all_to_all | solution.py:465
  46.4 13.2 %time.1.refs_1_ = bf16[1024,128]{1,0:T(8,128)(2,1)S(1)} custom-call(bf16[1024,768]{1,0:T(8,128)(2,1)S(1)} %bitcast.12, bf16[768,2304]{1,0:T(8,128)(2,1)} %qkv_ref.3, bf16[768,768]{1,0:T(8,128)(2,1)} %out_w_ref.3, bf16[768,128]{1,0:T(8,128)(2,1)} %proj_ref.1), custom_call_target="tpu_custom_call" | custom-call | tf_op jit(solution)/shard_map/time/pallas_call | solution.py:203
  59.6 0.0 collective-permute-done.3.refs_5_
  59.6 0.0 collective-permute-done.2.refs_4_
  59.6 0.0 collective-permute-done.1.refs_3_
  59.6 4.0 %terms.1 = (bf16[8,256,1024]{2,1,0:T(8,128)(2,1)}, f32[8,128,128]{2,1,0:T(8,128)S(1)}, bf16[8,128,128]{2,1,0:T(8,128)(2,1)S(1)}, f32[16,128]{1,0:T(8,128)S(1)}) custom-call(s32[3]{0:T(128)S(1)} %pad_add_fusion.refs_0_, bf16[1024,128]{1,0:T(8,128)(2,1)S(1)} %time.1.refs_1_, bf16[2,272,128]{2,1,0:T(8,128)(2,1)S(1)} %pad_maximum_fusion.refs_2_, ...), custom_call_target="tpu_custom_call" | custom-call | tf_op jit(solution)/shard_map/terms/pallas_call | solution.py:285
  63.6 1.0 collective-permute-start.4
  64.6 0.1 collective-permute-start.5
  64.7 1.1 %collective-permute-done.5.others_ref = f32[16,128]{1,0:T(8,128)S(1)} collective-permute-done((f32[16,128]{1,0:T(8,128)S(1)}, f32[16,128]{1,0:T(8,128)S(1)}, u32[]{:S(2)}, u32[]{:S(2)}) %collective-permute-start.5) | collective-permute-done | bytes 8224 | tf_op jit(solution)/shard_map/ppermute | solution.py:477
  65.8 0.0 collective-permute-done.4.got_ref
  65.8 0.1 join.1
  65.8 18.5 %all_to_all.15.refs_1_ = bf16[8,160,128]{2,1,0:T(8,128)(2,1)S(1)} all-to-all(bf16[8,160,128]{2,1,0:T(8,128)(2,1)S(1)} %join.1), channel_id=1, replica_groups={{0,2,4,6,8,10,12,14},{1,3,5,7,9,11,13,15},{16,18,20,22,24,26,28,30},{17..., dimensions={0} | all-to-all | bytes 655360 | tf_op jit(solution)/shard_map/all_to_all | solution.py:479
  84.3 1.8 %scales.1 = (bf16[8,16,16,128]{3,2,1,0:T(8,128)(2,1)}, f32[128,16]{1,0:T(8,128)S(1)}, f32[8,2,128]{2,1,0:T(2,128)S(1)}) custom-call(s32[3]{0:T(128)S(1)} %pad_add_fusion.refs_0_, bf16[8,160,128]{2,1,0:T(8,128)(2,1)S(1)} %all_to_all.15.refs_1_, bf16[2,272,128]{2,1,0:T(8,128)(2,1)S(1)} %pad_maximum_fusion.refs_2_, ...), custom_call_target="tpu_custom_call" | custom-call | tf_op jit(solution)/shard_map/scales/pallas_call | solution.py:380
  86.2 5.8 %all-to-all-start.2 = ((bf16[128,16,128]{2,1,0:T(8,128)(2,1)}), bf16[128,16,128]{2,1,0:T(8,128)(2,1)S(1)}, u32[]{:S(2)}, u32[]{:S(2)}) async-start(bf16[128,16,128]{2,1,0:T(8,128)(2,1)} %bitcast.8), calls=%async_computation.2 | async-start | bytes 1048576 | tf_op jit(solution)/shard_map/all_to_all | solution.py:481
  92.0 0.1 slice.3
  92.1 0.6 reshape.30
  92.7 3.7 %keys.1 = bf16[1024,128]{1,0:T(8,128)(2,1)} custom-call(f32[128,16]{1,0:T(8,128)S(1)} %get-tuple-element.21.refs_0_, bf16[8,256,1024]{2,1,0:T(8,128)(2,1)} %get-tuple-element.22.refs_1_, bf16[2,272,128]{2,1,0:T(8,128)(2,1)S(1)} %pad_maximum_fusion.refs_2_, bf16[2,272,128]{2,1,0:T(8,128)(2,1)S(1)} %collective-permute-done.1.refs_3_, ...), custom_call_target="tpu_custom_call" | custom-call | tf_op jit(solution)/shard_map/keys/pallas_call | solution.py:414
  96.4 9.1 %all-to-all-done.2 = bf16[128,16,128]{2,1,0:T(8,128)(2,1)S(1)} async-done(((bf16[128,16,128]{2,1,0:T(8,128)(2,1)}), bf16[128,16,128]{2,1,0:T(8,128)(2,1)S(1)}, u32[]{:S(2)}, u32[]{:S(2)}) %all-to-all-start.2) | async-done | bytes 524320 | tf_op jit(solution)/shard_map/all_to_all | solution.py:481
  105.5 0.7 totals.1
Async XLA Ops:
  14.4 32.0 %all-to-all-start = ((bf16[16,4,16,768]{3,2,1,0:T(8,128)(2,1)}), bf16[16,4,16,768]{3,2,1,0:T(8,128)(2,1)S(1)}, u32[]{:S(2)}, u32[]{:S(2)}) async-start(bf16[16,4,16,768]{3,2,1,0:T(8,128)(2,1)} %space.1), calls=%async_computation | async-start | bytes 3145728 | tf_op jit(solution)/shard_map/all_to_all | solution.py:465
  25.2 12.4 %collective-permute-start = (bf16[272,128]{1,0:T(8,128)(2,1)}, bf16[272,128]{1,0:T(8,128)(2,1)S(1)}, u32[]{:S(2)}, u32[]{:S(2)}) collective-permute-start(bf16[272,128]{1,0:T(8,128)(2,1)} %pack_queries.1), channel_id=1, source_target_pairs={{0,16},{16,0},{32,48},{48,32},{64,80},{80,64},{96,112},{112,96},{1... | collective-permute-start | bytes 208904 | tf_op jit(solution)/shard_map/ppermute | solution.py:467
  38.5 21.1 %collective-permute-start.3 = (bf16[2,272,128]{2,1,0:T(8,128)(2,1)S(1)}, bf16[2,272,128]{2,1,0:T(8,128)(2,1)S(1)}, u32[]{:S(2)}, u32[]{:S(2)}) collective-permute-start(bf16[2,272,128]{2,1,0:T(8,128)(2,1)S(1)} %pad_maximum_fusion.refs_2_), channel_id=1, source_target_pairs={{0,96},{16,112},{32,0},{48,16},{64,32},{80,48},{96,64},{112,80},{1... | collective-permute-start | bytes 417800 | tf_op jit(solution)/shard_map/ppermute | solution.py:470
  41.3 18.4 %collective-permute-start.2 = (bf16[2,272,128]{2,1,0:T(8,128)(2,1)S(1)}, bf16[2,272,128]{2,1,0:T(8,128)(2,1)S(1)}, u32[]{:S(2)}, u32[]{:S(2)}) collective-permute-start(bf16[2,272,128]{2,1,0:T(8,128)(2,1)S(1)} %pad_maximum_fusion.refs_2_), channel_id=1, source_target_pairs={{0,64},{16,80},{32,96},{48,112},{64,0},{80,16},{96,32},{112,48},{1... | collective-permute-start | bytes 417800 | tf_op jit(solution)/shard_map/ppermute | solution.py:470
  41.6 18.0 %collective-permute-start.1 = (bf16[2,272,128]{2,1,0:T(8,128)(2,1)S(1)}, bf16[2,272,128]{2,1,0:T(8,128)(2,1)S(1)}, u32[]{:S(2)}, u32[]{:S(2)}) collective-permute-start(bf16[2,272,128]{2,1,0:T(8,128)(2,1)S(1)} %pad_maximum_fusion.refs_2_), channel_id=1, source_target_pairs={{0,32},{16,48},{32,64},{48,80},{64,96},{80,112},{96,0},{112,16},{1... | collective-permute-start | bytes 417800 | tf_op jit(solution)/shard_map/ppermute | solution.py:470
  63.6 2.1 %collective-permute-start.4 = (bf16[8,128,128]{2,1,0:T(8,128)(2,1)S(1)}, bf16[8,128,128]{2,1,0:T(8,128)(2,1)S(1)}, u32[]{:S(2)}, u32[]{:S(2)}) collective-permute-start(bf16[8,128,128]{2,1,0:T(8,128)(2,1)S(1)} %get-tuple-element.18), channel_id=1, source_target_pairs={{0,1},{1,0},{2,3},{3,2},{4,5},{5,4},{6,7},{7,6},{8,9},{9,8},{10,11... | collective-permute-start | bytes 786440 | tf_op jit(solution)/shard_map/ppermute | solution.py:476
  64.6 1.2 %collective-permute-start.5 = (f32[16,128]{1,0:T(8,128)S(1)}, f32[16,128]{1,0:T(8,128)S(1)}, u32[]{:S(2)}, u32[]{:S(2)}) collective-permute-start(f32[16,128]{1,0:T(8,128)S(1)} %get-tuple-element.19.sums_ref), channel_id=1, source_target_pairs={{0,1},{1,0},{2,3},{3,2},{4,5},{5,4},{6,7},{7,6},{8,9},{9,8},{10,11... | collective-permute-start | bytes 24584 | tf_op jit(solution)/shard_map/ppermute | solution.py:477
  86.2 19.4 %all-to-all-start.2 = ((bf16[128,16,128]{2,1,0:T(8,128)(2,1)}), bf16[128,16,128]{2,1,0:T(8,128)(2,1)S(1)}, u32[]{:S(2)}, u32[]{:S(2)}) async-start(bf16[128,16,128]{2,1,0:T(8,128)(2,1)} %bitcast.8), calls=%async_computation.2 | async-start | bytes 1048576 | tf_op jit(solution)/shard_map/all_to_all | solution.py:481

commit v3 on v2

--- a/solution.py
+++ b/solution.py
@@ -249,25 +249,30 @@
 
 
 def group_of(mine, blocks, block):
-    return lax.rem(mine + blocks - block // 2 * 2, blocks) ^ (block % 2)
+    side, step = divmod(block, blocks // 2)
+    return lax.rem(mine + blocks - 2 * step, blocks) ^ side
+
+
+def block_of(packed_refs, block):
+    side, step = divmod(block, packed_refs[0].shape[0])
+    return packed_refs[side].at[step]
+
+
+def expo_terms(query, khat):
+    gain = LOG2E / TEMPER
+    return jnp.exp2(dot_t(query, khat) * gain - gain).astype(BF16)
 
 
 def terms_kernel(blocks, at_ref, khat_ref, *refs):
-    packed_refs = refs[: blocks // 2]
-    expo_ref, keep_ref, send_ref, sums_ref, expo_s, sem = refs[blocks // 2 :]
-    rows = expo_s.shape[1]
+    packed_refs, (keep_ref, send_ref, sums_ref) = refs[:-3], refs[-3:]
+    rows = packed_refs[0].shape[1] - EXTRA
     first = at_ref[1] == 0
     khat = khat_ref[...]
     wide = jnp.concatenate([khat, jnp.ones_like(khat)], axis=1)
-    gain = LOG2E / TEMPER
     eye = iota((E, E), 0) == iota((E, E), 1)
     sums = []
     for block in range(blocks):
-        dots = dot_t(packed_refs[block // 2][block % 2, :rows, :], khat)
-        expo = jnp.exp2(dots * gain - gain).astype(BF16)
-        expo_s[block] = expo
-        pltpu.make_async_copy(expo_s.at[block], expo_ref.at[block], sem.at[block]).start()
-        both = dot(expo, wide)
+        both = dot(expo_terms(block_of(packed_refs, block)[:rows, :], khat), wide)
         low, high = both[:E, :E], both[E:, :E]
         keep_ref[block] = jnp.where(first, low, high)
         send_ref[block] = jnp.where(first, high, low).astype(BF16)
@@ -275,26 +280,18 @@
             square = both[part * E : (part + 1) * E, E:]
             sums.append(jnp.sum(jnp.where(eye, square, 0.0), axis=0, keepdims=True))
     sums_ref[...] = jnp.concatenate(sums, axis=0)
-    for block in range(blocks):
-        pltpu.make_async_copy(expo_s.at[block], expo_ref.at[block], sem.at[block]).wait()
 
 
 def terms(packed, khat, place):
-    blocks, rows = 2 * len(packed), packed[0].shape[1] - EXTRA
-    tokens = khat.shape[0]
+    blocks, rows = 2 * packed[0].shape[0], packed[0].shape[1] - EXTRA
     return pl.pallas_call(
         lambda *refs: terms_kernel(blocks, *refs),
         in_specs=[SMEM] + [VMEM] * (1 + len(packed)),
-        out_specs=[HBM] + [VMEM] * 3,
+        out_specs=[VMEM] * 3,
         out_shape=[
-            pltpu.HBM((blocks, rows, tokens), BF16),
             jax.ShapeDtypeStruct((blocks, rows // 2, E), F32),
             jax.ShapeDtypeStruct((blocks, rows // 2, E), BF16),
             jax.ShapeDtypeStruct((blocks * rows // E, E), F32),
-        ],
-        scratch_shapes=[
-            pltpu.VMEM((blocks, rows, tokens), BF16),
-            pltpu.SemaphoreType.DMA((blocks,)),
         ],
         compiler_params=limit(16),
         name="terms",
@@ -341,7 +338,7 @@
     got = jnp.sum(got_ref[...].astype(F32), axis=0)
     blend, notes = got[: blocks * piece], got[blocks * piece :]
     total = notes[: blocks * per] + notes[blocks * per :]
-    notes = [packed_refs[b // 2][b % 2, rows:, :].astype(F32) for b in range(blocks)]
+    notes = [block_of(packed_refs, b)[rows:, :].astype(F32) for b in range(blocks)]
     lens = jnp.concatenate([note[:per] for note in notes], axis=0)
     pos = jnp.concatenate([note[per : 2 * per] for note in notes], axis=0)
     mask = ((iota(total.shape, 1) % slots).astype(F32) < lens).astype(F32)
@@ -375,7 +372,7 @@
 
 
 def scales(got, packed, place, slots, shards):
-    blocks, rows = 2 * len(packed), packed[0].shape[1] - EXTRA
+    blocks, rows = 2 * packed[0].shape[0], packed[0].shape[1] - EXTRA
     piece = rows // shards
     return pl.pallas_call(
         lambda *refs: scale_kernel(slots, *refs),
@@ -391,38 +388,32 @@
     )(place, got, *packed)
 
 
-def keys_kernel(gain, blocks, scale_ref, expo_ref, *refs):
-    packed_refs, (out_ref, expo_s, sem) = refs[:-3], refs[-3:]
-    copies = fetch([(expo_ref.at[b], expo_s.at[b]) for b in range(blocks)], sem)
-    rows = expo_s.shape[1]
+def keys_kernel(gain, blocks, scale_ref, khat_ref, *refs):
+    packed_refs, out_ref = refs[:-1], refs[-1]
+    khat = khat_ref[...]
+    rows = packed_refs[0].shape[1] - EXTRA
     per = rows // E
-    total = jnp.zeros((E, expo_s.shape[2]), F32)
+    total = jnp.zeros((E, khat.shape[0]), F32)
     for block in range(blocks):
+        query = block_of(packed_refs, block)[:rows, :]
         parts = []
         for part in range(per):
             at = block * per + part
-            down = slice(part * E, (part + 1) * E)
-            query = packed_refs[block // 2][block % 2, down, :].astype(F32)
-            parts.append((query * scale_ref[:, at : at + 1]).T.astype(BF16))
-        copies[block].wait()
-        total = total + dot(jnp.concatenate(parts, axis=1), expo_s[block])
+            scaled = query[part * E : (part + 1) * E].astype(F32) * scale_ref[:, at : at + 1]
+            parts.append(scaled.T.astype(BF16))
+        total = total + dot(jnp.concatenate(parts, axis=1), expo_terms(query, khat))
     out_ref[...] = (total.T * gain).astype(BF16)
 
 
-def keys(scale, expo, packed, gain):
-    blocks, _, tokens = expo.shape
-    return pl.pallas_call(
-        lambda *refs: keys_kernel(gain, blocks, *refs),
-        in_specs=[VMEM, HBM] + [VMEM] * len(packed),
+def keys(scale, khat, packed, gain):
+    return pl.pallas_call(
+        lambda *refs: keys_kernel(gain, 2 * packed[0].shape[0], *refs),
+        in_specs=[VMEM] * (2 + len(packed)),
         out_specs=VMEM,
-        out_shape=jax.ShapeDtypeStruct((tokens, E), BF16),
-        scratch_shapes=[
-            pltpu.VMEM(expo.shape, BF16),
-            pltpu.SemaphoreType.DMA((blocks,)),
-        ],
+        out_shape=jax.ShapeDtypeStruct(khat.shape, BF16),
         compiler_params=limit(16),
         name="keys",
-    )(scale, *in_hbm(expo), *packed)
+    )(scale, khat, *packed)
 
 
 def total_kernel(gain, in_ref, out_ref):
@@ -464,15 +455,18 @@
     spatial, flat = lax.optimization_barrier((spatial, queries.reshape(rows, E)))
     items = lax.all_to_all(spatial, "seq", 0, 0, tiled=True)
     mine = pack_queries(flat, query_len, positive)
-    near = lax.ppermute(mine, "dp", [(i, i ^ 1) for i in range(blocks)])
-    mine = jnp.stack([mine, near])
-    packed = [mine] + [
-        lax.ppermute(mine, "dp", [(i, (i + by) % blocks) for i in range(blocks)])
-        for by in range(2, blocks, 2)
-    ]
+    lane = jnp.stack(
+        [mine]
+        + [
+            lax.ppermute(mine, "dp", [(i, (i + by) % blocks) for i in range(blocks)])
+            for by in range(2, blocks, 2)
+        ]
+    )
+    items, lane = lax.optimization_barrier((items, lane))
+    packed = [lane, lax.ppermute(lane, "dp", [(i, i ^ 1) for i in range(blocks)])]
     khat = time(items.reshape(-1, D), time_qkv, time_out, proj_weight, patch_loc)
 
-    expo, keep, send, sums = terms(packed, khat, place)
+    keep, send, sums = terms(packed, khat, place)
     got = lax.ppermute(send, "seq", partner)
     others = lax.ppermute(sums, "seq", partner)
     joined = join(keep, got, sums, others, shards // 2)
@@ -481,7 +475,7 @@
     parts = lax.all_to_all(
         parts.reshape((-1,) + parts.shape[2:]), ("dp", "seq"), 0, 0, tiled=True
     )
-    video_grad = keys(scale, expo, packed, float(frames * P_SIZE))
+    video_grad = keys(scale, khat, packed, float(frames * P_SIZE))
     pair_loss = loss[:, :, ::slots].reshape(-1, 1)
     parts, video_grad, pair_loss = lax.optimization_barrier((parts, video_grad, pair_loss))
     query_grad = totals(parts.reshape((blocks, shards) + parts.shape[1:]), float(slots))

time: 107 us -> 102 us (0.953)
  blocking collectives: 18.5 us -> 12.7 us
  starting transfers between devices: 20.6 us -> 21.8 us
    ppermute x1, waiting for transfers between devices: 11.6 us -> 0.01 us  [body(): lax.ppermute(lane, 'dp', [(i, i ^ 1) for i in range(blocks)])]
    all_to_all x1, waiting for transfers between devices: 4.02 us -> 10.4 us  [body(): items = lax.all_to_all(spatial, 'seq', 0, 0, tiled=True)]
    ppermute x3, waiting for transfers between devices: 0.01 us -> 6.13 us  [body(): lax.ppermute(mine, 'dp', [(i, (i + by) % blocks) for i in range(blocks)])]
    all_to_all x1, blocking collectives: 18.5 us -> 12.7 us  [body(): lax.all_to_all(joined, 'seq', 0, 0, tiled=True, axis_index_groups=chips)]
  transfers between devices with their start and end apart: 8 -> 8, of which waited for: 4 -> 6; matrix products, arithmetic and copies ran while one was open for 2% -> 2% of each run, Pallas kernels for 17% -> 18%
where the time goes in v3:
time: 102 us
  Pallas kernels  38.1 us (37%)
  waiting for transfers between devices  26.7 us (26%)
  starting transfers between devices  21.8 us (21%)
  blocking collectives  12.7 us (12%)
    pallas_call x1, Pallas kernels, space(): pl.pallas_call(space_kernel, in_specs=[HBM] * 3, out_specs=HBM, out_shape...  13.8 us
    pallas_call x1, Pallas kernels, time(): pl.pallas_call(time_kernel, in_specs=[VMEM] + [HBM] * 3, out_specs=VMEM,...  13.2 us
    all_to_all x1, blocking collectives, body(): lax.all_to_all(joined, 'seq', 0, 0, tiled=True, axis_index_groups=chips)  12.7 us
    all_to_all x1, waiting for transfers between devices, body(): items = lax.all_to_all(spatial, 'seq', 0, 0, tiled=True)  10.4 us
    all_to_all x1, waiting for transfers between devices, body(): lax.all_to_all(parts.reshape((-1,) + parts.shape[2:]), ('dp', 'seq'), 0,...  9.17 us
    all_to_all x1, starting transfers between devices, body(): items = lax.all_to_all(spatial, 'seq', 0, 0, tiled=True)  9.14 us
    all_to_all x1, starting transfers between devices, body(): lax.all_to_all(parts.reshape((-1,) + parts.shape[2:]), ('dp', 'seq'), 0,...  6.74 us
    ppermute x3, waiting for transfers between devices, body(): lax.ppermute(mine, 'dp', [(i, (i + by) % blocks) for i in range(blocks)])  6.13 us
  transfers between devices with their start and end apart: 8, of which 6 were waited for; matrix products, arithmetic and copies ran while one was open for 2% of the time, Pallas kernels for 18%

profile of v3, /device:TPU:1, one launch (start us, length us, event | category | flops | bytes accessed | tf_op | source)
XLA Modules:
  0.0 101.7 jit_solution(15751588083684138732)
XLA Ops:
  0.6 13.8 %space.1 = bf16[16,4,16,768]{3,2,1,0:T(8,128)(2,1)} custom-call(bf16[4,256,768]{2,1,0:T(8,128)(2,1)} %bitcast.16, bf16[768,2304]{1,0:T(8,128)(2,1)} %qkv_ref.2, bf16[768,768]{1,0:T(8,128)(2,1)} %out_w_ref.2), custom_call_target="tpu_custom_call" | custom-call | tf_op jit(solution)/shard_map/space/pallas_call | solution.py:137
  14.4 9.1 %all-to-all-start = ((bf16[16,4,16,768]{3,2,1,0:T(8,128)(2,1)}), bf16[16,4,16,768]{3,2,1,0:T(8,128)(2,1)S(1)}, u32[]{:S(2)}, u32[]{:S(2)}) async-start(bf16[16,4,16,768]{3,2,1,0:T(8,128)(2,1)} %space.1), calls=%async_computation | async-start | bytes 3145728 | tf_op jit(solution)/shard_map/all_to_all | solution.py:456
  23.6 1.6 %pack_queries.1 = bf16[272,128]{1,0:T(8,128)(2,1)} custom-call(s32[8]{0:T(128)} %len_ref.1, s32[8]{0:T(128)} %pos_ref.1, bf16[256,128]{1,0:T(8,128)(2,1)} %bitcast.23), custom_call_target="tpu_custom_call" | custom-call | tf_op jit(solution)/shard_map/pack_queries/pallas_call | solution.py:242
  25.2 2.8 %collective-permute-start.2 = (bf16[272,128]{1,0:T(8,128)(2,1)}, bf16[272,128]{1,0:T(8,128)(2,1)S(1)}, u32[]{:S(2)}, u32[]{:S(2)}) collective-permute-start(bf16[272,128]{1,0:T(8,128)(2,1)} %pack_queries.1), channel_id=1, source_target_pairs={{0,96},{16,112},{32,0},{48,16},{64,32},{80,48},{96,64},{112,80},{1... | collective-permute-start | bytes 208904 | tf_op jit(solution)/shard_map/ppermute | solution.py:461
  28.0 0.3 collective-permute-start.1
  28.3 0.7 collective-permute-start
  29.0 0.8 collective-permute-done.2
  29.8 3.4 %collective-permute-done.1 = bf16[272,128]{1,0:T(8,128)(2,1)S(1)} collective-permute-done((bf16[272,128]{1,0:T(8,128)(2,1)}, bf16[272,128]{1,0:T(8,128)(2,1)S(1)}, u32[]{:S(2)}, u32[]{:S(2)}) %collective-permute-start.1) | collective-permute-done | bytes 69664 | tf_op jit(solution)/shard_map/ppermute | solution.py:461
  33.1 2.0 %collective-permute-done = bf16[272,128]{1,0:T(8,128)(2,1)S(1)} collective-permute-done((bf16[272,128]{1,0:T(8,128)(2,1)}, bf16[272,128]{1,0:T(8,128)(2,1)S(1)}, u32[]{:S(2)}, u32[]{:S(2)}) %collective-permute-start) | collective-permute-done | bytes 69664 | tf_op jit(solution)/shard_map/ppermute | solution.py:461
  35.1 0.9 pad_maximum_fusion.refs_2_
  36.1 10.4 %all-to-all-done = bf16[16,4,16,768]{3,2,1,0:T(8,128)(2,1)S(1)} async-done(((bf16[16,4,16,768]{3,2,1,0:T(8,128)(2,1)}), bf16[16,4,16,768]{3,2,1,0:T(8,128)(2,1)S(1)}, u32[]{:S(2)}, u32[]{:S(2)}) %all-to-all-start) | async-done | bytes 1572896 | tf_op jit(solution)/shard_map/all_to_all | solution.py:456
  46.4 0.7 collective-permute-start.3
  47.2 0.1 pad_add_fusion.refs_0_
  47.2 13.2 %time.1.refs_1_ = bf16[1024,128]{1,0:T(8,128)(2,1)S(1)} custom-call(bf16[1024,768]{1,0:T(8,128)(2,1)S(1)} %bitcast.14, bf16[768,2304]{1,0:T(8,128)(2,1)} %qkv_ref.3, bf16[768,768]{1,0:T(8,128)(2,1)} %out_w_ref.3, bf16[768,128]{1,0:T(8,128)(2,1)} %proj_ref.1), custom_call_target="tpu_custom_call" | custom-call | tf_op jit(solution)/shard_map/time/pallas_call | solution.py:203
  60.4 0.0 collective-permute-done.3.refs_3_
  60.4 3.3 %terms.1 = (f32[8,128,128]{2,1,0:T(8,128)S(1)}, bf16[8,128,128]{2,1,0:T(8,128)(2,1)S(1)}, f32[16,128]{1,0:T(8,128)S(1)}) custom-call(s32[3]{0:T(128)S(1)} %pad_add_fusion.refs_0_, bf16[1024,128]{1,0:T(8,128)(2,1)S(1)} %time.1.refs_1_, bf16[4,272,128]{2,1,0:T(8,128)(2,1)S(1)} %pad_maximum_fusion.refs_2_, bf16[4,272,128]{2,1,0:T(8,128)(2,1)S(1)} %collective-permute-done.3.refs_3_), custom_call_target="tpu_custom_call" | custom-call | tf_op jit(solution)/shard_map/terms/pallas_call | solution.py:287
  63.7 1.2 %collective-permute-start.4 = (bf16[8,128,128]{2,1,0:T(8,128)(2,1)S(1)}, bf16[8,128,128]{2,1,0:T(8,128)(2,1)S(1)}, u32[]{:S(2)}, u32[]{:S(2)}) collective-permute-start(bf16[8,128,128]{2,1,0:T(8,128)(2,1)S(1)} %get-tuple-element.21), channel_id=1, source_target_pairs={{0,1},{1,0},{2,3},{3,2},{4,5},{5,4},{6,7},{7,6},{8,9},{9,8},{10,11... | collective-permute-start | bytes 786440 | tf_op jit(solution)/shard_map/ppermute | solution.py:470
  64.9 0.1 collective-permute-start.5
  65.0 1.1 %collective-permute-done.5.others_ref = f32[16,128]{1,0:T(8,128)S(1)} collective-permute-done((f32[16,128]{1,0:T(8,128)S(1)}, f32[16,128]{1,0:T(8,128)S(1)}, u32[]{:S(2)}, u32[]{:S(2)}) %collective-permute-start.5) | collective-permute-done | bytes 8224 | tf_op jit(solution)/shard_map/ppermute | solution.py:471
  66.1 0.0 collective-permute-done.4.got_ref
  66.1 0.1 join.1
  66.2 12.7 %all_to_all.15.refs_1_ = bf16[8,160,128]{2,1,0:T(8,128)(2,1)S(1)} all-to-all(bf16[8,160,128]{2,1,0:T(8,128)(2,1)S(1)} %join.1), channel_id=1, replica_groups={{0,2,4,6,8,10,12,14},{1,3,5,7,9,11,13,15},{16,18,20,22,24,26,28,30},{17..., dimensions={0} | all-to-all | bytes 655360 | tf_op jit(solution)/shard_map/all_to_all | solution.py:473
  78.9 1.8 %scales.1 = (bf16[8,16,16,128]{3,2,1,0:T(8,128)(2,1)}, f32[128,16]{1,0:T(8,128)S(1)}, f32[8,2,128]{2,1,0:T(2,128)S(1)}) custom-call(s32[3]{0:T(128)S(1)} %pad_add_fusion.refs_0_, bf16[8,160,128]{2,1,0:T(8,128)(2,1)S(1)} %all_to_all.15.refs_1_, bf16[4,272,128]{2,1,0:T(8,128)(2,1)S(1)} %pad_maximum_fusion.refs_2_, ...), custom_call_target="tpu_custom_call" | custom-call | tf_op jit(solution)/shard_map/scales/pallas_call | solution.py:377
  80.7 6.7 %all-to-all-start.2 = ((bf16[128,16,128]{2,1,0:T(8,128)(2,1)}), bf16[128,16,128]{2,1,0:T(8,128)(2,1)S(1)}, u32[]{:S(2)}, u32[]{:S(2)}) async-start(bf16[128,16,128]{2,1,0:T(8,128)(2,1)} %bitcast.10), calls=%async_computation.2 | async-start | bytes 1048576 | tf_op jit(solution)/shard_map/all_to_all | solution.py:475
  87.5 0.1 slice.3
  87.6 0.6 reshape.30
  88.2 3.6 %keys.1 = bf16[1024,128]{1,0:T(8,128)(2,1)} custom-call(f32[128,16]{1,0:T(8,128)S(1)} %get-tuple-element.24.refs_0_, bf16[1024,128]{1,0:T(8,128)(2,1)S(1)} %time.1.refs_1_, bf16[4,272,128]{2,1,0:T(8,128)(2,1)S(1)} %pad_maximum_fusion.refs_2_, bf16[4,272,128]{2,1,0:T(8,128)(2,1)S(1)} %collective-permute-done.3.refs_3_), custom_call_target="tpu_custom_call" | custom-call | tf_op jit(solution)/shard_map/keys/pallas_call | solution.py:409
  91.8 9.2 %all-to-all-done.2 = bf16[128,16,128]{2,1,0:T(8,128)(2,1)S(1)} async-done(((bf16[128,16,128]{2,1,0:T(8,128)(2,1)}), bf16[128,16,128]{2,1,0:T(8,128)(2,1)S(1)}, u32[]{:S(2)}, u32[]{:S(2)}) %all-to-all-start.2) | async-done | bytes 524320 | tf_op jit(solution)/shard_map/all_to_all | solution.py:475
  101.0 0.7 totals.1
Async XLA Ops:
  14.4 32.0 %all-to-all-start = ((bf16[16,4,16,768]{3,2,1,0:T(8,128)(2,1)}), bf16[16,4,16,768]{3,2,1,0:T(8,128)(2,1)S(1)}, u32[]{:S(2)}, u32[]{:S(2)}) async-start(bf16[16,4,16,768]{3,2,1,0:T(8,128)(2,1)} %space.1), calls=%async_computation | async-start | bytes 3145728 | tf_op jit(solution)/shard_map/all_to_all | solution.py:456
  25.2 4.6 %collective-permute-start.2 = (bf16[272,128]{1,0:T(8,128)(2,1)}, bf16[272,128]{1,0:T(8,128)(2,1)S(1)}, u32[]{:S(2)}, u32[]{:S(2)}) collective-permute-start(bf16[272,128]{1,0:T(8,128)(2,1)} %pack_queries.1), channel_id=1, source_target_pairs={{0,96},{16,112},{32,0},{48,16},{64,32},{80,48},{96,64},{112,80},{1... | collective-permute-start | bytes 208904 | tf_op jit(solution)/shard_map/ppermute | solution.py:461
  28.0 5.2 %collective-permute-start.1 = (bf16[272,128]{1,0:T(8,128)(2,1)}, bf16[272,128]{1,0:T(8,128)(2,1)S(1)}, u32[]{:S(2)}, u32[]{:S(2)}) collective-permute-start(bf16[272,128]{1,0:T(8,128)(2,1)} %pack_queries.1), channel_id=1, source_target_pairs={{0,64},{16,80},{32,96},{48,112},{64,0},{80,16},{96,32},{112,48},{1... | collective-permute-start | bytes 208904 | tf_op jit(solution)/shard_map/ppermute | solution.py:461
  28.3 6.8 %collective-permute-start = (bf16[272,128]{1,0:T(8,128)(2,1)}, bf16[272,128]{1,0:T(8,128)(2,1)S(1)}, u32[]{:S(2)}, u32[]{:S(2)}) collective-permute-start(bf16[272,128]{1,0:T(8,128)(2,1)} %pack_queries.1), channel_id=1, source_target_pairs={{0,32},{16,48},{32,64},{48,80},{64,96},{80,112},{96,0},{112,16},{1... | collective-permute-start | bytes 208904 | tf_op jit(solution)/shard_map/ppermute | solution.py:461
  46.4 14.0 %collective-permute-start.3 = (bf16[4,272,128]{2,1,0:T(8,128)(2,1)S(1)}, bf16[4,272,128]{2,1,0:T(8,128)(2,1)S(1)}, u32[]{:S(2)}, u32[]{:S(2)}) collective-permute-start(bf16[4,272,128]{2,1,0:T(8,128)(2,1)S(1)} %pad_maximum_fusion.refs_2_), channel_id=1, source_target_pairs={{0,16},{16,0},{32,48},{48,32},{64,80},{80,64},{96,112},{112,96},{1... | collective-permute-start | bytes 835592 | tf_op jit(solution)/shard_map/ppermute | solution.py:466
  63.7 2.4 %collective-permute-start.4 = (bf16[8,128,128]{2,1,0:T(8,128)(2,1)S(1)}, bf16[8,128,128]{2,1,0:T(8,128)(2,1)S(1)}, u32[]{:S(2)}, u32[]{:S(2)}) collective-permute-start(bf16[8,128,128]{2,1,0:T(8,128)(2,1)S(1)} %get-tuple-element.21), channel_id=1, source_target_pairs={{0,1},{1,0},{2,3},{3,2},{4,5},{5,4},{6,7},{7,6},{8,9},{9,8},{10,11... | collective-permute-start | bytes 786440 | tf_op jit(solution)/shard_map/ppermute | solution.py:470
  64.9 1.2 %collective-permute-start.5 = (f32[16,128]{1,0:T(8,128)S(1)}, f32[16,128]{1,0:T(8,128)S(1)}, u32[]{:S(2)}, u32[]{:S(2)}) collective-permute-start(f32[16,128]{1,0:T(8,128)S(1)} %get-tuple-element.22.sums_ref), channel_id=1, source_target_pairs={{0,1},{1,0},{2,3},{3,2},{4,5},{5,4},{6,7},{7,6},{8,9},{9,8},{10,11... | collective-permute-start | bytes 24584 | tf_op jit(solution)/shard_map/ppermute | solution.py:471
  80.7 20.3 %all-to-all-start.2 = ((bf16[128,16,128]{2,1,0:T(8,128)(2,1)}), bf16[128,16,128]{2,1,0:T(8,128)(2,1)S(1)}, u32[]{:S(2)}, u32[]{:S(2)}) async-start(bf16[128,16,128]{2,1,0:T(8,128)(2,1)} %bitcast.10), calls=%async_computation.2 | async-start | bytes 1048576 | tf_op jit(solution)/shard_map/all_to_all | solution.py:475

commit v4 on v3

--- a/solution.py
+++ b/solution.py
@@ -332,7 +332,8 @@
 
 def scale_kernel(slots, at_ref, got_ref, *refs):
     packed_refs, (part_ref, scale_ref, loss_ref) = refs[:-3], refs[-3:]
-    blocks, shards, piece, _ = part_ref.shape
+    blocks, shards, share, _ = part_ref.shape
+    piece = 2 * share
     rows = packed_refs[0].shape[1] - EXTRA
     per = rows // E
     got = jnp.sum(got_ref[...].astype(F32), axis=0)
@@ -367,19 +368,19 @@
         column = jnp.where(first, scale[:, at : at + 1], scale[:, at + 1 : at + 2])
         part = (blend[block * piece : (block + 1) * piece] * column).astype(BF16)
         for shard in range(shards):
-            part_ref[group, shard] = part
+            part_ref[group, shard] = part[shard % 2 * share : (shard % 2 + 1) * share]
         loss_ref[group] = loss[at : at + per]
 
 
 def scales(got, packed, place, slots, shards):
     blocks, rows = 2 * packed[0].shape[0], packed[0].shape[1] - EXTRA
-    piece = rows // shards
+    share = rows // shards // 2
     return pl.pallas_call(
         lambda *refs: scale_kernel(slots, *refs),
         in_specs=[SMEM] + [VMEM] * (1 + len(packed)),
         out_specs=[VMEM] * 3,
         out_shape=[
-            jax.ShapeDtypeStruct((blocks, shards, piece, E), BF16),
+            jax.ShapeDtypeStruct((blocks, shards, share, E), BF16),
             jax.ShapeDtypeStruct((E, blocks * rows // E), F32),
             jax.ShapeDtypeStruct((blocks, rows // E, E), F32),
         ],
@@ -417,23 +418,40 @@
 
 
 def total_kernel(gain, in_ref, out_ref):
-    _, shards, piece, _ = in_ref.shape
-    total = (jnp.sum(in_ref[...].astype(F32), axis=0) * gain).astype(BF16)
-    for shard in range(shards):
-        at = (shard % 2) * (shards // 2) + shard // 2
-        out_ref[at * piece : (at + 1) * piece, :] = total[shard]
+    out_ref[...] = (jnp.sum(in_ref[...].astype(F32), axis=0) * gain).astype(BF16)
 
 
 def totals(parts, gain):
-    _, shards, piece, _ = parts.shape
     return pl.pallas_call(
         lambda *refs: total_kernel(gain, *refs),
         in_specs=[VMEM],
         out_specs=VMEM,
-        out_shape=jax.ShapeDtypeStruct((shards * piece, E), BF16),
+        out_shape=jax.ShapeDtypeStruct(parts.shape[1:], BF16),
         compiler_params=limit(4),
         name="totals",
     )(parts)
+
+
+def weave_kernel(at_ref, mine_ref, other_ref, out_ref):
+    shards, share, _ = mine_ref.shape
+    first = at_ref[1] == 0
+    for shard in range(shards):
+        at = ((shard % 2) * (shards // 2) + shard // 2) * 2 * share
+        mine, other = mine_ref[shard], other_ref[shard]
+        out_ref[at : at + share, :] = jnp.where(first, mine, other)
+        out_ref[at + share : at + 2 * share, :] = jnp.where(first, other, mine)
+
+
+def weave(place, mine, other):
+    shards, share, _ = mine.shape
+    return pl.pallas_call(
+        weave_kernel,
+        in_specs=[SMEM, VMEM, VMEM],
+        out_specs=VMEM,
+        out_shape=jax.ShapeDtypeStruct((2 * shards * share, E), BF16),
+        compiler_params=limit(4),
+        name="weave",
+    )(place, mine, other)
 
 
 def body(
@@ -478,7 +496,8 @@
     video_grad = keys(scale, khat, packed, float(frames * P_SIZE))
     pair_loss = loss[:, :, ::slots].reshape(-1, 1)
     parts, video_grad, pair_loss = lax.optimization_barrier((parts, video_grad, pair_loss))
-    query_grad = totals(parts.reshape((blocks, shards) + parts.shape[1:]), float(slots))
+    summed = totals(parts.reshape((blocks, shards) + parts.shape[1:]), float(slots))
+    query_grad = weave(place, summed, lax.ppermute(summed, "seq", partner))
     return (
         video_grad.reshape(1, frames, patch_loc, E),
         query_grad.reshape(query_dev, slots, E),

time: 102 us -> 102 us (level)
  waiting for transfers between devices: 26.7 us -> 25.4 us
    all_to_all x1, waiting for transfers between devices: 9.17 us -> 6.92 us  [body(): lax.all_to_all(parts.reshape((-1,) + parts.shape[2:]), ('dp', 'seq'), 0,...]
    pallas_call x0 -> x1, Pallas kernels: none -> 1.18 us  [weave(): pl.pallas_call(weave_kernel, in_specs=[SMEM, VMEM, VMEM], out_specs=VMEM,...]
  transfers between devices with their start and end apart: 8 -> 9, of which waited for: 6 -> 7; matrix products, arithmetic and copies ran while one was open for 2% -> 2% of each run, Pallas kernels for 18% -> 18%
where the time goes in v4:
time: 102 us; the launch traced here: 101 us
  Pallas kernels  38.5 us (38%)
  waiting for transfers between devices  25.4 us (25%)
  starting transfers between devices  22.5 us (22%)
  blocking collectives  12.7 us (12%)
    pallas_call x1, Pallas kernels, space(): pl.pallas_call(space_kernel, in_specs=[HBM] * 3, out_specs=HBM, out_shape...  13.8 us
    pallas_call x1, Pallas kernels, time(): pl.pallas_call(time_kernel, in_specs=[VMEM] + [HBM] * 3, out_specs=VMEM,...  13.2 us
    all_to_all x1, blocking collectives, body(): lax.all_to_all(joined, 'seq', 0, 0, tiled=True, axis_index_groups=chips)  12.7 us
    all_to_all x1, waiting for transfers between devices, body(): items = lax.all_to_all(spatial, 'seq', 0, 0, tiled=True)  10.4 us
    all_to_all x1, starting transfers between devices, body(): items = lax.all_to_all(spatial, 'seq', 0, 0, tiled=True)  9.14 us
    all_to_all x1, waiting for transfers between devices, body(): lax.all_to_all(parts.reshape((-1,) + parts.shape[2:]), ('dp', 'seq'), 0,...  6.92 us
    all_to_all x1, starting transfers between devices, body(): lax.all_to_all(parts.reshape((-1,) + parts.shape[2:]), ('dp', 'seq'), 0,...  6.74 us
    ppermute x3, waiting for transfers between devices, body(): lax.ppermute(mine, 'dp', [(i, (i + by) % blocks) for i in range(blocks)])  6.13 us
  transfers between devices with their start and end apart: 9, of which 7 were waited for; matrix products, arithmetic and copies ran while one was open for 2% of the time, Pallas kernels for 18%

profile of v4, /device:TPU:1, one launch (start us, length us, event | category | flops | bytes accessed | tf_op | source)
XLA Modules:
  0.0 101.5 jit_solution(5663292283824635490)
XLA Ops:
  0.6 13.8 %space.1 = bf16[16,4,16,768]{3,2,1,0:T(8,128)(2,1)} custom-call(bf16[4,256,768]{2,1,0:T(8,128)(2,1)} %bitcast.16, bf16[768,2304]{1,0:T(8,128)(2,1)} %qkv_ref.2, bf16[768,768]{1,0:T(8,128)(2,1)} %out_w_ref.2), custom_call_target="tpu_custom_call" | custom-call | tf_op jit(solution)/shard_map/space/pallas_call | solution.py:137
  14.4 9.1 %all-to-all-start = ((bf16[16,4,16,768]{3,2,1,0:T(8,128)(2,1)}), bf16[16,4,16,768]{3,2,1,0:T(8,128)(2,1)S(1)}, u32[]{:S(2)}, u32[]{:S(2)}) async-start(bf16[16,4,16,768]{3,2,1,0:T(8,128)(2,1)} %space.1), calls=%async_computation | async-start | bytes 3145728 | tf_op jit(solution)/shard_map/all_to_all | solution.py:474
  23.6 1.6 %pack_queries.1 = bf16[272,128]{1,0:T(8,128)(2,1)} custom-call(s32[8]{0:T(128)} %len_ref.1, s32[8]{0:T(128)} %pos_ref.1, bf16[256,128]{1,0:T(8,128)(2,1)} %bitcast.22), custom_call_target="tpu_custom_call" | custom-call | tf_op jit(solution)/shard_map/pack_queries/pallas_call | solution.py:242
  25.2 2.8 %collective-permute-start.2 = (bf16[272,128]{1,0:T(8,128)(2,1)}, bf16[272,128]{1,0:T(8,128)(2,1)S(1)}, u32[]{:S(2)}, u32[]{:S(2)}) collective-permute-start(bf16[272,128]{1,0:T(8,128)(2,1)} %pack_queries.1), channel_id=1, source_target_pairs={{0,96},{16,112},{32,0},{48,16},{64,32},{80,48},{96,64},{112,80},{1... | collective-permute-start | bytes 208904 | tf_op jit(solution)/shard_map/ppermute | solution.py:479
  28.0 0.3 collective-permute-start.1
  28.3 0.7 collective-permute-start
  29.0 0.8 collective-permute-done.2
  29.8 3.4 %collective-permute-done.1 = bf16[272,128]{1,0:T(8,128)(2,1)S(1)} collective-permute-done((bf16[272,128]{1,0:T(8,128)(2,1)}, bf16[272,128]{1,0:T(8,128)(2,1)S(1)}, u32[]{:S(2)}, u32[]{:S(2)}) %collective-permute-start.1) | collective-permute-done | bytes 69664 | tf_op jit(solution)/shard_map/ppermute | solution.py:479
  33.1 2.0 %collective-permute-done = bf16[272,128]{1,0:T(8,128)(2,1)S(1)} collective-permute-done((bf16[272,128]{1,0:T(8,128)(2,1)}, bf16[272,128]{1,0:T(8,128)(2,1)S(1)}, u32[]{:S(2)}, u32[]{:S(2)}) %collective-permute-start) | collective-permute-done | bytes 69664 | tf_op jit(solution)/shard_map/ppermute | solution.py:479
  35.1 0.9 pad_maximum_fusion.refs_2_
  36.1 10.4 %all-to-all-done = bf16[16,4,16,768]{3,2,1,0:T(8,128)(2,1)S(1)} async-done(((bf16[16,4,16,768]{3,2,1,0:T(8,128)(2,1)}), bf16[16,4,16,768]{3,2,1,0:T(8,128)(2,1)S(1)}, u32[]{:S(2)}, u32[]{:S(2)}) %all-to-all-start) | async-done | bytes 1572896 | tf_op jit(solution)/shard_map/all_to_all | solution.py:474
  46.4 0.7 collective-permute-start.3
  47.2 0.1 pad_add_fusion.refs_0_.at_ref
  47.2 13.2 %time.1.refs_1_ = bf16[1024,128]{1,0:T(8,128)(2,1)S(1)} custom-call(bf16[1024,768]{1,0:T(8,128)(2,1)S(1)} %bitcast.14, bf16[768,2304]{1,0:T(8,128)(2,1)} %qkv_ref.3, bf16[768,768]{1,0:T(8,128)(2,1)} %out_w_ref.3, bf16[768,128]{1,0:T(8,128)(2,1)} %proj_ref.1), custom_call_target="tpu_custom_call" | custom-call | tf_op jit(solution)/shard_map/time/pallas_call | solution.py:203
  60.4 0.0 collective-permute-done.3.refs_3_
  60.5 3.3 %terms.1 = (f32[8,128,128]{2,1,0:T(8,128)S(1)}, bf16[8,128,128]{2,1,0:T(8,128)(2,1)S(1)}, f32[16,128]{1,0:T(8,128)S(1)}) custom-call(s32[3]{0:T(128)S(1)} %pad_add_fusion.refs_0_.at_ref, bf16[1024,128]{1,0:T(8,128)(2,1)S(1)} %time.1.refs_1_, bf16[4,272,128]{2,1,0:T(8,128)(2,1)S(1)} %pad_maximum_fusion.refs_2_, ...), custom_call_target="tpu_custom_call" | custom-call | tf_op jit(solution)/shard_map/terms/pallas_call | solution.py:287
  63.7 1.2 %collective-permute-start.4 = (bf16[8,128,128]{2,1,0:T(8,128)(2,1)S(1)}, bf16[8,128,128]{2,1,0:T(8,128)(2,1)S(1)}, u32[]{:S(2)}, u32[]{:S(2)}) collective-permute-start(bf16[8,128,128]{2,1,0:T(8,128)(2,1)S(1)} %get-tuple-element.21), channel_id=1, source_target_pairs={{0,1},{1,0},{2,3},{3,2},{4,5},{5,4},{6,7},{7,6},{8,9},{9,8},{10,11... | collective-permute-start | bytes 786440 | tf_op jit(solution)/shard_map/ppermute | solution.py:488
  64.9 0.1 collective-permute-start.5
  65.0 1.1 %collective-permute-done.5.others_ref = f32[16,128]{1,0:T(8,128)S(1)} collective-permute-done((f32[16,128]{1,0:T(8,128)S(1)}, f32[16,128]{1,0:T(8,128)S(1)}, u32[]{:S(2)}, u32[]{:S(2)}) %collective-permute-start.5) | collective-permute-done | bytes 8224 | tf_op jit(solution)/shard_map/ppermute | solution.py:489
  66.1 0.0 collective-permute-done.4.got_ref
  66.1 0.1 join.1
  66.2 12.7 %all_to_all.15.refs_1_ = bf16[8,160,128]{2,1,0:T(8,128)(2,1)S(1)} all-to-all(bf16[8,160,128]{2,1,0:T(8,128)(2,1)S(1)} %join.1), channel_id=1, replica_groups={{0,2,4,6,8,10,12,14},{1,3,5,7,9,11,13,15},{16,18,20,22,24,26,28,30},{17..., dimensions={0} | all-to-all | bytes 655360 | tf_op jit(solution)/shard_map/all_to_all | solution.py:491
  78.9 1.7 %scales.1 = (bf16[8,16,8,128]{3,2,1,0:T(8,128)(2,1)}, f32[128,16]{1,0:T(8,128)S(1)}, f32[8,2,128]{2,1,0:T(2,128)S(1)}) custom-call(s32[3]{0:T(128)S(1)} %pad_add_fusion.refs_0_.at_ref, bf16[8,160,128]{2,1,0:T(8,128)(2,1)S(1)} %all_to_all.15.refs_1_, bf16[4,272,128]{2,1,0:T(8,128)(2,1)S(1)} %pad_maximum_fusion.refs_2_, ...), custom_call_target="tpu_custom_call" | custom-call | tf_op jit(solution)/shard_map/scales/pallas_call | solution.py:378
  80.6 6.7 %all-to-all-start.2 = ((bf16[128,8,128]{2,1,0:T(8,128)(2,1)}), bf16[128,8,128]{2,1,0:T(8,128)(2,1)S(1)}, u32[]{:S(2)}, u32[]{:S(2)}) async-start(bf16[128,8,128]{2,1,0:T(8,128)(2,1)} %bitcast.10), calls=%async_computation.2 | async-start | bytes 524288 | tf_op jit(solution)/shard_map/all_to_all | solution.py:493
  87.4 0.1 slice.3
  87.5 0.6 reshape.30
  88.1 3.6 %keys.1 = bf16[1024,128]{1,0:T(8,128)(2,1)} custom-call(f32[128,16]{1,0:T(8,128)S(1)} %get-tuple-element.24.refs_0_, bf16[1024,128]{1,0:T(8,128)(2,1)S(1)} %time.1.refs_1_, bf16[4,272,128]{2,1,0:T(8,128)(2,1)S(1)} %pad_maximum_fusion.refs_2_, bf16[4,272,128]{2,1,0:T(8,128)(2,1)S(1)} %collective-permute-done.3.refs_3_), custom_call_target="tpu_custom_call" | custom-call | tf_op jit(solution)/shard_map/keys/pallas_call | solution.py:410
  91.7 6.9 %all-to-all-done.2 = bf16[128,8,128]{2,1,0:T(8,128)(2,1)S(1)} async-done(((bf16[128,8,128]{2,1,0:T(8,128)(2,1)}), bf16[128,8,128]{2,1,0:T(8,128)(2,1)S(1)}, u32[]{:S(2)}, u32[]{:S(2)}) %all-to-all-start.2) | async-done | bytes 262176 | tf_op jit(solution)/shard_map/all_to_all | solution.py:493
  98.7 0.8 collective-permute-start.6
  99.4 0.9 collective-permute-done.6.other_ref
  100.3 1.2 %weave.1 = bf16[256,128]{1,0:T(8,128)(2,1)} custom-call(s32[3]{0:T(128)S(1)} %pad_add_fusion.refs_0_.at_ref, bf16[16,8,128]{2,1,0:T(8,128)(2,1)S(1)} %totals.1.mine_ref, bf16[16,8,128]{2,1,0:T(8,128)(2,1)S(1)} %collective-permute-done.6.other_ref), custom_call_target="tpu_custom_call" | custom-call | tf_op jit(solution)/shard_map/weave/pallas_call | solution.py:447
  (1 shorter events, 0.0 us)
Async XLA Ops:
  14.4 32.0 %all-to-all-start = ((bf16[16,4,16,768]{3,2,1,0:T(8,128)(2,1)}), bf16[16,4,16,768]{3,2,1,0:T(8,128)(2,1)S(1)}, u32[]{:S(2)}, u32[]{:S(2)}) async-start(bf16[16,4,16,768]{3,2,1,0:T(8,128)(2,1)} %space.1), calls=%async_computation | async-start | bytes 3145728 | tf_op jit(solution)/shard_map/all_to_all | solution.py:474
  25.2 4.6 %collective-permute-start.2 = (bf16[272,128]{1,0:T(8,128)(2,1)}, bf16[272,128]{1,0:T(8,128)(2,1)S(1)}, u32[]{:S(2)}, u32[]{:S(2)}) collective-permute-start(bf16[272,128]{1,0:T(8,128)(2,1)} %pack_queries.1), channel_id=1, source_target_pairs={{0,96},{16,112},{32,0},{48,16},{64,32},{80,48},{96,64},{112,80},{1... | collective-permute-start | bytes 208904 | tf_op jit(solution)/shard_map/ppermute | solution.py:479
  28.0 5.2 %collective-permute-start.1 = (bf16[272,128]{1,0:T(8,128)(2,1)}, bf16[272,128]{1,0:T(8,128)(2,1)S(1)}, u32[]{:S(2)}, u32[]{:S(2)}) collective-permute-start(bf16[272,128]{1,0:T(8,128)(2,1)} %pack_queries.1), channel_id=1, source_target_pairs={{0,64},{16,80},{32,96},{48,112},{64,0},{80,16},{96,32},{112,48},{1... | collective-permute-start | bytes 208904 | tf_op jit(solution)/shard_map/ppermute | solution.py:479
  28.3 6.8 %collective-permute-start = (bf16[272,128]{1,0:T(8,128)(2,1)}, bf16[272,128]{1,0:T(8,128)(2,1)S(1)}, u32[]{:S(2)}, u32[]{:S(2)}) collective-permute-start(bf16[272,128]{1,0:T(8,128)(2,1)} %pack_queries.1), channel_id=1, source_target_pairs={{0,32},{16,48},{32,64},{48,80},{64,96},{80,112},{96,0},{112,16},{1... | collective-permute-start | bytes 208904 | tf_op jit(solution)/shard_map/ppermute | solution.py:479
  46.4 14.0 %collective-permute-start.3 = (bf16[4,272,128]{2,1,0:T(8,128)(2,1)S(1)}, bf16[4,272,128]{2,1,0:T(8,128)(2,1)S(1)}, u32[]{:S(2)}, u32[]{:S(2)}) collective-permute-start(bf16[4,272,128]{2,1,0:T(8,128)(2,1)S(1)} %pad_maximum_fusion.refs_2_), channel_id=1, source_target_pairs={{0,16},{16,0},{32,48},{48,32},{64,80},{80,64},{96,112},{112,96},{1... | collective-permute-start | bytes 835592 | tf_op jit(solution)/shard_map/ppermute | solution.py:484
  63.7 2.4 %collective-permute-start.4 = (bf16[8,128,128]{2,1,0:T(8,128)(2,1)S(1)}, bf16[8,128,128]{2,1,0:T(8,128)(2,1)S(1)}, u32[]{:S(2)}, u32[]{:S(2)}) collective-permute-start(bf16[8,128,128]{2,1,0:T(8,128)(2,1)S(1)} %get-tuple-element.21), channel_id=1, source_target_pairs={{0,1},{1,0},{2,3},{3,2},{4,5},{5,4},{6,7},{7,6},{8,9},{9,8},{10,11... | collective-permute-start | bytes 786440 | tf_op jit(solution)/shard_map/ppermute | solution.py:488
  64.9 1.2 %collective-permute-start.5 = (f32[16,128]{1,0:T(8,128)S(1)}, f32[16,128]{1,0:T(8,128)S(1)}, u32[]{:S(2)}, u32[]{:S(2)}) collective-permute-start(f32[16,128]{1,0:T(8,128)S(1)} %get-tuple-element.22.sums_ref), channel_id=1, source_target_pairs={{0,1},{1,0},{2,3},{3,2},{4,5},{5,4},{6,7},{7,6},{8,9},{9,8},{10,11... | collective-permute-start | bytes 24584 | tf_op jit(solution)/shard_map/ppermute | solution.py:489
  80.6 18.0 %all-to-all-start.2 = ((bf16[128,8,128]{2,1,0:T(8,128)(2,1)}), bf16[128,8,128]{2,1,0:T(8,128)(2,1)S(1)}, u32[]{:S(2)}, u32[]{:S(2)}) async-start(bf16[128,8,128]{2,1,0:T(8,128)(2,1)} %bitcast.10), calls=%async_computation.2 | async-start | bytes 524288 | tf_op jit(solution)/shard_map/all_to_all | solution.py:493
  98.7 1.6 %collective-permute-start.6 = (bf16[16,8,128]{2,1,0:T(8,128)(2,1)S(1)}, bf16[16,8,128]{2,1,0:T(8,128)(2,1)S(1)}, u32[]{:S(2)}, u32[]{:S(2)}) collective-permute-start(bf16[16,8,128]{2,1,0:T(8,128)(2,1)S(1)} %totals.1.mine_ref), channel_id=1, source_target_pairs={{0,1},{1,0},{2,3},{3,2},{4,5},{5,4},{6,7},{7,6},{8,9},{9,8},{10,11... | collective-permute-start | bytes 98312 | tf_op jit(solution)/shard_map/ppermute | solution.py:500

commit v5 on v4

--- a/solution.py
+++ b/solution.py
@@ -244,8 +244,14 @@
         in_specs=[SMEM, SMEM, VMEM],
         out_specs=VMEM,
         out_shape=jax.ShapeDtypeStruct((rows + EXTRA, E), BF16),
+        compiler_params=limit(4),
         name="pack_queries",
     )(query_len, positive, queries)
+
+
+def own_place():
+    seat = lax.axis_index("seq")
+    return lax.axis_index("dp"), lax.rem(seat, 2), seat // 2
 
 
 def group_of(mine, blocks, block):
@@ -263,10 +269,10 @@
     return jnp.exp2(dot_t(query, khat) * gain - gain).astype(BF16)
 
 
-def terms_kernel(blocks, at_ref, khat_ref, *refs):
+def terms_kernel(blocks, khat_ref, *refs):
     packed_refs, (keep_ref, send_ref, sums_ref) = refs[:-3], refs[-3:]
     rows = packed_refs[0].shape[1] - EXTRA
-    first = at_ref[1] == 0
+    first = own_place()[1] == 0
     khat = khat_ref[...]
     wide = jnp.concatenate([khat, jnp.ones_like(khat)], axis=1)
     eye = iota((E, E), 0) == iota((E, E), 1)
@@ -282,11 +288,11 @@
     sums_ref[...] = jnp.concatenate(sums, axis=0)
 
 
-def terms(packed, khat, place):
+def terms(packed, khat):
     blocks, rows = 2 * packed[0].shape[0], packed[0].shape[1] - EXTRA
     return pl.pallas_call(
         lambda *refs: terms_kernel(blocks, *refs),
-        in_specs=[SMEM] + [VMEM] * (1 + len(packed)),
+        in_specs=[VMEM] * (1 + len(packed)),
         out_specs=[VMEM] * 3,
         out_shape=[
             jax.ShapeDtypeStruct((blocks, rows // 2, E), F32),
@@ -295,7 +301,7 @@
         ],
         compiler_params=limit(16),
         name="terms",
-    )(place, khat, *packed)
+    )(khat, *packed)
 
 
 def join_kernel(keep_ref, got_ref, sums_ref, others_ref, out_ref):
@@ -330,10 +336,11 @@
     )(keep, got, sums, others)
 
 
-def scale_kernel(slots, at_ref, got_ref, *refs):
+def scale_kernel(slots, got_ref, *refs):
     packed_refs, (part_ref, scale_ref, loss_ref) = refs[:-3], refs[-3:]
     blocks, shards, share, _ = part_ref.shape
     piece = 2 * share
+    video, core, chip = own_place()
     rows = packed_refs[0].shape[1] - EXTRA
     per = rows // E
     got = jnp.sum(got_ref[...].astype(F32), axis=0)
@@ -355,15 +362,15 @@
         )
         / lens
     )
-    sign = jnp.where(pos == at_ref[0].astype(F32), 1.0, -1.0)
+    sign = jnp.where(pos == video.astype(F32), 1.0, -1.0)
     margin = sign * (SLOPE * score + OFFSET)
     loss = jnp.maximum(-margin, 0.0) + jnp.log1p(jnp.exp(-jnp.abs(margin)))
     coeff = -SLOPE * sign / (1.0 + jnp.exp(margin)) * mask / lens
     scale_ref[...] = (coeff / total).T
-    scale = scale_ref[pl.ds(pl.multiple_of(at_ref[2] * piece, piece), piece), :]
-    first = at_ref[1] == 0
+    scale = scale_ref[pl.ds(pl.multiple_of(chip * piece, piece), piece), :]
+    first = core == 0
     for block in range(blocks):
-        group = group_of(at_ref[0], blocks, block)
+        group = group_of(video, blocks, block)
         at = block * per
         column = jnp.where(first, scale[:, at : at + 1], scale[:, at + 1 : at + 2])
         part = (blend[block * piece : (block + 1) * piece] * column).astype(BF16)
@@ -372,12 +379,12 @@
         loss_ref[group] = loss[at : at + per]
 
 
-def scales(got, packed, place, slots, shards):
+def scales(got, packed, slots, shards):
     blocks, rows = 2 * packed[0].shape[0], packed[0].shape[1] - EXTRA
     share = rows // shards // 2
     return pl.pallas_call(
         lambda *refs: scale_kernel(slots, *refs),
-        in_specs=[SMEM] + [VMEM] * (1 + len(packed)),
+        in_specs=[VMEM] * (1 + len(packed)),
         out_specs=[VMEM] * 3,
         out_shape=[
             jax.ShapeDtypeStruct((blocks, shards, share, E), BF16),
@@ -386,7 +393,7 @@
         ],
         compiler_params=limit(8),
         name="scales",
-    )(place, got, *packed)
+    )(got, *packed)
 
 
 def keys_kernel(gain, blocks, scale_ref, khat_ref, *refs):
@@ -432,9 +439,9 @@
     )(parts)
 
 
-def weave_kernel(at_ref, mine_ref, other_ref, out_ref):
+def weave_kernel(mine_ref, other_ref, out_ref):
     shards, share, _ = mine_ref.shape
-    first = at_ref[1] == 0
+    first = own_place()[1] == 0
     for shard in range(shards):
         at = ((shard % 2) * (shards // 2) + shard // 2) * 2 * share
         mine, other = mine_ref[shard], other_ref[shard]
@@ -442,16 +449,16 @@
         out_ref[at + share : at + 2 * share, :] = jnp.where(first, other, mine)
 
 
-def weave(place, mine, other):
+def weave(mine, other):
     shards, share, _ = mine.shape
     return pl.pallas_call(
         weave_kernel,
-        in_specs=[SMEM, VMEM, VMEM],
+        in_specs=[VMEM, VMEM],
         out_specs=VMEM,
         out_shape=jax.ShapeDtypeStruct((2 * shards * share, E), BF16),
         compiler_params=limit(4),
         name="weave",
-    )(place, mine, other)
+    )(mine, other)
 
 
 def body(
@@ -464,8 +471,6 @@
     frames = frames_dev * shards
     query_dev, slots, _ = queries.shape
     rows = query_dev * slots
-    seat = lax.axis_index("seq")
-    place = jnp.stack([lax.axis_index("dp"), lax.rem(seat, 2), seat // 2]).astype(jnp.int32)
     partner = [(i, i ^ 1) for i in range(shards)]
     chips = [[2 * chip + own for chip in range(shards // 2)] for own in range(2)]
 
@@ -484,24 +489,23 @@
     packed = [lane, lax.ppermute(lane, "dp", [(i, i ^ 1) for i in range(blocks)])]
     khat = time(items.reshape(-1, D), time_qkv, time_out, proj_weight, patch_loc)
 
-    keep, send, sums = terms(packed, khat, place)
+    keep, send, sums = terms(packed, khat)
     got = lax.ppermute(send, "seq", partner)
     others = lax.ppermute(sums, "seq", partner)
     joined = join(keep, got, sums, others, shards // 2)
     joined = lax.all_to_all(joined, "seq", 0, 0, tiled=True, axis_index_groups=chips)
-    parts, scale, loss = scales(joined, packed, place, slots, shards)
+    parts, scale, loss = scales(joined, packed, slots, shards)
     parts = lax.all_to_all(
         parts.reshape((-1,) + parts.shape[2:]), ("dp", "seq"), 0, 0, tiled=True
     )
     video_grad = keys(scale, khat, packed, float(frames * P_SIZE))
-    pair_loss = loss[:, :, ::slots].reshape(-1, 1)
-    parts, video_grad, pair_loss = lax.optimization_barrier((parts, video_grad, pair_loss))
+    parts, video_grad = lax.optimization_barrier((parts, video_grad))
     summed = totals(parts.reshape((blocks, shards) + parts.shape[1:]), float(slots))
-    query_grad = weave(place, summed, lax.ppermute(summed, "seq", partner))
+    query_grad = weave(summed, lax.ppermute(summed, "seq", partner))
     return (
         video_grad.reshape(1, frames, patch_loc, E),
         query_grad.reshape(query_dev, slots, E),
-        pair_loss,
+        loss[:, :, ::slots].reshape(-1, 1),
     )
 
 

time: 102 us -> 100 us (0.980)
  Pallas kernels: 38.5 us -> 35.9 us
  waiting for transfers between devices: 25.4 us -> 27.1 us
    all_to_all x1, waiting for transfers between devices: 10.4 us -> 12.3 us  [body(): items = lax.all_to_all(spatial, 'seq', 0, 0, tiled=True)]
    pallas_call x3, Pallas kernels: 6.17 us -> 4.54 us  [the longest x1 2.72 us: terms(): pl.pallas_call(lambda *refs: terms_kernel(blocks, *refs), in_specs=[VMEM]...]
  transfers between devices with their start and end apart: 9 -> 9, of which waited for: 7 -> 7; matrix products, arithmetic and copies ran while one was open for 2% -> 1% of each run, Pallas kernels for 18% -> 18%
where the time goes in v5:
time: 100 us; the launch traced here: 99.9 us
  Pallas kernels  35.9 us (36%)
  waiting for transfers between devices  27.1 us (27%)
  starting transfers between devices  22.7 us (23%)
  blocking collectives  12.7 us (13%)
    pallas_call x1, Pallas kernels, space(): pl.pallas_call(space_kernel, in_specs=[HBM] * 3, out_specs=HBM, out_shape...  13.8 us
    pallas_call x1, Pallas kernels, time(): pl.pallas_call(time_kernel, in_specs=[VMEM] + [HBM] * 3, out_specs=VMEM,...  13.2 us
    all_to_all x1, blocking collectives, body(): lax.all_to_all(joined, 'seq', 0, 0, tiled=True, axis_index_groups=chips)  12.7 us
    all_to_all x1, waiting for transfers between devices, body(): items = lax.all_to_all(spatial, 'seq', 0, 0, tiled=True)  12.3 us
    all_to_all x1, starting transfers between devices, body(): items = lax.all_to_all(spatial, 'seq', 0, 0, tiled=True)  9.28 us
    all_to_all x1, waiting for transfers between devices, body(): lax.all_to_all(parts.reshape((-1,) + parts.shape[2:]), ('dp', 'seq'), 0,...  7.63 us
    all_to_all x1, starting transfers between devices, body(): lax.all_to_all(parts.reshape((-1,) + parts.shape[2:]), ('dp', 'seq'), 0,...  6.72 us
    ppermute x3, waiting for transfers between devices, body(): lax.ppermute(mine, 'dp', [(i, (i + by) % blocks) for i in range(blocks)])  5.92 us
  transfers between devices with their start and end apart: 9, of which 7 were waited for; matrix products, arithmetic and copies ran while one was open for 1% of the time, Pallas kernels for 18%

profile of v5, /device:TPU:1, one launch (start us, length us, event | category | flops | bytes accessed | tf_op | source)
XLA Modules:
  0.0 99.9 jit_solution(10984957988068657214)
XLA Ops:
  0.6 13.8 %space.1 = bf16[16,4,16,768]{3,2,1,0:T(8,128)(2,1)} custom-call(bf16[4,256,768]{2,1,0:T(8,128)(2,1)} %bitcast.15, bf16[768,2304]{1,0:T(8,128)(2,1)} %qkv_ref.2, bf16[768,768]{1,0:T(8,128)(2,1)} %out_w_ref.2), custom_call_target="tpu_custom_call" | custom-call | tf_op jit(solution)/shard_map/space/pallas_call | solution.py:137
  14.4 0.0 copy-start
  14.4 0.0 copy-start.1
  14.4 0.0 copy-start.2
  14.4 9.3 %all-to-all-start = ((bf16[16,4,16,768]{3,2,1,0:T(8,128)(2,1)}), bf16[16,4,16,768]{3,2,1,0:T(8,128)(2,1)S(1)}, u32[]{:S(2)}, u32[]{:S(2)}) async-start(bf16[16,4,16,768]{3,2,1,0:T(8,128)(2,1)} %space.1), calls=%async_computation | async-start | bytes 3145728 | tf_op jit(solution)/shard_map/all_to_all | solution.py:479
  23.7 0.7 pack_queries.1
  24.4 2.8 %collective-permute-start.2 = (bf16[272,128]{1,0:T(8,128)(2,1)S(1)}, bf16[272,128]{1,0:T(8,128)(2,1)S(1)}, u32[]{:S(2)}, u32[]{:S(2)}) collective-permute-start(bf16[272,128]{1,0:T(8,128)(2,1)S(1)} %pack_queries.1), channel_id=1, source_target_pairs={{0,96},{16,112},{32,0},{48,16},{64,32},{80,48},{96,64},{112,80},{1... | collective-permute-start | bytes 208904 | tf_op jit(solution)/shard_map/ppermute | solution.py:484
  27.3 0.3 collective-permute-start.1
  27.6 0.7 collective-permute-start
  28.3 0.3 collective-permute-done.2
  28.6 3.6 %collective-permute-done.1 = bf16[272,128]{1,0:T(8,128)(2,1)S(1)} collective-permute-done((bf16[272,128]{1,0:T(8,128)(2,1)S(1)}, bf16[272,128]{1,0:T(8,128)(2,1)S(1)}, u32[]{:S(2)}, u32[]{:S(2)}) %collective-permute-start.1) | collective-permute-done | bytes 69664 | tf_op jit(solution)/shard_map/ppermute | solution.py:484
  32.2 2.0 %collective-permute-done = bf16[272,128]{1,0:T(8,128)(2,1)S(1)} collective-permute-done((bf16[272,128]{1,0:T(8,128)(2,1)S(1)}, bf16[272,128]{1,0:T(8,128)(2,1)S(1)}, u32[]{:S(2)}, u32[]{:S(2)}) %collective-permute-start) | collective-permute-done | bytes 69664 | tf_op jit(solution)/shard_map/ppermute | solution.py:484
  34.3 12.3 %all-to-all-done = bf16[16,4,16,768]{3,2,1,0:T(8,128)(2,1)S(1)} async-done(((bf16[16,4,16,768]{3,2,1,0:T(8,128)(2,1)}), bf16[16,4,16,768]{3,2,1,0:T(8,128)(2,1)S(1)}, u32[]{:S(2)}, u32[]{:S(2)}) %all-to-all-start) | async-done | bytes 1572896 | tf_op jit(solution)/shard_map/all_to_all | solution.py:479
  46.6 0.7 collective-permute-start.3
  47.3 13.2 %time.1.refs_0_.refs_1_ = bf16[1024,128]{1,0:T(8,128)(2,1)S(1)} custom-call(bf16[1024,768]{1,0:T(8,128)(2,1)S(1)} %bitcast.11, bf16[768,2304]{1,0:T(8,128)(2,1)} %qkv_ref.3, bf16[768,768]{1,0:T(8,128)(2,1)} %out_w_ref.3, bf16[768,128]{1,0:T(8,128)(2,1)} %proj_ref.1), custom_call_target="tpu_custom_call" | custom-call | tf_op jit(solution)/shard_map/time/pallas_call | solution.py:203
  60.5 0.0 collective-permute-done.3.refs_2_.refs_3_
  60.5 2.7 %terms.1 = (f32[8,128,128]{2,1,0:T(8,128)S(1)}, bf16[8,128,128]{2,1,0:T(8,128)(2,1)S(1)}, f32[16,128]{1,0:T(8,128)S(1)}) custom-call(bf16[1024,128]{1,0:T(8,128)(2,1)S(1)} %time.1.refs_0_.refs_1_, bf16[4,272,128]{2,1,0:T(8,128)(2,1)S(1)} %pad_maximum_fusion.refs_1_.refs_2_, bf16[4,272,128]{2,1,0:T(8,128)(2,1)S(1)} %collective-permute-done.3.refs_2_.refs_3_), custom_call_target="tpu_custom_call" | custom-call | tf_op jit(solution)/shard_map/terms/pallas_call | solution.py:293
  63.2 1.2 %collective-permute-start.4 = (bf16[8,128,128]{2,1,0:T(8,128)(2,1)S(1)}, bf16[8,128,128]{2,1,0:T(8,128)(2,1)S(1)}, u32[]{:S(2)}, u32[]{:S(2)}) collective-permute-start(bf16[8,128,128]{2,1,0:T(8,128)(2,1)S(1)} %get-tuple-element.20), channel_id=1, source_target_pairs={{0,1},{1,0},{2,3},{3,2},{4,5},{5,4},{6,7},{7,6},{8,9},{9,8},{10,11... | collective-permute-start | bytes 786440 | tf_op jit(solution)/shard_map/ppermute | solution.py:493
  64.5 0.1 collective-permute-start.5
  64.6 1.1 %collective-permute-done.5.others_ref = f32[16,128]{1,0:T(8,128)S(1)} collective-permute-done((f32[16,128]{1,0:T(8,128)S(1)}, f32[16,128]{1,0:T(8,128)S(1)}, u32[]{:S(2)}, u32[]{:S(2)}) %collective-permute-start.5) | collective-permute-done | bytes 8224 | tf_op jit(solution)/shard_map/ppermute | solution.py:494
  65.6 0.0 collective-permute-done.4.got_ref
  65.6 0.1 join.1
  65.7 12.7 %all_to_all.15.refs_0_ = bf16[8,160,128]{2,1,0:T(8,128)(2,1)S(1)} all-to-all(bf16[8,160,128]{2,1,0:T(8,128)(2,1)S(1)} %join.1), channel_id=1, replica_groups={{0,2,4,6,8,10,12,14},{1,3,5,7,9,11,13,15},{16,18,20,22,24,26,28,30},{17..., dimensions={0} | all-to-all | bytes 655360 | tf_op jit(solution)/shard_map/all_to_all | solution.py:496
  78.4 1.2 %scales.1 = (bf16[8,16,8,128]{3,2,1,0:T(8,128)(2,1)}, f32[128,16]{1,0:T(8,128)S(1)}, f32[8,2,128]{2,1,0:T(2,128)S(1)}) custom-call(bf16[8,160,128]{2,1,0:T(8,128)(2,1)S(1)} %all_to_all.15.refs_0_, bf16[4,272,128]{2,1,0:T(8,128)(2,1)S(1)} %pad_maximum_fusion.refs_1_.refs_2_, bf16[4,272,128]{2,1,0:T(8,128)(2,1)S(1)} %collective-permute-done.3.refs_2_.refs_3_), custom_call_target="tpu_custom_call" | custom-call | tf_op jit(solution)/shard_map/scales/pallas_call | solution.py:385
  79.6 6.7 %all-to-all-start.2 = ((bf16[128,8,128]{2,1,0:T(8,128)(2,1)}), bf16[128,8,128]{2,1,0:T(8,128)(2,1)S(1)}, u32[]{:S(2)}, u32[]{:S(2)}) async-start(bf16[128,8,128]{2,1,0:T(8,128)(2,1)} %bitcast.7), calls=%async_computation.2 | async-start | bytes 524288 | tf_op jit(solution)/shard_map/all_to_all | solution.py:498
  86.3 3.6 %keys.1 = bf16[1024,128]{1,0:T(8,128)(2,1)} custom-call(f32[128,16]{1,0:T(8,128)S(1)} %get-tuple-element.23.refs_0_, bf16[1024,128]{1,0:T(8,128)(2,1)S(1)} %time.1.refs_0_.refs_1_, bf16[4,272,128]{2,1,0:T(8,128)(2,1)S(1)} %pad_maximum_fusion.refs_1_.refs_2_, bf16[4,272,128]{2,1,0:T(8,128)(2,1)S(1)} %collective-permute-done.3.refs_2_.refs_3_), custom_call_target="tpu_custom_call" | custom-call | tf_op jit(solution)/shard_map/keys/pallas_call | solution.py:417
  90.0 7.6 %all-to-all-done.2 = bf16[128,8,128]{2,1,0:T(8,128)(2,1)S(1)} async-done(((bf16[128,8,128]{2,1,0:T(8,128)(2,1)}), bf16[128,8,128]{2,1,0:T(8,128)(2,1)S(1)}, u32[]{:S(2)}, u32[]{:S(2)}) %all-to-all-start.2) | async-done | bytes 262176 | tf_op jit(solution)/shard_map/all_to_all | solution.py:498
  97.6 0.8 collective-permute-start.6
  98.4 0.1 slice.3
  98.5 0.6 reshape.33
  99.1 0.2 collective-permute-done.6.other_ref
  99.3 0.6 weave.1
  (5 shorter events, 0.1 us)
Async XLA Ops:
  14.4 9.3 %copy-start = (bf16[8,32,128]{2,1,0:T(8,128)(2,1)S(1)}, bf16[8,32,128]{2,1,0:T(8,128)(2,1)}, u32[]{:S(2)}) copy-start(bf16[8,32,128]{2,1,0:T(8,128)(2,1)} %param.15) | copy-start | bytes 196612
  14.4 9.3 %copy-start.1 = (s32[8]{0:T(128)S(1)}, s32[8]{0:T(128)}, u32[]{:S(2)}) copy-start(s32[8]{0:T(128)} %len_ref.1) | copy-start | bytes 100
  14.4 9.3 %copy-start.2 = (s32[8]{0:T(128)S(1)}, s32[8]{0:T(128)}, u32[]{:S(2)}) copy-start(s32[8]{0:T(128)} %pos_ref.1) | copy-start | bytes 100
  14.4 32.1 %all-to-all-start = ((bf16[16,4,16,768]{3,2,1,0:T(8,128)(2,1)}), bf16[16,4,16,768]{3,2,1,0:T(8,128)(2,1)S(1)}, u32[]{:S(2)}, u32[]{:S(2)}) async-start(bf16[16,4,16,768]{3,2,1,0:T(8,128)(2,1)} %space.1), calls=%async_computation | async-start | bytes 3145728 | tf_op jit(solution)/shard_map/all_to_all | solution.py:479
  24.4 4.2 %collective-permute-start.2 = (bf16[272,128]{1,0:T(8,128)(2,1)S(1)}, bf16[272,128]{1,0:T(8,128)(2,1)S(1)}, u32[]{:S(2)}, u32[]{:S(2)}) collective-permute-start(bf16[272,128]{1,0:T(8,128)(2,1)S(1)} %pack_queries.1), channel_id=1, source_target_pairs={{0,96},{16,112},{32,0},{48,16},{64,32},{80,48},{96,64},{112,80},{1... | collective-permute-start | bytes 208904 | tf_op jit(solution)/shard_map/ppermute | solution.py:484
  27.3 5.0 %collective-permute-start.1 = (bf16[272,128]{1,0:T(8,128)(2,1)S(1)}, bf16[272,128]{1,0:T(8,128)(2,1)S(1)}, u32[]{:S(2)}, u32[]{:S(2)}) collective-permute-start(bf16[272,128]{1,0:T(8,128)(2,1)S(1)} %pack_queries.1), channel_id=1, source_target_pairs={{0,64},{16,80},{32,96},{48,112},{64,0},{80,16},{96,32},{112,48},{1... | collective-permute-start | bytes 208904 | tf_op jit(solution)/shard_map/ppermute | solution.py:484
  27.6 6.6 %collective-permute-start = (bf16[272,128]{1,0:T(8,128)(2,1)S(1)}, bf16[272,128]{1,0:T(8,128)(2,1)S(1)}, u32[]{:S(2)}, u32[]{:S(2)}) collective-permute-start(bf16[272,128]{1,0:T(8,128)(2,1)S(1)} %pack_queries.1), channel_id=1, source_target_pairs={{0,32},{16,48},{32,64},{48,80},{64,96},{80,112},{96,0},{112,16},{1... | collective-permute-start | bytes 208904 | tf_op jit(solution)/shard_map/ppermute | solution.py:484
  46.6 14.0 %collective-permute-start.3 = (bf16[4,272,128]{2,1,0:T(8,128)(2,1)S(1)}, bf16[4,272,128]{2,1,0:T(8,128)(2,1)S(1)}, u32[]{:S(2)}, u32[]{:S(2)}) collective-permute-start(bf16[4,272,128]{2,1,0:T(8,128)(2,1)S(1)} %pad_maximum_fusion.refs_1_.refs_2_), channel_id=1, source_target_pairs={{0,16},{16,0},{32,48},{48,32},{64,80},{80,64},{96,112},{112,96},{1... | collective-permute-start | bytes 835592 | tf_op jit(solution)/shard_map/ppermute | solution.py:489
  63.2 2.4 %collective-permute-start.4 = (bf16[8,128,128]{2,1,0:T(8,128)(2,1)S(1)}, bf16[8,128,128]{2,1,0:T(8,128)(2,1)S(1)}, u32[]{:S(2)}, u32[]{:S(2)}) collective-permute-start(bf16[8,128,128]{2,1,0:T(8,128)(2,1)S(1)} %get-tuple-element.20), channel_id=1, source_target_pairs={{0,1},{1,0},{2,3},{3,2},{4,5},{5,4},{6,7},{7,6},{8,9},{9,8},{10,11... | collective-permute-start | bytes 786440 | tf_op jit(solution)/shard_map/ppermute | solution.py:493
  64.5 1.2 %collective-permute-start.5 = (f32[16,128]{1,0:T(8,128)S(1)}, f32[16,128]{1,0:T(8,128)S(1)}, u32[]{:S(2)}, u32[]{:S(2)}) collective-permute-start(f32[16,128]{1,0:T(8,128)S(1)} %get-tuple-element.21.sums_ref), channel_id=1, source_target_pairs={{0,1},{1,0},{2,3},{3,2},{4,5},{5,4},{6,7},{7,6},{8,9},{9,8},{10,11... | collective-permute-start | bytes 24584 | tf_op jit(solution)/shard_map/ppermute | solution.py:494
  79.6 18.0 %all-to-all-start.2 = ((bf16[128,8,128]{2,1,0:T(8,128)(2,1)}), bf16[128,8,128]{2,1,0:T(8,128)(2,1)S(1)}, u32[]{:S(2)}, u32[]{:S(2)}) async-start(bf16[128,8,128]{2,1,0:T(8,128)(2,1)} %bitcast.7), calls=%async_computation.2 | async-start | bytes 524288 | tf_op jit(solution)/shard_map/all_to_all | solution.py:498
  97.6 1.6 %collective-permute-start.6 = (bf16[16,8,128]{2,1,0:T(8,128)(2,1)S(1)}, bf16[16,8,128]{2,1,0:T(8,128)(2,1)S(1)}, u32[]{:S(2)}, u32[]{:S(2)}) collective-permute-start(bf16[16,8,128]{2,1,0:T(8,128)(2,1)S(1)} %totals.1.mine_ref), channel_id=1, source_target_pairs={{0,1},{1,0},{2,3},{3,2},{4,5},{5,4},{6,7},{7,6},{8,9},{9,8},{10,11... | collective-permute-start | bytes 98312 | tf_op jit(solution)/shard_map/ppermute | solution.py:504

commit v6 on v5

--- a/solution.py
+++ b/solution.py
@@ -60,12 +60,19 @@
     return jnp.concatenate(parts, axis=1)
 
 
-def pair_blend(query, key, value, keep):
+def pair_scores(query, key):
     extent = key.shape[0]
     low = iota((extent, PAIR), 1) < HEAD
     zero = jnp.zeros((extent, PAIR), BF16)
+    keys = jnp.concatenate([jnp.where(low, key, zero), jnp.where(low, zero, key)], axis=0)
+    return dot_t(query, keys)
+
+
+def pair_mix(scores, value, keep):
+    extent = value.shape[0]
+    low = iota((extent, PAIR), 1) < HEAD
+    zero = jnp.zeros((extent, PAIR), BF16)
     one = jnp.ones((extent, PAIR), BF16)
-    keys = jnp.concatenate([jnp.where(low, key, zero), jnp.where(low, zero, key)], axis=0)
     values = jnp.concatenate(
         [
             jnp.concatenate([jnp.where(low, value, zero), jnp.where(low, one, zero)], axis=1),
@@ -73,11 +80,38 @@
         ],
         axis=0,
     )
-    weights = jnp.exp2(dot_t(query, keys))
+    weights = jnp.exp2(scores).astype(BF16)
     if keep is not None:
-        weights = jnp.where(keep, weights, 0.0)
-    mixed = dot(weights.astype(BF16), values)
+        weights = jnp.where(keep, weights, jnp.zeros_like(weights))
+    return dot(weights, values)
+
+
+def pair_done(mixed):
     return (mixed[:, :PAIR] / mixed[:, PAIR:]).astype(BF16)
+
+
+class Flat:
+    def __init__(self, ref):
+        self.ref = ref
+
+    def __getitem__(self, at):
+        down, across = at
+        extent = self.ref.shape[1]
+        part = self.ref[down.start // extent : down.stop // extent, :, across]
+        return part.reshape(down.stop - down.start, part.shape[-1])
+
+
+def blend_all(units, q_s, k_s, v_s, keep, put):
+    scores, mixes = {}, {}
+    for i in range(len(units) + 2):
+        if i < len(units):
+            d, a = units[i]
+            scores[i] = pair_scores(q_s[d, a], k_s[d, a])
+        if 0 <= i - 1 < len(units):
+            d, a = units[i - 1]
+            mixes[i - 1] = pair_mix(scores.pop(i - 1), v_s[d, a], keep)
+        if 0 <= i - 2:
+            put(units[i - 2], pair_done(mixes.pop(i - 2)))
 
 
 def fetch(pairs, sem):
@@ -95,11 +129,23 @@
     return [pltpu.with_memory_space_constraint(array, pltpu.HBM) for array in arrays]
 
 
-def qkv_all(normed, weight_s, copies, outs):
+def qkv_all(chunks, weight_s, copies, outs):
+    queue = []
+
+    def flush():
+        part, out, gain, at = queue.pop(0)
+        part = part.astype(BF16) if gain is None else unit_heads(part, gain)
+        out[at] = part.reshape(out[at].shape)
+
     for third, (out, gain) in enumerate(zip(outs, (SHARP * LOG2E, 1.0, None))):
         copies[third].wait()
-        part = dot(normed, weight_s[:, third * D : (third + 1) * D])
-        out[...] = part.astype(BF16) if gain is None else unit_heads(part, gain)
+        for at, rows in chunks:
+            part = dot(rows(third), weight_s[:, third * D : (third + 1) * D])
+            queue.append((part, out, gain, at))
+            if len(queue) > 1:
+                flush()
+    while queue:
+        flush()
 
 
 def space_kernel(
@@ -114,19 +160,30 @@
     for f in range(frames):
         video[f].wait()
         n_s[f * patches : (f + 1) * patches, :] = layer_norm(x_s[f])
-    qkv_all(n_s[...], qkv_s, weights, (q_s, k_s, v_s))
+    chunks = [
+        (slice(at, at + 128), lambda third, at=at: n_s[at : at + 128, :])
+        for at in range(0, frames * patches, 128)
+    ]
+    qkv_all(chunks, qkv_s, weights, (q_s, k_s, v_s))
     weights[3].wait()
+    units = [
+        (slice(f * patches, (f + 1) * patches), slice(pair * PAIR, (pair + 1) * PAIR))
+        for f in range(frames)
+        for pair in range(PAIRS)
+    ]
     stores = []
-    for f in range(frames):
-        down = slice(f * patches, (f + 1) * patches)
-        blended = []
-        for pair in range(PAIRS):
-            at = slice(pair * PAIR, (pair + 1) * PAIR)
-            blended.append(pair_blend(q_s[down, at], k_s[down, at], v_s[down, at], None))
-        update = dot(jnp.concatenate(blended, axis=1), w_s[...])
+
+    def put(unit, blended):
+        n_s[unit] = blended
+        if unit[1].stop < D:
+            return
+        f = unit[0].start // patches
+        update = dot(n_s[unit[0], :], w_s[...])
         y_s[f] = (x_s[f].astype(F32) + update).astype(BF16).reshape(y_s.shape[1:])
         stores.append(pltpu.make_async_copy(y_s.at[f], out_ref.at[:, f], out_sem.at[f]))
         stores[-1].start()
+
+    blend_all(units, q_s, k_s, v_s, None, put)
     for store in stores:
         store.wait()
 
@@ -178,20 +235,40 @@
         at = slice(tile * side, (tile + 1) * side)
         x_s[:, at, :] = tokens.reshape(side, side, D)
         n_s[:, at, :] = layer_norm(tokens).reshape(side, side, D)
-    qkv_all(n_s[...].reshape(rows, D), qkv_s, weights, (q_s, k_s, v_s))
+    chunks = [
+        (
+            (slice(at // frames, (at + 128) // frames), slice(None), slice(None)),
+            lambda third, at=at: n_s[at // frames : (at + 128) // frames].reshape(128, D),
+        )
+        for at in range(0, rows, 128)
+    ]
+    qkv_all(chunks, qkv_s, weights, (q_s, k_s, v_s))
     keep = iota((SUB, 2 * SUB), 0) // frames == (iota((SUB, 2 * SUB), 1) % SUB) // frames
-    for sub in range(rows // SUB):
-        down = slice(sub * SUB, (sub + 1) * SUB)
-        for pair in range(PAIRS):
-            at = slice(pair * PAIR, (pair + 1) * PAIR)
-            b_s[down, at] = pair_blend(q_s[down, at], k_s[down, at], v_s[down, at], keep)
     weights[3].wait()
     weights[4].wait()
-    update = dot(b_s[...], w_s[...])
-    mixed = (x_s[...].reshape(rows, D).astype(F32) + update).astype(BF16)
-    projected = dot(layer_norm(mixed), p_s[...])
-    norm = jnp.sum(projected * projected, axis=-1, keepdims=True)
-    kh_s[...] = (projected * lax.rsqrt(norm + 1e-06)).astype(BF16).reshape(kh_s.shape)
+
+    def finish(down):
+        groups = slice(down.start // frames, down.stop // frames)
+        tokens = x_s[groups].reshape(down.stop - down.start, D)
+        update = dot(b_s[down, :], w_s[...])
+        mixed = (tokens.astype(F32) + update).astype(BF16)
+        projected = dot(layer_norm(mixed), p_s[...])
+        norm = jnp.sum(projected * projected, axis=-1, keepdims=True)
+        unit = (projected * lax.rsqrt(norm + 1e-06)).astype(BF16)
+        kh_s[groups] = unit.reshape(kh_s[groups].shape)
+
+    def put(unit, blended):
+        b_s[unit] = blended
+        stop = unit[0].stop
+        if unit[1].stop == D and stop % 1024 == 0:
+            finish(slice(stop - 1024, stop))
+
+    units = [
+        (slice(at, at + SUB), slice(pair * PAIR, (pair + 1) * PAIR))
+        for at in range(0, rows, SUB)
+        for pair in range(PAIRS)
+    ]
+    blend_all(units, Flat(q_s), Flat(k_s), Flat(v_s), keep, put)
     for tile in range(rows // TILE):
         part = kh_s[:, tile * side : (tile + 1) * side, :].reshape(TILE, E)
         khat_ref[tile * TILE : (tile + 1) * TILE, :] = swap_rows(part, side)
@@ -212,7 +289,8 @@
             pltpu.VMEM((D, D), BF16),
             pltpu.VMEM((D, E), BF16),
         ]
-        + [pltpu.VMEM((rows, D), BF16)] * 4
+        + [pltpu.VMEM((patches, frames, D), BF16)] * 3
+        + [pltpu.VMEM((rows, D), BF16)]
         + [pltpu.VMEM((patches, frames, E), BF16), pltpu.SemaphoreType.DMA((5,))],
         compiler_params=limit(40),
         name="time",

time: 100 us -> 98.2 us (0.982)
  Pallas kernels: 35.9 us -> 33.9 us
    pallas_call x1, Pallas kernels: 13.2 us -> 12.1 us  [time(): pl.pallas_call(time_kernel, in_specs=[VMEM] + [HBM] * 3, out_specs=VMEM,...]
  transfers between devices with their start and end apart: 9 -> 9, of which waited for: 7 -> 7; matrix products, arithmetic and copies ran while one was open for 1% -> 1% of each run, Pallas kernels for 18% -> 17%
where the time goes in v6:
time: 98.2 us; the launch traced here: 97.9 us
  Pallas kernels  33.9 us (35%)
  waiting for transfers between devices  27.1 us (28%)
  starting transfers between devices  22.7 us (23%)
  blocking collectives  12.7 us (13%)
    pallas_call x1, Pallas kernels, space(): pl.pallas_call(space_kernel, in_specs=[HBM] * 3, out_specs=HBM, out_shape...  12.9 us
    all_to_all x1, blocking collectives, body(): lax.all_to_all(joined, 'seq', 0, 0, tiled=True, axis_index_groups=chips)  12.7 us
    all_to_all x1, waiting for transfers between devices, body(): items = lax.all_to_all(spatial, 'seq', 0, 0, tiled=True)  12.3 us
    pallas_call x1, Pallas kernels, time(): pl.pallas_call(time_kernel, in_specs=[VMEM] + [HBM] * 3, out_specs=VMEM,...  12.1 us
    all_to_all x1, starting transfers between devices, body(): items = lax.all_to_all(spatial, 'seq', 0, 0, tiled=True)  9.27 us
    all_to_all x1, waiting for transfers between devices, body(): lax.all_to_all(parts.reshape((-1,) + parts.shape[2:]), ('dp', 'seq'), 0,...  7.62 us
    all_to_all x1, starting transfers between devices, body(): lax.all_to_all(parts.reshape((-1,) + parts.shape[2:]), ('dp', 'seq'), 0,...  6.76 us
    ppermute x3, waiting for transfers between devices, body(): lax.ppermute(mine, 'dp', [(i, (i + by) % blocks) for i in range(blocks)])  5.92 us
  transfers between devices with their start and end apart: 9, of which 7 were waited for; matrix products, arithmetic and copies ran while one was open for 1% of the time, Pallas kernels for 17%

profile of v6, /device:TPU:1, one launch (start us, length us, event | category | flops | bytes accessed | tf_op | source)
XLA Modules:
  0.0 97.9 jit_solution(13749443022285462726)
XLA Ops:
  0.6 12.9 %space.1 = bf16[16,4,16,768]{3,2,1,0:T(8,128)(2,1)} custom-call(bf16[4,256,768]{2,1,0:T(8,128)(2,1)} %bitcast.15, bf16[768,2304]{1,0:T(8,128)(2,1)} %qkv_ref.2, bf16[768,768]{1,0:T(8,128)(2,1)} %out_w_ref.2), custom_call_target="tpu_custom_call" | custom-call | tf_op jit(solution)/shard_map/space/pallas_call | solution.py:194
  13.5 0.0 copy-start
  13.5 0.0 copy-start.1
  13.5 0.0 copy-start.2
  13.5 9.3 %all-to-all-start = ((bf16[16,4,16,768]{3,2,1,0:T(8,128)(2,1)}), bf16[16,4,16,768]{3,2,1,0:T(8,128)(2,1)S(1)}, u32[]{:S(2)}, u32[]{:S(2)}) async-start(bf16[16,4,16,768]{3,2,1,0:T(8,128)(2,1)} %space.1), calls=%async_computation | async-start | bytes 3145728 | tf_op jit(solution)/shard_map/all_to_all | solution.py:557
  22.8 0.7 pack_queries.1
  23.5 2.8 %collective-permute-start.2 = (bf16[272,128]{1,0:T(8,128)(2,1)S(1)}, bf16[272,128]{1,0:T(8,128)(2,1)S(1)}, u32[]{:S(2)}, u32[]{:S(2)}) collective-permute-start(bf16[272,128]{1,0:T(8,128)(2,1)S(1)} %pack_queries.1), channel_id=1, source_target_pairs={{0,96},{16,112},{32,0},{48,16},{64,32},{80,48},{96,64},{112,80},{1... | collective-permute-start | bytes 208904 | tf_op jit(solution)/shard_map/ppermute | solution.py:562
  26.3 0.3 collective-permute-start.1
  26.7 0.7 collective-permute-start
  27.4 0.3 collective-permute-done.2
  27.7 3.6 %collective-permute-done.1 = bf16[272,128]{1,0:T(8,128)(2,1)S(1)} collective-permute-done((bf16[272,128]{1,0:T(8,128)(2,1)S(1)}, bf16[272,128]{1,0:T(8,128)(2,1)S(1)}, u32[]{:S(2)}, u32[]{:S(2)}) %collective-permute-start.1) | collective-permute-done | bytes 69664 | tf_op jit(solution)/shard_map/ppermute | solution.py:562
  31.3 2.0 %collective-permute-done = bf16[272,128]{1,0:T(8,128)(2,1)S(1)} collective-permute-done((bf16[272,128]{1,0:T(8,128)(2,1)S(1)}, bf16[272,128]{1,0:T(8,128)(2,1)S(1)}, u32[]{:S(2)}, u32[]{:S(2)}) %collective-permute-start) | collective-permute-done | bytes 69664 | tf_op jit(solution)/shard_map/ppermute | solution.py:562
  33.4 12.3 %all-to-all-done = bf16[16,4,16,768]{3,2,1,0:T(8,128)(2,1)S(1)} async-done(((bf16[16,4,16,768]{3,2,1,0:T(8,128)(2,1)}), bf16[16,4,16,768]{3,2,1,0:T(8,128)(2,1)S(1)}, u32[]{:S(2)}, u32[]{:S(2)}) %all-to-all-start) | async-done | bytes 1572896 | tf_op jit(solution)/shard_map/all_to_all | solution.py:557
  45.6 0.7 collective-permute-start.3
  46.4 12.1 %time.1.refs_0_.refs_1_ = bf16[1024,128]{1,0:T(8,128)(2,1)S(1)} custom-call(bf16[1024,768]{1,0:T(8,128)(2,1)S(1)} %bitcast.11, bf16[768,2304]{1,0:T(8,128)(2,1)} %qkv_ref.3, bf16[768,768]{1,0:T(8,128)(2,1)} %out_w_ref.3, bf16[768,128]{1,0:T(8,128)(2,1)} %proj_ref.1), custom_call_target="tpu_custom_call" | custom-call | tf_op jit(solution)/shard_map/time/pallas_call | solution.py:280
  58.5 0.0 collective-permute-done.3.refs_2_.refs_3_
  58.5 2.7 %terms.1 = (f32[8,128,128]{2,1,0:T(8,128)S(1)}, bf16[8,128,128]{2,1,0:T(8,128)(2,1)S(1)}, f32[16,128]{1,0:T(8,128)S(1)}) custom-call(bf16[1024,128]{1,0:T(8,128)(2,1)S(1)} %time.1.refs_0_.refs_1_, bf16[4,272,128]{2,1,0:T(8,128)(2,1)S(1)} %pad_maximum_fusion.refs_1_.refs_2_, bf16[4,272,128]{2,1,0:T(8,128)(2,1)S(1)} %collective-permute-done.3.refs_2_.refs_3_), custom_call_target="tpu_custom_call" | custom-call | tf_op jit(solution)/shard_map/terms/pallas_call | solution.py:371
  61.2 1.2 %collective-permute-start.4 = (bf16[8,128,128]{2,1,0:T(8,128)(2,1)S(1)}, bf16[8,128,128]{2,1,0:T(8,128)(2,1)S(1)}, u32[]{:S(2)}, u32[]{:S(2)}) collective-permute-start(bf16[8,128,128]{2,1,0:T(8,128)(2,1)S(1)} %get-tuple-element.20), channel_id=1, source_target_pairs={{0,1},{1,0},{2,3},{3,2},{4,5},{5,4},{6,7},{7,6},{8,9},{9,8},{10,11... | collective-permute-start | bytes 786440 | tf_op jit(solution)/shard_map/ppermute | solution.py:571
  62.4 0.1 collective-permute-start.5
  62.5 1.1 %collective-permute-done.5.others_ref = f32[16,128]{1,0:T(8,128)S(1)} collective-permute-done((f32[16,128]{1,0:T(8,128)S(1)}, f32[16,128]{1,0:T(8,128)S(1)}, u32[]{:S(2)}, u32[]{:S(2)}) %collective-permute-start.5) | collective-permute-done | bytes 8224 | tf_op jit(solution)/shard_map/ppermute | solution.py:572
  63.6 0.0 collective-permute-done.4.got_ref
  63.6 0.1 join.1
  63.7 12.7 %all_to_all.15.refs_0_ = bf16[8,160,128]{2,1,0:T(8,128)(2,1)S(1)} all-to-all(bf16[8,160,128]{2,1,0:T(8,128)(2,1)S(1)} %join.1), channel_id=1, replica_groups={{0,2,4,6,8,10,12,14},{1,3,5,7,9,11,13,15},{16,18,20,22,24,26,28,30},{17..., dimensions={0} | all-to-all | bytes 655360 | tf_op jit(solution)/shard_map/all_to_all | solution.py:574
  76.4 1.2 %scales.1 = (bf16[8,16,8,128]{3,2,1,0:T(8,128)(2,1)}, f32[128,16]{1,0:T(8,128)S(1)}, f32[8,2,128]{2,1,0:T(2,128)S(1)}) custom-call(bf16[8,160,128]{2,1,0:T(8,128)(2,1)S(1)} %all_to_all.15.refs_0_, bf16[4,272,128]{2,1,0:T(8,128)(2,1)S(1)} %pad_maximum_fusion.refs_1_.refs_2_, bf16[4,272,128]{2,1,0:T(8,128)(2,1)S(1)} %collective-permute-done.3.refs_2_.refs_3_), custom_call_target="tpu_custom_call" | custom-call | tf_op jit(solution)/shard_map/scales/pallas_call | solution.py:463
  77.5 6.8 %all-to-all-start.2 = ((bf16[128,8,128]{2,1,0:T(8,128)(2,1)}), bf16[128,8,128]{2,1,0:T(8,128)(2,1)S(1)}, u32[]{:S(2)}, u32[]{:S(2)}) async-start(bf16[128,8,128]{2,1,0:T(8,128)(2,1)} %bitcast.7), calls=%async_computation.2 | async-start | bytes 524288 | tf_op jit(solution)/shard_map/all_to_all | solution.py:576
  84.3 3.7 %keys.1 = bf16[1024,128]{1,0:T(8,128)(2,1)} custom-call(f32[128,16]{1,0:T(8,128)S(1)} %get-tuple-element.23.refs_0_, bf16[1024,128]{1,0:T(8,128)(2,1)S(1)} %time.1.refs_0_.refs_1_, bf16[4,272,128]{2,1,0:T(8,128)(2,1)S(1)} %pad_maximum_fusion.refs_1_.refs_2_, bf16[4,272,128]{2,1,0:T(8,128)(2,1)S(1)} %collective-permute-done.3.refs_2_.refs_3_), custom_call_target="tpu_custom_call" | custom-call | tf_op jit(solution)/shard_map/keys/pallas_call | solution.py:495
  88.0 7.6 %all-to-all-done.2 = bf16[128,8,128]{2,1,0:T(8,128)(2,1)S(1)} async-done(((bf16[128,8,128]{2,1,0:T(8,128)(2,1)}), bf16[128,8,128]{2,1,0:T(8,128)(2,1)S(1)}, u32[]{:S(2)}, u32[]{:S(2)}) %all-to-all-start.2) | async-done | bytes 262176 | tf_op jit(solution)/shard_map/all_to_all | solution.py:576
  95.6 0.8 collective-permute-start.6
  96.4 0.1 slice.3
  96.5 0.6 reshape.33
  97.1 0.2 collective-permute-done.6.other_ref
  97.2 0.6 weave.1
  (5 shorter events, 0.1 us)
Async XLA Ops:
  13.5 9.3 %copy-start = (bf16[8,32,128]{2,1,0:T(8,128)(2,1)S(1)}, bf16[8,32,128]{2,1,0:T(8,128)(2,1)}, u32[]{:S(2)}) copy-start(bf16[8,32,128]{2,1,0:T(8,128)(2,1)} %param.15) | copy-start | bytes 196612
  13.5 9.3 %copy-start.1 = (s32[8]{0:T(128)S(1)}, s32[8]{0:T(128)}, u32[]{:S(2)}) copy-start(s32[8]{0:T(128)} %len_ref.1) | copy-start | bytes 100
  13.5 9.3 %copy-start.2 = (s32[8]{0:T(128)S(1)}, s32[8]{0:T(128)}, u32[]{:S(2)}) copy-start(s32[8]{0:T(128)} %pos_ref.1) | copy-start | bytes 100
  13.5 32.1 %all-to-all-start = ((bf16[16,4,16,768]{3,2,1,0:T(8,128)(2,1)}), bf16[16,4,16,768]{3,2,1,0:T(8,128)(2,1)S(1)}, u32[]{:S(2)}, u32[]{:S(2)}) async-start(bf16[16,4,16,768]{3,2,1,0:T(8,128)(2,1)} %space.1), calls=%async_computation | async-start | bytes 3145728 | tf_op jit(solution)/shard_map/all_to_all | solution.py:557
  23.5 4.2 %collective-permute-start.2 = (bf16[272,128]{1,0:T(8,128)(2,1)S(1)}, bf16[272,128]{1,0:T(8,128)(2,1)S(1)}, u32[]{:S(2)}, u32[]{:S(2)}) collective-permute-start(bf16[272,128]{1,0:T(8,128)(2,1)S(1)} %pack_queries.1), channel_id=1, source_target_pairs={{0,96},{16,112},{32,0},{48,16},{64,32},{80,48},{96,64},{112,80},{1... | collective-permute-start | bytes 208904 | tf_op jit(solution)/shard_map/ppermute | solution.py:562
  26.3 5.0 %collective-permute-start.1 = (bf16[272,128]{1,0:T(8,128)(2,1)S(1)}, bf16[272,128]{1,0:T(8,128)(2,1)S(1)}, u32[]{:S(2)}, u32[]{:S(2)}) collective-permute-start(bf16[272,128]{1,0:T(8,128)(2,1)S(1)} %pack_queries.1), channel_id=1, source_target_pairs={{0,64},{16,80},{32,96},{48,112},{64,0},{80,16},{96,32},{112,48},{1... | collective-permute-start | bytes 208904 | tf_op jit(solution)/shard_map/ppermute | solution.py:562
  26.7 6.6 %collective-permute-start = (bf16[272,128]{1,0:T(8,128)(2,1)S(1)}, bf16[272,128]{1,0:T(8,128)(2,1)S(1)}, u32[]{:S(2)}, u32[]{:S(2)}) collective-permute-start(bf16[272,128]{1,0:T(8,128)(2,1)S(1)} %pack_queries.1), channel_id=1, source_target_pairs={{0,32},{16,48},{32,64},{48,80},{64,96},{80,112},{96,0},{112,16},{1... | collective-permute-start | bytes 208904 | tf_op jit(solution)/shard_map/ppermute | solution.py:562
  45.6 12.8 %collective-permute-start.3 = (bf16[4,272,128]{2,1,0:T(8,128)(2,1)S(1)}, bf16[4,272,128]{2,1,0:T(8,128)(2,1)S(1)}, u32[]{:S(2)}, u32[]{:S(2)}) collective-permute-start(bf16[4,272,128]{2,1,0:T(8,128)(2,1)S(1)} %pad_maximum_fusion.refs_1_.refs_2_), channel_id=1, source_target_pairs={{0,16},{16,0},{32,48},{48,32},{64,80},{80,64},{96,112},{112,96},{1... | collective-permute-start | bytes 835592 | tf_op jit(solution)/shard_map/ppermute | solution.py:567
  61.2 2.4 %collective-permute-start.4 = (bf16[8,128,128]{2,1,0:T(8,128)(2,1)S(1)}, bf16[8,128,128]{2,1,0:T(8,128)(2,1)S(1)}, u32[]{:S(2)}, u32[]{:S(2)}) collective-permute-start(bf16[8,128,128]{2,1,0:T(8,128)(2,1)S(1)} %get-tuple-element.20), channel_id=1, source_target_pairs={{0,1},{1,0},{2,3},{3,2},{4,5},{5,4},{6,7},{7,6},{8,9},{9,8},{10,11... | collective-permute-start | bytes 786440 | tf_op jit(solution)/shard_map/ppermute | solution.py:571
  62.4 1.2 %collective-permute-start.5 = (f32[16,128]{1,0:T(8,128)S(1)}, f32[16,128]{1,0:T(8,128)S(1)}, u32[]{:S(2)}, u32[]{:S(2)}) collective-permute-start(f32[16,128]{1,0:T(8,128)S(1)} %get-tuple-element.21.sums_ref), channel_id=1, source_target_pairs={{0,1},{1,0},{2,3},{3,2},{4,5},{5,4},{6,7},{7,6},{8,9},{9,8},{10,11... | collective-permute-start | bytes 24584 | tf_op jit(solution)/shard_map/ppermute | solution.py:572
  77.5 18.0 %all-to-all-start.2 = ((bf16[128,8,128]{2,1,0:T(8,128)(2,1)}), bf16[128,8,128]{2,1,0:T(8,128)(2,1)S(1)}, u32[]{:S(2)}, u32[]{:S(2)}) async-start(bf16[128,8,128]{2,1,0:T(8,128)(2,1)} %bitcast.7), calls=%async_computation.2 | async-start | bytes 524288 | tf_op jit(solution)/shard_map/all_to_all | solution.py:576
  95.6 1.6 %collective-permute-start.6 = (bf16[16,8,128]{2,1,0:T(8,128)(2,1)S(1)}, bf16[16,8,128]{2,1,0:T(8,128)(2,1)S(1)}, u32[]{:S(2)}, u32[]{:S(2)}) collective-permute-start(bf16[16,8,128]{2,1,0:T(8,128)(2,1)S(1)} %totals.1.mine_ref), channel_id=1, source_target_pairs={{0,1},{1,0},{2,3},{3,2},{4,5},{5,4},{6,7},{7,6},{8,9},{9,8},{10,11... | collective-permute-start | bytes 98312 | tf_op jit(solution)/shard_map/ppermute | solution.py:582

commit v7 on v6

--- a/solution.py
+++ b/solution.py
@@ -247,21 +247,8 @@
     weights[3].wait()
     weights[4].wait()
 
-    def finish(down):
-        groups = slice(down.start // frames, down.stop // frames)
-        tokens = x_s[groups].reshape(down.stop - down.start, D)
-        update = dot(b_s[down, :], w_s[...])
-        mixed = (tokens.astype(F32) + update).astype(BF16)
-        projected = dot(layer_norm(mixed), p_s[...])
-        norm = jnp.sum(projected * projected, axis=-1, keepdims=True)
-        unit = (projected * lax.rsqrt(norm + 1e-06)).astype(BF16)
-        kh_s[groups] = unit.reshape(kh_s[groups].shape)
-
     def put(unit, blended):
         b_s[unit] = blended
-        stop = unit[0].stop
-        if unit[1].stop == D and stop % 1024 == 0:
-            finish(slice(stop - 1024, stop))
 
     units = [
         (slice(at, at + SUB), slice(pair * PAIR, (pair + 1) * PAIR))
@@ -269,6 +256,22 @@
         for pair in range(PAIRS)
     ]
     blend_all(units, Flat(q_s), Flat(k_s), Flat(v_s), keep, put)
+    ahead = []
+
+    def mixed(groups, update):
+        tokens = x_s[groups].reshape(update.shape)
+        normed = layer_norm((tokens.astype(F32) + update).astype(BF16))
+        projected = dot(normed, p_s[...])
+        norm = jnp.sum(projected * projected, axis=-1, keepdims=True)
+        unit = (projected * lax.rsqrt(norm + 1e-06)).astype(BF16)
+        kh_s[groups] = unit.reshape(kh_s[groups].shape)
+
+    for at in range(0, rows, 256):
+        groups = slice(at // frames, (at + 256) // frames)
+        ahead.append((groups, dot(b_s[at : at + 256, :], w_s[...])))
+        if len(ahead) > 1:
+            mixed(*ahead.pop(0))
+    mixed(*ahead.pop(0))
     for tile in range(rows // TILE):
         part = kh_s[:, tile * side : (tile + 1) * side, :].reshape(TILE, E)
         khat_ref[tile * TILE : (tile + 1) * TILE, :] = swap_rows(part, side)
@@ -342,9 +345,18 @@
     return packed_refs[side].at[step]
 
 
-def expo_terms(query, khat):
+def expo_of(dots):
     gain = LOG2E / TEMPER
-    return jnp.exp2(dot_t(query, khat) * gain - gain).astype(BF16)
+    return jnp.exp2(dots * gain - gain).astype(BF16)
+
+
+def dots_ahead(packed_refs, blocks, rows, khat):
+    ahead = []
+    for block in range(blocks):
+        ahead.append(dot_t(block_of(packed_refs, block)[:rows, :], khat))
+        if block > 0:
+            yield block - 1, ahead.pop(0)
+    yield blocks - 1, ahead.pop(0)
 
 
 def terms_kernel(blocks, khat_ref, *refs):
@@ -355,8 +367,8 @@
     wide = jnp.concatenate([khat, jnp.ones_like(khat)], axis=1)
     eye = iota((E, E), 0) == iota((E, E), 1)
     sums = []
-    for block in range(blocks):
-        both = dot(expo_terms(block_of(packed_refs, block)[:rows, :], khat), wide)
+    for block, dots in dots_ahead(packed_refs, blocks, rows, khat):
+        both = dot(expo_of(dots), wide)
         low, high = both[:E, :E], both[E:, :E]
         keep_ref[block] = jnp.where(first, low, high)
         send_ref[block] = jnp.where(first, high, low).astype(BF16)
@@ -480,14 +492,14 @@
     rows = packed_refs[0].shape[1] - EXTRA
     per = rows // E
     total = jnp.zeros((E, khat.shape[0]), F32)
-    for block in range(blocks):
+    for block, dots in dots_ahead(packed_refs, blocks, rows, khat):
         query = block_of(packed_refs, block)[:rows, :]
         parts = []
         for part in range(per):
             at = block * per + part
             scaled = query[part * E : (part + 1) * E].astype(F32) * scale_ref[:, at : at + 1]
             parts.append(scaled.T.astype(BF16))
-        total = total + dot(jnp.concatenate(parts, axis=1), expo_terms(query, khat))
+        total = total + dot(jnp.concatenate(parts, axis=1), expo_of(dots))
     out_ref[...] = (total.T * gain).astype(BF16)
 
 

time: 98.2 us -> 97.4 us (level)
  Pallas kernels: 33.9 us -> 32.4 us
  transfers between devices with their start and end apart: 9 -> 9, of which waited for: 7 -> 7; matrix products, arithmetic and copies ran while one was open for 1% -> 1% of each run, Pallas kernels for 17% -> 15%
where the time goes in v7:
time: 97.4 us; the launch traced here: 97.1 us
  Pallas kernels  32.4 us (33%)
  waiting for transfers between devices  27.8 us (29%)
  starting transfers between devices  22.7 us (23%)
  blocking collectives  12.7 us (13%)
    pallas_call x1, Pallas kernels, space(): pl.pallas_call(space_kernel, in_specs=[HBM] * 3, out_specs=HBM, out_shape...  12.9 us
    all_to_all x1, blocking collectives, body(): lax.all_to_all(joined, 'seq', 0, 0, tiled=True, axis_index_groups=chips)  12.7 us
    all_to_all x1, waiting for transfers between devices, body(): items = lax.all_to_all(spatial, 'seq', 0, 0, tiled=True)  12.3 us
    pallas_call x1, Pallas kernels, time(): pl.pallas_call(time_kernel, in_specs=[VMEM] + [HBM] * 3, out_specs=VMEM,...  11.4 us
    all_to_all x1, starting transfers between devices, body(): items = lax.all_to_all(spatial, 'seq', 0, 0, tiled=True)  9.27 us
    all_to_all x1, waiting for transfers between devices, body(): lax.all_to_all(parts.reshape((-1,) + parts.shape[2:]), ('dp', 'seq'), 0,...  8.39 us
    all_to_all x1, starting transfers between devices, body(): lax.all_to_all(parts.reshape((-1,) + parts.shape[2:]), ('dp', 'seq'), 0,...  6.75 us
    ppermute x3, waiting for transfers between devices, body(): lax.ppermute(mine, 'dp', [(i, (i + by) % blocks) for i in range(blocks)])  5.92 us
  transfers between devices with their start and end apart: 9, of which 7 were waited for; matrix products, arithmetic and copies ran while one was open for 1% of the time, Pallas kernels for 15%

profile of v7, /device:TPU:1, one launch (start us, length us, event | category | flops | bytes accessed | tf_op | source)
XLA Modules:
  0.0 97.1 jit_solution(12038433416875872669)
XLA Ops:
  0.6 12.9 %space.1 = bf16[16,4,16,768]{3,2,1,0:T(8,128)(2,1)} custom-call(bf16[4,256,768]{2,1,0:T(8,128)(2,1)} %bitcast.15, bf16[768,2304]{1,0:T(8,128)(2,1)} %qkv_ref.2, bf16[768,768]{1,0:T(8,128)(2,1)} %out_w_ref.2), custom_call_target="tpu_custom_call" | custom-call | tf_op jit(solution)/shard_map/space/pallas_call | solution.py:194
  13.5 0.0 copy-start
  13.5 0.0 copy-start.1
  13.5 0.0 copy-start.2
  13.5 9.3 %all-to-all-start = ((bf16[16,4,16,768]{3,2,1,0:T(8,128)(2,1)}), bf16[16,4,16,768]{3,2,1,0:T(8,128)(2,1)S(1)}, u32[]{:S(2)}, u32[]{:S(2)}) async-start(bf16[16,4,16,768]{3,2,1,0:T(8,128)(2,1)} %space.1), calls=%async_computation | async-start | bytes 3145728 | tf_op jit(solution)/shard_map/all_to_all | solution.py:569
  22.8 0.7 pack_queries.1
  23.5 2.8 %collective-permute-start.2 = (bf16[272,128]{1,0:T(8,128)(2,1)S(1)}, bf16[272,128]{1,0:T(8,128)(2,1)S(1)}, u32[]{:S(2)}, u32[]{:S(2)}) collective-permute-start(bf16[272,128]{1,0:T(8,128)(2,1)S(1)} %pack_queries.1), channel_id=1, source_target_pairs={{0,96},{16,112},{32,0},{48,16},{64,32},{80,48},{96,64},{112,80},{1... | collective-permute-start | bytes 208904 | tf_op jit(solution)/shard_map/ppermute | solution.py:574
  26.3 0.3 collective-permute-start.1
  26.7 0.7 collective-permute-start
  27.4 0.3 collective-permute-done.2
  27.7 3.6 %collective-permute-done.1 = bf16[272,128]{1,0:T(8,128)(2,1)S(1)} collective-permute-done((bf16[272,128]{1,0:T(8,128)(2,1)S(1)}, bf16[272,128]{1,0:T(8,128)(2,1)S(1)}, u32[]{:S(2)}, u32[]{:S(2)}) %collective-permute-start.1) | collective-permute-done | bytes 69664 | tf_op jit(solution)/shard_map/ppermute | solution.py:574
  31.3 2.0 %collective-permute-done = bf16[272,128]{1,0:T(8,128)(2,1)S(1)} collective-permute-done((bf16[272,128]{1,0:T(8,128)(2,1)S(1)}, bf16[272,128]{1,0:T(8,128)(2,1)S(1)}, u32[]{:S(2)}, u32[]{:S(2)}) %collective-permute-start) | collective-permute-done | bytes 69664 | tf_op jit(solution)/shard_map/ppermute | solution.py:574
  33.4 12.3 %all-to-all-done = bf16[16,4,16,768]{3,2,1,0:T(8,128)(2,1)S(1)} async-done(((bf16[16,4,16,768]{3,2,1,0:T(8,128)(2,1)}), bf16[16,4,16,768]{3,2,1,0:T(8,128)(2,1)S(1)}, u32[]{:S(2)}, u32[]{:S(2)}) %all-to-all-start) | async-done | bytes 1572896 | tf_op jit(solution)/shard_map/all_to_all | solution.py:569
  45.6 0.7 collective-permute-start.3
  46.4 11.4 %time.1.refs_0_.refs_1_ = bf16[1024,128]{1,0:T(8,128)(2,1)S(1)} custom-call(bf16[1024,768]{1,0:T(8,128)(2,1)S(1)} %bitcast.11, bf16[768,2304]{1,0:T(8,128)(2,1)} %qkv_ref.3, bf16[768,768]{1,0:T(8,128)(2,1)} %out_w_ref.3, bf16[768,128]{1,0:T(8,128)(2,1)} %proj_ref.1), custom_call_target="tpu_custom_call" | custom-call | tf_op jit(solution)/shard_map/time/pallas_call | solution.py:283
  57.8 0.0 collective-permute-done.3.refs_2_.refs_3_
  57.8 2.6 %terms.1 = (f32[8,128,128]{2,1,0:T(8,128)S(1)}, bf16[8,128,128]{2,1,0:T(8,128)(2,1)S(1)}, f32[16,128]{1,0:T(8,128)S(1)}) custom-call(bf16[1024,128]{1,0:T(8,128)(2,1)S(1)} %time.1.refs_0_.refs_1_, bf16[4,272,128]{2,1,0:T(8,128)(2,1)S(1)} %pad_maximum_fusion.refs_1_.refs_2_, bf16[4,272,128]{2,1,0:T(8,128)(2,1)S(1)} %collective-permute-done.3.refs_2_.refs_3_), custom_call_target="tpu_custom_call" | custom-call | tf_op jit(solution)/shard_map/terms/pallas_call | solution.py:383
  60.5 1.2 %collective-permute-start.4 = (bf16[8,128,128]{2,1,0:T(8,128)(2,1)S(1)}, bf16[8,128,128]{2,1,0:T(8,128)(2,1)S(1)}, u32[]{:S(2)}, u32[]{:S(2)}) collective-permute-start(bf16[8,128,128]{2,1,0:T(8,128)(2,1)S(1)} %get-tuple-element.20), channel_id=1, source_target_pairs={{0,1},{1,0},{2,3},{3,2},{4,5},{5,4},{6,7},{7,6},{8,9},{9,8},{10,11... | collective-permute-start | bytes 786440 | tf_op jit(solution)/shard_map/ppermute | solution.py:583
  61.7 0.1 collective-permute-start.5
  61.8 1.1 %collective-permute-done.5.others_ref = f32[16,128]{1,0:T(8,128)S(1)} collective-permute-done((f32[16,128]{1,0:T(8,128)S(1)}, f32[16,128]{1,0:T(8,128)S(1)}, u32[]{:S(2)}, u32[]{:S(2)}) %collective-permute-start.5) | collective-permute-done | bytes 8224 | tf_op jit(solution)/shard_map/ppermute | solution.py:584
  62.9 0.0 collective-permute-done.4.got_ref
  62.9 0.1 join.1
  62.9 12.7 %all_to_all.15.refs_0_ = bf16[8,160,128]{2,1,0:T(8,128)(2,1)S(1)} all-to-all(bf16[8,160,128]{2,1,0:T(8,128)(2,1)S(1)} %join.1), channel_id=1, replica_groups={{0,2,4,6,8,10,12,14},{1,3,5,7,9,11,13,15},{16,18,20,22,24,26,28,30},{17..., dimensions={0} | all-to-all | bytes 655360 | tf_op jit(solution)/shard_map/all_to_all | solution.py:586
  75.6 1.2 %scales.1 = (bf16[8,16,8,128]{3,2,1,0:T(8,128)(2,1)}, f32[128,16]{1,0:T(8,128)S(1)}, f32[8,2,128]{2,1,0:T(2,128)S(1)}) custom-call(bf16[8,160,128]{2,1,0:T(8,128)(2,1)S(1)} %all_to_all.15.refs_0_, bf16[4,272,128]{2,1,0:T(8,128)(2,1)S(1)} %pad_maximum_fusion.refs_1_.refs_2_, bf16[4,272,128]{2,1,0:T(8,128)(2,1)S(1)} %collective-permute-done.3.refs_2_.refs_3_), custom_call_target="tpu_custom_call" | custom-call | tf_op jit(solution)/shard_map/scales/pallas_call | solution.py:475
  76.8 6.7 %all-to-all-start.2 = ((bf16[128,8,128]{2,1,0:T(8,128)(2,1)}), bf16[128,8,128]{2,1,0:T(8,128)(2,1)S(1)}, u32[]{:S(2)}, u32[]{:S(2)}) async-start(bf16[128,8,128]{2,1,0:T(8,128)(2,1)} %bitcast.7), calls=%async_computation.2 | async-start | bytes 524288 | tf_op jit(solution)/shard_map/all_to_all | solution.py:588
  83.6 2.9 %keys.1 = bf16[1024,128]{1,0:T(8,128)(2,1)} custom-call(f32[128,16]{1,0:T(8,128)S(1)} %get-tuple-element.23.refs_0_, bf16[1024,128]{1,0:T(8,128)(2,1)S(1)} %time.1.refs_0_.refs_1_, bf16[4,272,128]{2,1,0:T(8,128)(2,1)S(1)} %pad_maximum_fusion.refs_1_.refs_2_, bf16[4,272,128]{2,1,0:T(8,128)(2,1)S(1)} %collective-permute-done.3.refs_2_.refs_3_), custom_call_target="tpu_custom_call" | custom-call | tf_op jit(solution)/shard_map/keys/pallas_call | solution.py:507
  86.4 8.4 %all-to-all-done.2 = bf16[128,8,128]{2,1,0:T(8,128)(2,1)S(1)} async-done(((bf16[128,8,128]{2,1,0:T(8,128)(2,1)}), bf16[128,8,128]{2,1,0:T(8,128)(2,1)S(1)}, u32[]{:S(2)}, u32[]{:S(2)}) %all-to-all-start.2) | async-done | bytes 262176 | tf_op jit(solution)/shard_map/all_to_all | solution.py:588
  94.9 0.8 collective-permute-start.6
  95.6 0.1 slice.3
  95.7 0.6 reshape.33
  96.3 0.2 collective-permute-done.6.other_ref
  96.5 0.6 weave.1
  (5 shorter events, 0.1 us)
Async XLA Ops:
  13.5 9.3 %copy-start = (bf16[8,32,128]{2,1,0:T(8,128)(2,1)S(1)}, bf16[8,32,128]{2,1,0:T(8,128)(2,1)}, u32[]{:S(2)}) copy-start(bf16[8,32,128]{2,1,0:T(8,128)(2,1)} %param.15) | copy-start | bytes 196612
  13.5 9.3 %copy-start.1 = (s32[8]{0:T(128)S(1)}, s32[8]{0:T(128)}, u32[]{:S(2)}) copy-start(s32[8]{0:T(128)} %len_ref.1) | copy-start | bytes 100
  13.5 9.3 %copy-start.2 = (s32[8]{0:T(128)S(1)}, s32[8]{0:T(128)}, u32[]{:S(2)}) copy-start(s32[8]{0:T(128)} %pos_ref.1) | copy-start | bytes 100
  13.5 32.1 %all-to-all-start = ((bf16[16,4,16,768]{3,2,1,0:T(8,128)(2,1)}), bf16[16,4,16,768]{3,2,1,0:T(8,128)(2,1)S(1)}, u32[]{:S(2)}, u32[]{:S(2)}) async-start(bf16[16,4,16,768]{3,2,1,0:T(8,128)(2,1)} %space.1), calls=%async_computation | async-start | bytes 3145728 | tf_op jit(solution)/shard_map/all_to_all | solution.py:569
  23.5 4.2 %collective-permute-start.2 = (bf16[272,128]{1,0:T(8,128)(2,1)S(1)}, bf16[272,128]{1,0:T(8,128)(2,1)S(1)}, u32[]{:S(2)}, u32[]{:S(2)}) collective-permute-start(bf16[272,128]{1,0:T(8,128)(2,1)S(1)} %pack_queries.1), channel_id=1, source_target_pairs={{0,96},{16,112},{32,0},{48,16},{64,32},{80,48},{96,64},{112,80},{1... | collective-permute-start | bytes 208904 | tf_op jit(solution)/shard_map/ppermute | solution.py:574
  26.3 5.0 %collective-permute-start.1 = (bf16[272,128]{1,0:T(8,128)(2,1)S(1)}, bf16[272,128]{1,0:T(8,128)(2,1)S(1)}, u32[]{:S(2)}, u32[]{:S(2)}) collective-permute-start(bf16[272,128]{1,0:T(8,128)(2,1)S(1)} %pack_queries.1), channel_id=1, source_target_pairs={{0,64},{16,80},{32,96},{48,112},{64,0},{80,16},{96,32},{112,48},{1... | collective-permute-start | bytes 208904 | tf_op jit(solution)/shard_map/ppermute | solution.py:574
  26.7 6.6 %collective-permute-start = (bf16[272,128]{1,0:T(8,128)(2,1)S(1)}, bf16[272,128]{1,0:T(8,128)(2,1)S(1)}, u32[]{:S(2)}, u32[]{:S(2)}) collective-permute-start(bf16[272,128]{1,0:T(8,128)(2,1)S(1)} %pack_queries.1), channel_id=1, source_target_pairs={{0,32},{16,48},{32,64},{48,80},{64,96},{80,112},{96,0},{112,16},{1... | collective-permute-start | bytes 208904 | tf_op jit(solution)/shard_map/ppermute | solution.py:574
  45.6 12.2 %collective-permute-start.3 = (bf16[4,272,128]{2,1,0:T(8,128)(2,1)S(1)}, bf16[4,272,128]{2,1,0:T(8,128)(2,1)S(1)}, u32[]{:S(2)}, u32[]{:S(2)}) collective-permute-start(bf16[4,272,128]{2,1,0:T(8,128)(2,1)S(1)} %pad_maximum_fusion.refs_1_.refs_2_), channel_id=1, source_target_pairs={{0,16},{16,0},{32,48},{48,32},{64,80},{80,64},{96,112},{112,96},{1... | collective-permute-start | bytes 835592 | tf_op jit(solution)/shard_map/ppermute | solution.py:579
  60.5 2.4 %collective-permute-start.4 = (bf16[8,128,128]{2,1,0:T(8,128)(2,1)S(1)}, bf16[8,128,128]{2,1,0:T(8,128)(2,1)S(1)}, u32[]{:S(2)}, u32[]{:S(2)}) collective-permute-start(bf16[8,128,128]{2,1,0:T(8,128)(2,1)S(1)} %get-tuple-element.20), channel_id=1, source_target_pairs={{0,1},{1,0},{2,3},{3,2},{4,5},{5,4},{6,7},{7,6},{8,9},{9,8},{10,11... | collective-permute-start | bytes 786440 | tf_op jit(solution)/shard_map/ppermute | solution.py:583
  61.7 1.2 %collective-permute-start.5 = (f32[16,128]{1,0:T(8,128)S(1)}, f32[16,128]{1,0:T(8,128)S(1)}, u32[]{:S(2)}, u32[]{:S(2)}) collective-permute-start(f32[16,128]{1,0:T(8,128)S(1)} %get-tuple-element.21.sums_ref), channel_id=1, source_target_pairs={{0,1},{1,0},{2,3},{3,2},{4,5},{5,4},{6,7},{7,6},{8,9},{9,8},{10,11... | collective-permute-start | bytes 24584 | tf_op jit(solution)/shard_map/ppermute | solution.py:584
  76.8 18.0 %all-to-all-start.2 = ((bf16[128,8,128]{2,1,0:T(8,128)(2,1)}), bf16[128,8,128]{2,1,0:T(8,128)(2,1)S(1)}, u32[]{:S(2)}, u32[]{:S(2)}) async-start(bf16[128,8,128]{2,1,0:T(8,128)(2,1)} %bitcast.7), calls=%async_computation.2 | async-start | bytes 524288 | tf_op jit(solution)/shard_map/all_to_all | solution.py:588
  94.9 1.6 %collective-permute-start.6 = (bf16[16,8,128]{2,1,0:T(8,128)(2,1)S(1)}, bf16[16,8,128]{2,1,0:T(8,128)(2,1)S(1)}, u32[]{:S(2)}, u32[]{:S(2)}) collective-permute-start(bf16[16,8,128]{2,1,0:T(8,128)(2,1)S(1)} %totals.1.mine_ref), channel_id=1, source_target_pairs={{0,1},{1,0},{2,3},{3,2},{4,5},{5,4},{6,7},{7,6},{8,9},{9,8},{10,11... | collective-permute-start | bytes 98312 | tf_op jit(solution)/shard_map/ppermute | solution.py:594

commit v8 on v7

--- a/solution.py
+++ b/solution.py
@@ -103,15 +103,15 @@
 
 def blend_all(units, q_s, k_s, v_s, keep, put):
     scores, mixes = {}, {}
-    for i in range(len(units) + 2):
+    for i in range(len(units) + 3):
         if i < len(units):
             d, a = units[i]
             scores[i] = pair_scores(q_s[d, a], k_s[d, a])
-        if 0 <= i - 1 < len(units):
-            d, a = units[i - 1]
-            mixes[i - 1] = pair_mix(scores.pop(i - 1), v_s[d, a], keep)
-        if 0 <= i - 2:
-            put(units[i - 2], pair_done(mixes.pop(i - 2)))
+        if 0 <= i - 2 < len(units):
+            d, a = units[i - 2]
+            mixes[i - 2] = pair_mix(scores.pop(i - 2), v_s[d, a], keep)
+        if 0 <= i - 3:
+            put(units[i - 3], pair_done(mixes.pop(i - 3)))
 
 
 def fetch(pairs, sem):

time: 97.4 us -> 97.5 us (level)
  no operation moved by 1% of the time
where the time goes in v8:
time: 97.5 us; the launch traced here: 97.2 us
  Pallas kernels  32.4 us (33%)
  waiting for transfers between devices  27.8 us (29%)
  starting transfers between devices  22.7 us (23%)
  blocking collectives  12.7 us (13%)
    pallas_call x1, Pallas kernels, space(): pl.pallas_call(space_kernel, in_specs=[HBM] * 3, out_specs=HBM, out_shape...  13 us
    all_to_all x1, blocking collectives, body(): lax.all_to_all(joined, 'seq', 0, 0, tiled=True, axis_index_groups=chips)  12.7 us
    all_to_all x1, waiting for transfers between devices, body(): items = lax.all_to_all(spatial, 'seq', 0, 0, tiled=True)  12.3 us
    pallas_call x1, Pallas kernels, time(): pl.pallas_call(time_kernel, in_specs=[VMEM] + [HBM] * 3, out_specs=VMEM,...  11.3 us
    all_to_all x1, starting transfers between devices, body(): items = lax.all_to_all(spatial, 'seq', 0, 0, tiled=True)  9.28 us
    all_to_all x1, waiting for transfers between devices, body(): lax.all_to_all(parts.reshape((-1,) + parts.shape[2:]), ('dp', 'seq'), 0,...  8.39 us
    all_to_all x1, starting transfers between devices, body(): lax.all_to_all(parts.reshape((-1,) + parts.shape[2:]), ('dp', 'seq'), 0,...  6.74 us
    ppermute x3, waiting for transfers between devices, body(): lax.ppermute(mine, 'dp', [(i, (i + by) % blocks) for i in range(blocks)])  5.92 us
  transfers between devices with their start and end apart: 9, of which 7 were waited for; matrix products, arithmetic and copies ran while one was open for 1% of the time, Pallas kernels for 15%

profile of v8, /device:TPU:1, one launch (start us, length us, event | category | flops | bytes accessed | tf_op | source)
XLA Modules:
  0.0 97.2 jit_solution(10823083740808147735)
XLA Ops:
  0.6 13.0 %space.1 = bf16[16,4,16,768]{3,2,1,0:T(8,128)(2,1)} custom-call(bf16[4,256,768]{2,1,0:T(8,128)(2,1)} %bitcast.15, bf16[768,2304]{1,0:T(8,128)(2,1)} %qkv_ref.2, bf16[768,768]{1,0:T(8,128)(2,1)} %out_w_ref.2), custom_call_target="tpu_custom_call" | custom-call | tf_op jit(solution)/shard_map/space/pallas_call | solution.py:194
  13.6 0.0 copy-start
  13.7 0.0 copy-start.1
  13.7 0.0 copy-start.2
  13.7 9.3 %all-to-all-start = ((bf16[16,4,16,768]{3,2,1,0:T(8,128)(2,1)}), bf16[16,4,16,768]{3,2,1,0:T(8,128)(2,1)S(1)}, u32[]{:S(2)}, u32[]{:S(2)}) async-start(bf16[16,4,16,768]{3,2,1,0:T(8,128)(2,1)} %space.1), calls=%async_computation | async-start | bytes 3145728 | tf_op jit(solution)/shard_map/all_to_all | solution.py:569
  23.0 0.7 pack_queries.1
  23.7 2.8 %collective-permute-start.2 = (bf16[272,128]{1,0:T(8,128)(2,1)S(1)}, bf16[272,128]{1,0:T(8,128)(2,1)S(1)}, u32[]{:S(2)}, u32[]{:S(2)}) collective-permute-start(bf16[272,128]{1,0:T(8,128)(2,1)S(1)} %pack_queries.1), channel_id=1, source_target_pairs={{0,96},{16,112},{32,0},{48,16},{64,32},{80,48},{96,64},{112,80},{1... | collective-permute-start | bytes 208904 | tf_op jit(solution)/shard_map/ppermute | solution.py:574
  26.5 0.4 collective-permute-start.1
  26.8 0.7 collective-permute-start
  27.5 0.3 collective-permute-done.2
  27.9 3.6 %collective-permute-done.1 = bf16[272,128]{1,0:T(8,128)(2,1)S(1)} collective-permute-done((bf16[272,128]{1,0:T(8,128)(2,1)S(1)}, bf16[272,128]{1,0:T(8,128)(2,1)S(1)}, u32[]{:S(2)}, u32[]{:S(2)}) %collective-permute-start.1) | collective-permute-done | bytes 69664 | tf_op jit(solution)/shard_map/ppermute | solution.py:574
  31.4 2.0 %collective-permute-done = bf16[272,128]{1,0:T(8,128)(2,1)S(1)} collective-permute-done((bf16[272,128]{1,0:T(8,128)(2,1)S(1)}, bf16[272,128]{1,0:T(8,128)(2,1)S(1)}, u32[]{:S(2)}, u32[]{:S(2)}) %collective-permute-start) | collective-permute-done | bytes 69664 | tf_op jit(solution)/shard_map/ppermute | solution.py:574
  33.5 12.3 %all-to-all-done = bf16[16,4,16,768]{3,2,1,0:T(8,128)(2,1)S(1)} async-done(((bf16[16,4,16,768]{3,2,1,0:T(8,128)(2,1)}), bf16[16,4,16,768]{3,2,1,0:T(8,128)(2,1)S(1)}, u32[]{:S(2)}, u32[]{:S(2)}) %all-to-all-start) | async-done | bytes 1572896 | tf_op jit(solution)/shard_map/all_to_all | solution.py:569
  45.8 0.7 collective-permute-start.3
  46.5 11.3 %time.1.refs_0_.refs_1_ = bf16[1024,128]{1,0:T(8,128)(2,1)S(1)} custom-call(bf16[1024,768]{1,0:T(8,128)(2,1)S(1)} %bitcast.11, bf16[768,2304]{1,0:T(8,128)(2,1)} %qkv_ref.3, bf16[768,768]{1,0:T(8,128)(2,1)} %out_w_ref.3, bf16[768,128]{1,0:T(8,128)(2,1)} %proj_ref.1), custom_call_target="tpu_custom_call" | custom-call | tf_op jit(solution)/shard_map/time/pallas_call | solution.py:283
  57.9 0.0 collective-permute-done.3.refs_2_.refs_3_
  57.9 2.6 %terms.1 = (f32[8,128,128]{2,1,0:T(8,128)S(1)}, bf16[8,128,128]{2,1,0:T(8,128)(2,1)S(1)}, f32[16,128]{1,0:T(8,128)S(1)}) custom-call(bf16[1024,128]{1,0:T(8,128)(2,1)S(1)} %time.1.refs_0_.refs_1_, bf16[4,272,128]{2,1,0:T(8,128)(2,1)S(1)} %pad_maximum_fusion.refs_1_.refs_2_, bf16[4,272,128]{2,1,0:T(8,128)(2,1)S(1)} %collective-permute-done.3.refs_2_.refs_3_), custom_call_target="tpu_custom_call" | custom-call | tf_op jit(solution)/shard_map/terms/pallas_call | solution.py:383
  60.5 1.2 %collective-permute-start.4 = (bf16[8,128,128]{2,1,0:T(8,128)(2,1)S(1)}, bf16[8,128,128]{2,1,0:T(8,128)(2,1)S(1)}, u32[]{:S(2)}, u32[]{:S(2)}) collective-permute-start(bf16[8,128,128]{2,1,0:T(8,128)(2,1)S(1)} %get-tuple-element.20), channel_id=1, source_target_pairs={{0,1},{1,0},{2,3},{3,2},{4,5},{5,4},{6,7},{7,6},{8,9},{9,8},{10,11... | collective-permute-start | bytes 786440 | tf_op jit(solution)/shard_map/ppermute | solution.py:583
  61.7 0.1 collective-permute-start.5
  61.8 1.1 %collective-permute-done.5.others_ref = f32[16,128]{1,0:T(8,128)S(1)} collective-permute-done((f32[16,128]{1,0:T(8,128)S(1)}, f32[16,128]{1,0:T(8,128)S(1)}, u32[]{:S(2)}, u32[]{:S(2)}) %collective-permute-start.5) | collective-permute-done | bytes 8224 | tf_op jit(solution)/shard_map/ppermute | solution.py:584
  62.9 0.0 collective-permute-done.4.got_ref
  62.9 0.1 join.1
  63.0 12.7 %all_to_all.15.refs_0_ = bf16[8,160,128]{2,1,0:T(8,128)(2,1)S(1)} all-to-all(bf16[8,160,128]{2,1,0:T(8,128)(2,1)S(1)} %join.1), channel_id=1, replica_groups={{0,2,4,6,8,10,12,14},{1,3,5,7,9,11,13,15},{16,18,20,22,24,26,28,30},{17..., dimensions={0} | all-to-all | bytes 655360 | tf_op jit(solution)/shard_map/all_to_all | solution.py:586
  75.7 1.2 %scales.1 = (bf16[8,16,8,128]{3,2,1,0:T(8,128)(2,1)}, f32[128,16]{1,0:T(8,128)S(1)}, f32[8,2,128]{2,1,0:T(2,128)S(1)}) custom-call(bf16[8,160,128]{2,1,0:T(8,128)(2,1)S(1)} %all_to_all.15.refs_0_, bf16[4,272,128]{2,1,0:T(8,128)(2,1)S(1)} %pad_maximum_fusion.refs_1_.refs_2_, bf16[4,272,128]{2,1,0:T(8,128)(2,1)S(1)} %collective-permute-done.3.refs_2_.refs_3_), custom_call_target="tpu_custom_call" | custom-call | tf_op jit(solution)/shard_map/scales/pallas_call | solution.py:475
  76.9 6.7 %all-to-all-start.2 = ((bf16[128,8,128]{2,1,0:T(8,128)(2,1)}), bf16[128,8,128]{2,1,0:T(8,128)(2,1)S(1)}, u32[]{:S(2)}, u32[]{:S(2)}) async-start(bf16[128,8,128]{2,1,0:T(8,128)(2,1)} %bitcast.7), calls=%async_computation.2 | async-start | bytes 524288 | tf_op jit(solution)/shard_map/all_to_all | solution.py:588
  83.6 2.9 %keys.1 = bf16[1024,128]{1,0:T(8,128)(2,1)} custom-call(f32[128,16]{1,0:T(8,128)S(1)} %get-tuple-element.23.refs_0_, bf16[1024,128]{1,0:T(8,128)(2,1)S(1)} %time.1.refs_0_.refs_1_, bf16[4,272,128]{2,1,0:T(8,128)(2,1)S(1)} %pad_maximum_fusion.refs_1_.refs_2_, bf16[4,272,128]{2,1,0:T(8,128)(2,1)S(1)} %collective-permute-done.3.refs_2_.refs_3_), custom_call_target="tpu_custom_call" | custom-call | tf_op jit(solution)/shard_map/keys/pallas_call | solution.py:507
  86.5 8.4 %all-to-all-done.2 = bf16[128,8,128]{2,1,0:T(8,128)(2,1)S(1)} async-done(((bf16[128,8,128]{2,1,0:T(8,128)(2,1)}), bf16[128,8,128]{2,1,0:T(8,128)(2,1)S(1)}, u32[]{:S(2)}, u32[]{:S(2)}) %all-to-all-start.2) | async-done | bytes 262176 | tf_op jit(solution)/shard_map/all_to_all | solution.py:588
  94.9 0.8 collective-permute-start.6
  95.7 0.1 slice.3
  95.8 0.6 reshape.33
  96.4 0.2 collective-permute-done.6.other_ref
  96.6 0.6 weave.1
  (5 shorter events, 0.1 us)
Async XLA Ops:
  13.6 9.3 %copy-start = (bf16[8,32,128]{2,1,0:T(8,128)(2,1)S(1)}, bf16[8,32,128]{2,1,0:T(8,128)(2,1)}, u32[]{:S(2)}) copy-start(bf16[8,32,128]{2,1,0:T(8,128)(2,1)} %param.15) | copy-start | bytes 196612
  13.7 9.3 %copy-start.1 = (s32[8]{0:T(128)S(1)}, s32[8]{0:T(128)}, u32[]{:S(2)}) copy-start(s32[8]{0:T(128)} %len_ref.1) | copy-start | bytes 100
  13.7 9.3 %copy-start.2 = (s32[8]{0:T(128)S(1)}, s32[8]{0:T(128)}, u32[]{:S(2)}) copy-start(s32[8]{0:T(128)} %pos_ref.1) | copy-start | bytes 100
  13.7 32.1 %all-to-all-start = ((bf16[16,4,16,768]{3,2,1,0:T(8,128)(2,1)}), bf16[16,4,16,768]{3,2,1,0:T(8,128)(2,1)S(1)}, u32[]{:S(2)}, u32[]{:S(2)}) async-start(bf16[16,4,16,768]{3,2,1,0:T(8,128)(2,1)} %space.1), calls=%async_computation | async-start | bytes 3145728 | tf_op jit(solution)/shard_map/all_to_all | solution.py:569
  23.7 4.2 %collective-permute-start.2 = (bf16[272,128]{1,0:T(8,128)(2,1)S(1)}, bf16[272,128]{1,0:T(8,128)(2,1)S(1)}, u32[]{:S(2)}, u32[]{:S(2)}) collective-permute-start(bf16[272,128]{1,0:T(8,128)(2,1)S(1)} %pack_queries.1), channel_id=1, source_target_pairs={{0,96},{16,112},{32,0},{48,16},{64,32},{80,48},{96,64},{112,80},{1... | collective-permute-start | bytes 208904 | tf_op jit(solution)/shard_map/ppermute | solution.py:574
  26.5 5.0 %collective-permute-start.1 = (bf16[272,128]{1,0:T(8,128)(2,1)S(1)}, bf16[272,128]{1,0:T(8,128)(2,1)S(1)}, u32[]{:S(2)}, u32[]{:S(2)}) collective-permute-start(bf16[272,128]{1,0:T(8,128)(2,1)S(1)} %pack_queries.1), channel_id=1, source_target_pairs={{0,64},{16,80},{32,96},{48,112},{64,0},{80,16},{96,32},{112,48},{1... | collective-permute-start | bytes 208904 | tf_op jit(solution)/shard_map/ppermute | solution.py:574
  26.8 6.6 %collective-permute-start = (bf16[272,128]{1,0:T(8,128)(2,1)S(1)}, bf16[272,128]{1,0:T(8,128)(2,1)S(1)}, u32[]{:S(2)}, u32[]{:S(2)}) collective-permute-start(bf16[272,128]{1,0:T(8,128)(2,1)S(1)} %pack_queries.1), channel_id=1, source_target_pairs={{0,32},{16,48},{32,64},{48,80},{64,96},{80,112},{96,0},{112,16},{1... | collective-permute-start | bytes 208904 | tf_op jit(solution)/shard_map/ppermute | solution.py:574
  45.8 12.1 %collective-permute-start.3 = (bf16[4,272,128]{2,1,0:T(8,128)(2,1)S(1)}, bf16[4,272,128]{2,1,0:T(8,128)(2,1)S(1)}, u32[]{:S(2)}, u32[]{:S(2)}) collective-permute-start(bf16[4,272,128]{2,1,0:T(8,128)(2,1)S(1)} %pad_maximum_fusion.refs_1_.refs_2_), channel_id=1, source_target_pairs={{0,16},{16,0},{32,48},{48,32},{64,80},{80,64},{96,112},{112,96},{1... | collective-permute-start | bytes 835592 | tf_op jit(solution)/shard_map/ppermute | solution.py:579
  60.5 2.4 %collective-permute-start.4 = (bf16[8,128,128]{2,1,0:T(8,128)(2,1)S(1)}, bf16[8,128,128]{2,1,0:T(8,128)(2,1)S(1)}, u32[]{:S(2)}, u32[]{:S(2)}) collective-permute-start(bf16[8,128,128]{2,1,0:T(8,128)(2,1)S(1)} %get-tuple-element.20), channel_id=1, source_target_pairs={{0,1},{1,0},{2,3},{3,2},{4,5},{5,4},{6,7},{7,6},{8,9},{9,8},{10,11... | collective-permute-start | bytes 786440 | tf_op jit(solution)/shard_map/ppermute | solution.py:583
  61.7 1.2 %collective-permute-start.5 = (f32[16,128]{1,0:T(8,128)S(1)}, f32[16,128]{1,0:T(8,128)S(1)}, u32[]{:S(2)}, u32[]{:S(2)}) collective-permute-start(f32[16,128]{1,0:T(8,128)S(1)} %get-tuple-element.21.sums_ref), channel_id=1, source_target_pairs={{0,1},{1,0},{2,3},{3,2},{4,5},{5,4},{6,7},{7,6},{8,9},{9,8},{10,11... | collective-permute-start | bytes 24584 | tf_op jit(solution)/shard_map/ppermute | solution.py:584
  76.9 18.0 %all-to-all-start.2 = ((bf16[128,8,128]{2,1,0:T(8,128)(2,1)}), bf16[128,8,128]{2,1,0:T(8,128)(2,1)S(1)}, u32[]{:S(2)}, u32[]{:S(2)}) async-start(bf16[128,8,128]{2,1,0:T(8,128)(2,1)} %bitcast.7), calls=%async_computation.2 | async-start | bytes 524288 | tf_op jit(solution)/shard_map/all_to_all | solution.py:588
  94.9 1.6 %collective-permute-start.6 = (bf16[16,8,128]{2,1,0:T(8,128)(2,1)S(1)}, bf16[16,8,128]{2,1,0:T(8,128)(2,1)S(1)}, u32[]{:S(2)}, u32[]{:S(2)}) collective-permute-start(bf16[16,8,128]{2,1,0:T(8,128)(2,1)S(1)} %totals.1.mine_ref), channel_id=1, source_target_pairs={{0,1},{1,0},{2,3},{3,2},{4,5},{5,4},{6,7},{7,6},{8,9},{9,8},{10,11... | collective-permute-start | bytes 98312 | tf_op jit(solution)/shard_map/ppermute | solution.py:594

commit v9 on v7

--- a/solution.py
+++ b/solution.py
@@ -375,7 +375,12 @@
         for part in range(rows // E):
             square = both[part * E : (part + 1) * E, E:]
             sums.append(jnp.sum(jnp.where(eye, square, 0.0), axis=0, keepdims=True))
-    sums_ref[...] = jnp.concatenate(sums, axis=0)
+    sums = jnp.concatenate(sums, axis=0)
+    sums_ref[...] = sums
+    upper = sums.astype(BF16)
+    send_ref[blocks, : sums.shape[0], :] = upper
+    send_ref[blocks, sums.shape[0] : 2 * sums.shape[0], :] = (sums - upper.astype(F32)).astype(BF16)
+    send_ref[blocks, 2 * sums.shape[0] :, :] = jnp.zeros((E - 2 * sums.shape[0], E), BF16)
 
 
 def terms(packed, khat):
@@ -386,7 +391,7 @@
         out_specs=[VMEM] * 3,
         out_shape=[
             jax.ShapeDtypeStruct((blocks, rows // 2, E), F32),
-            jax.ShapeDtypeStruct((blocks, rows // 2, E), BF16),
+            jax.ShapeDtypeStruct((blocks + 1, rows // 2, E), BF16),
             jax.ShapeDtypeStruct((blocks * rows // E, E), F32),
         ],
         compiler_params=limit(16),
@@ -394,11 +399,13 @@
     )(khat, *packed)
 
 
-def join_kernel(keep_ref, got_ref, sums_ref, others_ref, out_ref):
+def join_kernel(keep_ref, got_ref, sums_ref, out_ref):
     blocks, half, _ = keep_ref.shape
     chips = out_ref.shape[0]
     piece = half // chips
-    sums = sums_ref[...] + others_ref[...]
+    count = sums_ref.shape[0]
+    others = got_ref[blocks, : 2 * count, :].astype(F32)
+    sums = sums_ref[...] + others[:count] + others[count:]
     upper = sums.astype(BF16)
     lower = (sums - upper.astype(F32)).astype(BF16)
     notes = jnp.concatenate([upper, lower], axis=0)
@@ -412,18 +419,18 @@
         out_ref[chip, blocks * piece :, :] = notes
 
 
-def join(keep, got, sums, others, chips):
+def join(keep, got, sums, chips):
     blocks, half, _ = keep.shape
     return pl.pallas_call(
         join_kernel,
-        in_specs=[VMEM] * 4,
+        in_specs=[VMEM] * 3,
         out_specs=VMEM,
         out_shape=jax.ShapeDtypeStruct(
             (chips, blocks * half // chips + 2 * sums.shape[0], E), BF16
         ),
         compiler_params=limit(8),
         name="join",
-    )(keep, got, sums, others)
+    )(keep, got, sums)
 
 
 def scale_kernel(slots, got_ref, *refs):
@@ -581,8 +588,7 @@
 
     keep, send, sums = terms(packed, khat)
     got = lax.ppermute(send, "seq", partner)
-    others = lax.ppermute(sums, "seq", partner)
-    joined = join(keep, got, sums, others, shards // 2)
+    joined = join(keep, got, sums, shards // 2)
     joined = lax.all_to_all(joined, "seq", 0, 0, tiled=True, axis_index_groups=chips)
     parts, scale, loss = scales(joined, packed, slots, shards)
     parts = lax.all_to_all(

time: 97.4 us -> 97.5 us (level)
    ppermute x1, waiting for transfers between devices: 0.01 us -> 1.21 us  [body(): got = lax.ppermute(send, 'seq', partner)]
    ppermute x1 -> x0, waiting for transfers between devices: 1.08 us -> none  [body(): others = lax.ppermute(sums, 'seq', partner)]
  transfers between devices with their start and end apart: 9 -> 8, of which waited for: 7 -> 7; matrix products, arithmetic and copies ran while one was open for 1% -> 1% of each run, Pallas kernels for 15% -> 15%
where the time goes in v9:
time: 97.5 us; the launch traced here: 97.2 us
  Pallas kernels  32.4 us (33%)
  waiting for transfers between devices  28 us (29%)
  starting transfers between devices  22.6 us (23%)
  blocking collectives  12.7 us (13%)
    pallas_call x1, Pallas kernels, space(): pl.pallas_call(space_kernel, in_specs=[HBM] * 3, out_specs=HBM, out_shape...  12.9 us
    all_to_all x1, blocking collectives, body(): lax.all_to_all(joined, 'seq', 0, 0, tiled=True, axis_index_groups=chips)  12.7 us
    all_to_all x1, waiting for transfers between devices, body(): items = lax.all_to_all(spatial, 'seq', 0, 0, tiled=True)  12.3 us
    pallas_call x1, Pallas kernels, time(): pl.pallas_call(time_kernel, in_specs=[VMEM] + [HBM] * 3, out_specs=VMEM,...  11.4 us
    all_to_all x1, starting transfers between devices, body(): items = lax.all_to_all(spatial, 'seq', 0, 0, tiled=True)  9.27 us
    all_to_all x1, waiting for transfers between devices, body(): lax.all_to_all(parts.reshape((-1,) + parts.shape[2:]), ('dp', 'seq'), 0,...  8.4 us
    all_to_all x1, starting transfers between devices, body(): lax.all_to_all(parts.reshape((-1,) + parts.shape[2:]), ('dp', 'seq'), 0,...  6.74 us
    ppermute x3, waiting for transfers between devices, body(): lax.ppermute(mine, 'dp', [(i, (i + by) % blocks) for i in range(blocks)])  5.92 us
  transfers between devices with their start and end apart: 8, of which 7 were waited for; matrix products, arithmetic and copies ran while one was open for 1% of the time, Pallas kernels for 15%

profile of v9, /device:TPU:1, one launch (start us, length us, event | category | flops | bytes accessed | tf_op | source)
XLA Modules:
  0.0 97.2 jit_solution(1663992076577151578)
XLA Ops:
  0.6 12.9 %space.1 = bf16[16,4,16,768]{3,2,1,0:T(8,128)(2,1)} custom-call(bf16[4,256,768]{2,1,0:T(8,128)(2,1)} %bitcast.15, bf16[768,2304]{1,0:T(8,128)(2,1)} %qkv_ref.2, bf16[768,768]{1,0:T(8,128)(2,1)} %out_w_ref.2), custom_call_target="tpu_custom_call" | custom-call | tf_op jit(solution)/shard_map/space/pallas_call | solution.py:194
  13.5 0.0 copy-start
  13.5 0.0 copy-start.1
  13.6 0.0 copy-start.2
  13.6 9.3 %all-to-all-start = ((bf16[16,4,16,768]{3,2,1,0:T(8,128)(2,1)}), bf16[16,4,16,768]{3,2,1,0:T(8,128)(2,1)S(1)}, u32[]{:S(2)}, u32[]{:S(2)}) async-start(bf16[16,4,16,768]{3,2,1,0:T(8,128)(2,1)} %space.1), calls=%async_computation | async-start | bytes 3145728 | tf_op jit(solution)/shard_map/all_to_all | solution.py:576
  22.8 0.0 copy-done
  22.8 0.0 copy-done.1
  22.9 0.7 pack_queries.1
  23.5 2.8 %collective-permute-start.2 = (bf16[272,128]{1,0:T(8,128)(2,1)S(1)}, bf16[272,128]{1,0:T(8,128)(2,1)S(1)}, u32[]{:S(2)}, u32[]{:S(2)}) collective-permute-start(bf16[272,128]{1,0:T(8,128)(2,1)S(1)} %pack_queries.1), channel_id=1, source_target_pairs={{0,96},{16,112},{32,0},{48,16},{64,32},{80,48},{96,64},{112,80},{1... | collective-permute-start | bytes 208904 | tf_op jit(solution)/shard_map/ppermute | solution.py:581
  26.4 0.3 collective-permute-start.1
  26.7 0.7 collective-permute-start
  27.4 0.3 collective-permute-done.2
  27.7 3.6 %collective-permute-done.1 = bf16[272,128]{1,0:T(8,128)(2,1)S(1)} collective-permute-done((bf16[272,128]{1,0:T(8,128)(2,1)S(1)}, bf16[272,128]{1,0:T(8,128)(2,1)S(1)}, u32[]{:S(2)}, u32[]{:S(2)}) %collective-permute-start.1) | collective-permute-done | bytes 69664 | tf_op jit(solution)/shard_map/ppermute | solution.py:581
  31.3 2.0 %collective-permute-done = bf16[272,128]{1,0:T(8,128)(2,1)S(1)} collective-permute-done((bf16[272,128]{1,0:T(8,128)(2,1)S(1)}, bf16[272,128]{1,0:T(8,128)(2,1)S(1)}, u32[]{:S(2)}, u32[]{:S(2)}) %collective-permute-start) | collective-permute-done | bytes 69664 | tf_op jit(solution)/shard_map/ppermute | solution.py:581
  33.4 12.3 %all-to-all-done = bf16[16,4,16,768]{3,2,1,0:T(8,128)(2,1)S(1)} async-done(((bf16[16,4,16,768]{3,2,1,0:T(8,128)(2,1)}), bf16[16,4,16,768]{3,2,1,0:T(8,128)(2,1)S(1)}, u32[]{:S(2)}, u32[]{:S(2)}) %all-to-all-start) | async-done | bytes 1572896 | tf_op jit(solution)/shard_map/all_to_all | solution.py:576
  45.7 0.7 collective-permute-start.3
  46.4 11.4 %time.1.refs_0_.refs_1_ = bf16[1024,128]{1,0:T(8,128)(2,1)S(1)} custom-call(bf16[1024,768]{1,0:T(8,128)(2,1)S(1)} %bitcast.11, bf16[768,2304]{1,0:T(8,128)(2,1)} %qkv_ref.3, bf16[768,768]{1,0:T(8,128)(2,1)} %out_w_ref.3, bf16[768,128]{1,0:T(8,128)(2,1)} %proj_ref.1), custom_call_target="tpu_custom_call" | custom-call | tf_op jit(solution)/shard_map/time/pallas_call | solution.py:283
  57.8 0.0 collective-permute-done.3.refs_2_.refs_3_
  57.9 2.6 %terms.1 = (f32[8,128,128]{2,1,0:T(8,128)S(1)}, bf16[9,128,128]{2,1,0:T(8,128)(2,1)S(1)}, f32[16,128]{1,0:T(8,128)S(1)}) custom-call(bf16[1024,128]{1,0:T(8,128)(2,1)S(1)} %time.1.refs_0_.refs_1_, bf16[4,272,128]{2,1,0:T(8,128)(2,1)S(1)} %pad_maximum_fusion.refs_1_.refs_2_, bf16[4,272,128]{2,1,0:T(8,128)(2,1)S(1)} %collective-permute-done.3.refs_2_.refs_3_), custom_call_target="tpu_custom_call" | custom-call | tf_op jit(solution)/shard_map/terms/pallas_call | solution.py:388
  60.5 1.2 %collective-permute-start.4 = (bf16[9,128,128]{2,1,0:T(8,128)(2,1)S(1)}, bf16[9,128,128]{2,1,0:T(8,128)(2,1)S(1)}, u32[]{:S(2)}, u32[]{:S(2)}) collective-permute-start(bf16[9,128,128]{2,1,0:T(8,128)(2,1)S(1)} %get-tuple-element.20), channel_id=1, source_target_pairs={{0,1},{1,0},{2,3},{3,2},{4,5},{5,4},{6,7},{7,6},{8,9},{9,8},{10,11... | collective-permute-start | bytes 884744 | tf_op jit(solution)/shard_map/ppermute | solution.py:590
  61.7 1.2 %collective-permute-done.4.got_ref = bf16[9,128,128]{2,1,0:T(8,128)(2,1)S(1)} collective-permute-done((bf16[9,128,128]{2,1,0:T(8,128)(2,1)S(1)}, bf16[9,128,128]{2,1,0:T(8,128)(2,1)S(1)}, u32[]{:S(2)}, u32[]{:S(2)}) %collective-permute-start.4) | collective-permute-done | bytes 294944 | tf_op jit(solution)/shard_map/ppermute | solution.py:590
  62.9 0.1 join.1
  63.0 12.7 %all_to_all.15.refs_0_ = bf16[8,160,128]{2,1,0:T(8,128)(2,1)S(1)} all-to-all(bf16[8,160,128]{2,1,0:T(8,128)(2,1)S(1)} %join.1), channel_id=1, replica_groups={{0,2,4,6,8,10,12,14},{1,3,5,7,9,11,13,15},{16,18,20,22,24,26,28,30},{17..., dimensions={0} | all-to-all | bytes 655360 | tf_op jit(solution)/shard_map/all_to_all | solution.py:592
  75.7 1.2 %scales.1 = (bf16[8,16,8,128]{3,2,1,0:T(8,128)(2,1)}, f32[128,16]{1,0:T(8,128)S(1)}, f32[8,2,128]{2,1,0:T(2,128)S(1)}) custom-call(bf16[8,160,128]{2,1,0:T(8,128)(2,1)S(1)} %all_to_all.15.refs_0_, bf16[4,272,128]{2,1,0:T(8,128)(2,1)S(1)} %pad_maximum_fusion.refs_1_.refs_2_, bf16[4,272,128]{2,1,0:T(8,128)(2,1)S(1)} %collective-permute-done.3.refs_2_.refs_3_), custom_call_target="tpu_custom_call" | custom-call | tf_op jit(solution)/shard_map/scales/pallas_call | solution.py:482
  76.9 6.7 %all-to-all-start.2 = ((bf16[128,8,128]{2,1,0:T(8,128)(2,1)}), bf16[128,8,128]{2,1,0:T(8,128)(2,1)S(1)}, u32[]{:S(2)}, u32[]{:S(2)}) async-start(bf16[128,8,128]{2,1,0:T(8,128)(2,1)} %bitcast.7), calls=%async_computation.2 | async-start | bytes 524288 | tf_op jit(solution)/shard_map/all_to_all | solution.py:594
  83.6 2.9 %keys.1 = bf16[1024,128]{1,0:T(8,128)(2,1)} custom-call(f32[128,16]{1,0:T(8,128)S(1)} %get-tuple-element.23.refs_0_, bf16[1024,128]{1,0:T(8,128)(2,1)S(1)} %time.1.refs_0_.refs_1_, bf16[4,272,128]{2,1,0:T(8,128)(2,1)S(1)} %pad_maximum_fusion.refs_1_.refs_2_, bf16[4,272,128]{2,1,0:T(8,128)(2,1)S(1)} %collective-permute-done.3.refs_2_.refs_3_), custom_call_target="tpu_custom_call" | custom-call | tf_op jit(solution)/shard_map/keys/pallas_call | solution.py:514
  86.5 8.4 %all-to-all-done.2 = bf16[128,8,128]{2,1,0:T(8,128)(2,1)S(1)} async-done(((bf16[128,8,128]{2,1,0:T(8,128)(2,1)}), bf16[128,8,128]{2,1,0:T(8,128)(2,1)S(1)}, u32[]{:S(2)}, u32[]{:S(2)}) %all-to-all-start.2) | async-done | bytes 262176 | tf_op jit(solution)/shard_map/all_to_all | solution.py:594
  94.9 0.8 collective-permute-start.5
  95.7 0.1 slice.3
  95.8 0.6 reshape.33
  96.4 0.2 collective-permute-done.5.other_ref
  96.6 0.6 weave.1
  (3 shorter events, 0.1 us)
Async XLA Ops:
  13.5 9.3 %copy-start = (bf16[8,32,128]{2,1,0:T(8,128)(2,1)S(1)}, bf16[8,32,128]{2,1,0:T(8,128)(2,1)}, u32[]{:S(2)}) copy-start(bf16[8,32,128]{2,1,0:T(8,128)(2,1)} %param.15) | copy-start | bytes 196612
  13.5 9.3 %copy-start.1 = (s32[8]{0:T(128)S(1)}, s32[8]{0:T(128)}, u32[]{:S(2)}) copy-start(s32[8]{0:T(128)} %len_ref.1) | copy-start | bytes 100
  13.6 9.3 %copy-start.2 = (s32[8]{0:T(128)S(1)}, s32[8]{0:T(128)}, u32[]{:S(2)}) copy-start(s32[8]{0:T(128)} %pos_ref.1) | copy-start | bytes 100
  13.6 32.1 %all-to-all-start = ((bf16[16,4,16,768]{3,2,1,0:T(8,128)(2,1)}), bf16[16,4,16,768]{3,2,1,0:T(8,128)(2,1)S(1)}, u32[]{:S(2)}, u32[]{:S(2)}) async-start(bf16[16,4,16,768]{3,2,1,0:T(8,128)(2,1)} %space.1), calls=%async_computation | async-start | bytes 3145728 | tf_op jit(solution)/shard_map/all_to_all | solution.py:576
  23.5 4.2 %collective-permute-start.2 = (bf16[272,128]{1,0:T(8,128)(2,1)S(1)}, bf16[272,128]{1,0:T(8,128)(2,1)S(1)}, u32[]{:S(2)}, u32[]{:S(2)}) collective-permute-start(bf16[272,128]{1,0:T(8,128)(2,1)S(1)} %pack_queries.1), channel_id=1, source_target_pairs={{0,96},{16,112},{32,0},{48,16},{64,32},{80,48},{96,64},{112,80},{1... | collective-permute-start | bytes 208904 | tf_op jit(solution)/shard_map/ppermute | solution.py:581
  26.4 5.0 %collective-permute-start.1 = (bf16[272,128]{1,0:T(8,128)(2,1)S(1)}, bf16[272,128]{1,0:T(8,128)(2,1)S(1)}, u32[]{:S(2)}, u32[]{:S(2)}) collective-permute-start(bf16[272,128]{1,0:T(8,128)(2,1)S(1)} %pack_queries.1), channel_id=1, source_target_pairs={{0,64},{16,80},{32,96},{48,112},{64,0},{80,16},{96,32},{112,48},{1... | collective-permute-start | bytes 208904 | tf_op jit(solution)/shard_map/ppermute | solution.py:581
  26.7 6.6 %collective-permute-start = (bf16[272,128]{1,0:T(8,128)(2,1)S(1)}, bf16[272,128]{1,0:T(8,128)(2,1)S(1)}, u32[]{:S(2)}, u32[]{:S(2)}) collective-permute-start(bf16[272,128]{1,0:T(8,128)(2,1)S(1)} %pack_queries.1), channel_id=1, source_target_pairs={{0,32},{16,48},{32,64},{48,80},{64,96},{80,112},{96,0},{112,16},{1... | collective-permute-start | bytes 208904 | tf_op jit(solution)/shard_map/ppermute | solution.py:581
  45.7 12.2 %collective-permute-start.3 = (bf16[4,272,128]{2,1,0:T(8,128)(2,1)S(1)}, bf16[4,272,128]{2,1,0:T(8,128)(2,1)S(1)}, u32[]{:S(2)}, u32[]{:S(2)}) collective-permute-start(bf16[4,272,128]{2,1,0:T(8,128)(2,1)S(1)} %pad_maximum_fusion.refs_1_.refs_2_), channel_id=1, source_target_pairs={{0,16},{16,0},{32,48},{48,32},{64,80},{80,64},{96,112},{112,96},{1... | collective-permute-start | bytes 835592 | tf_op jit(solution)/shard_map/ppermute | solution.py:586
  60.5 2.4 %collective-permute-start.4 = (bf16[9,128,128]{2,1,0:T(8,128)(2,1)S(1)}, bf16[9,128,128]{2,1,0:T(8,128)(2,1)S(1)}, u32[]{:S(2)}, u32[]{:S(2)}) collective-permute-start(bf16[9,128,128]{2,1,0:T(8,128)(2,1)S(1)} %get-tuple-element.20), channel_id=1, source_target_pairs={{0,1},{1,0},{2,3},{3,2},{4,5},{5,4},{6,7},{7,6},{8,9},{9,8},{10,11... | collective-permute-start | bytes 884744 | tf_op jit(solution)/shard_map/ppermute | solution.py:590
  76.9 18.0 %all-to-all-start.2 = ((bf16[128,8,128]{2,1,0:T(8,128)(2,1)}), bf16[128,8,128]{2,1,0:T(8,128)(2,1)S(1)}, u32[]{:S(2)}, u32[]{:S(2)}) async-start(bf16[128,8,128]{2,1,0:T(8,128)(2,1)} %bitcast.7), calls=%async_computation.2 | async-start | bytes 524288 | tf_op jit(solution)/shard_map/all_to_all | solution.py:594
  94.9 1.6 %collective-permute-start.5 = (bf16[16,8,128]{2,1,0:T(8,128)(2,1)S(1)}, bf16[16,8,128]{2,1,0:T(8,128)(2,1)S(1)}, u32[]{:S(2)}, u32[]{:S(2)}) collective-permute-start(bf16[16,8,128]{2,1,0:T(8,128)(2,1)S(1)} %totals.1.mine_ref), channel_id=1, source_target_pairs={{0,1},{1,0},{2,3},{3,2},{4,5},{5,4},{6,7},{7,6},{8,9},{9,8},{10,11... | collective-permute-start | bytes 98312 | tf_op jit(solution)/shard_map/ppermute | solution.py:600
